TPU v7x, 32 devices: a whole 2x2x4 slice. The times are simulated.
32 devices in a mesh: member: 4 (over x, core), space: 8 (over z, y).
Axes of the slice: x: 2, y: 2, z: 4, core: 2. Of those that a mesh axis runs over, the one named last changes fastest.
Arguments:
- spectra: float32 [16, 12, 320, 641], P('member', None, 'space'), may hold values from -6 to 6
- legendre: bfloat16 [320, 641, 384], P('space'), as said below
- sin_lat: float32 [384], replicated, may hold values from 0 to 1, as said below
- gravity: float32 [2, 2], replicated, may hold values from 0.1 to 2, as said below
- stability: float32 [2, 2], replicated, may hold values from 0.1 to 2, as said below
- clones: int32 [2, 2], replicated, may hold values from 0 to 15, as said below
Outputs:
- new_state: float32 [16, 12, 320, 641], P('member', None, 'space')
Inputs may be any that keep to these rules, and one draw needn't show every extreme that they name: `clones`: column 0 holds 2 distinct killed trajectories, column 1 for each a survivor; no survivor is killed, and a survivor may be copied onto several killed trajectories. legendre[p, j, l] is the associated Legendre function of the (m, n) of position (p, j), normalized so that its square integrates to one over -1 to 1, at mu = sin_lat[l]. `sin_lat`: decreasing from the pole towards the equator. `gravity`: diagonal entries 1 to 2, off-diagonal entries 0.1 to 0.6. `stability`: diagonal entries 1 to 2, off-diagonal entries 0.1 to 0.6.
All inputs are finite; a program needn't handle non-finite values.
Results may differ from a plain program's by a relative error of at most 0.0016.
Values may be sent and summed in bfloat16 or wider, within the bound.
No kernel may reach another device: no remote copies, remote signals or barrier semaphores. Data moves between devices by JAX's collectives and lax.ppermute only.
A program may use at most 192 MiB of HBM per device.

v0:
```python
import functools
import math

import jax
import jax.numpy as jnp
from jax import lax
from jax.experimental import pallas as pl
from jax.experimental.pallas import tpu as pltpu
from jax.sharding import PartitionSpec as P


LANES = 128
SUB = 8
PACKED = 16
UNROLL_FORWARD = 8
UNROLL_INVERSE = 8
LONGITUDES_PER_WAVE = 2

time_step = 0.25
wave_scale = 16.0
diffusion = 0.02


def layout_terms(first_pair, count, lane0, lanes, truncation):
    pair = first_pair + lax.broadcasted_iota(jnp.int32, (count, lanes), 0)
    column = lane0 + lax.broadcasted_iota(jnp.int32, (count, lanes), 1)
    leading = column < truncation - pair
    offset = jnp.where(leading, column, column - (truncation - pair))
    order = jnp.where(leading, pair, truncation - 1 - pair)
    return leading, (offset & 1) == 1, order + offset


def slot_place(n, direct):
    return jnp.bitwise_xor(lax.axis_index("space"), n) if direct else jnp.int32(n)


def forward_kernel(
    *refs, truncation, pairs, real_pairs, keep, count, made, span, direct
):
    if count:
        slot_ref, refs = refs[0], refs[1:]
    spec_ref, leg_ref, refs = refs[0], refs[1], refs[2:]
    step = pl.program_id(0)
    row_length = truncation + 1
    _, comps, block, _ = spec_ref.shape
    rows = span * comps
    fresh_refs, refs = refs[:count], refs[count:]
    out_refs, refs = refs[: len(made)], refs[len(made) :]
    if keep:
        keep_ref, refs = refs[0], refs[1:]
    wide, xs, res = refs
    tiles = xs.shape[0]
    padded = tiles * LANES
    first_place = lax.div(slot_place(made[0], direct), 2)
    t0 = lax.div(first_place, span) * span

    @pl.when(step == 0)
    def _():
        wide[row_length * block :, :] = jnp.zeros(
            (wide.shape[0] - row_length * block, LANES), jnp.float32
        )

    wide[: row_length * block, :] = (
        leg_ref[...].astype(jnp.float32).reshape(row_length * block, LANES)
    )
    for k in range(tiles):
        width = min(LANES, row_length - k * LANES)
        lanes = slice(k * LANES, k * LANES + width)
        if width < LANES:
            xs[k] = jnp.zeros((rows * block, LANES), jnp.float32)
        xs[k, :, :width] = spec_ref[pl.ds(t0, span), :, :, lanes].reshape(rows * block, width)

    for i in range(count):
        slot = slot_ref[i] - t0

        @pl.when(jnp.logical_and(slot >= 0, slot < span))
        def _():
            at = pl.multiple_of(slot * comps * block, SUB)
            for k in range(tiles):
                width = min(LANES, row_length - k * LANES)
                fresh = fresh_refs[i][:, :, k * LANES : k * LANES + width].astype(jnp.float32)
                xs[k, pl.ds(at, comps * block), :width] = fresh.reshape(comps * block, width)

    first_pair = lax.axis_index("space") * real_pairs + step * block

    def one(q, carry):
        x = jnp.concatenate(
            [xs[k, pl.ds(q, rows, stride=block), :] for k in range(tiles)], axis=1
        )
        edge = truncation - first_pair - q
        group = PACKED if rows % PACKED == 0 else SUB
        column = lax.broadcasted_iota(jnp.int32, (group, padded), 1)
        leading = column < edge
        odd = (jnp.where(leading, column, column - edge) & 1) == 1
        sign = jnp.where(odd, -1.0, 1.0)
        kind = jnp.bfloat16 if group == PACKED else jnp.float32
        factors = [
            jnp.where(leading, 1.0, 0.0),
            jnp.where(leading, 0.0, 1.0),
            jnp.where(leading, sign, 0.0),
            jnp.where(leading, 0.0, sign),
        ]
        x = x.astype(kind)
        lhs = []
        for factor in factors:
            factor = factor.astype(kind)
            for at in range(0, rows, group):
                lhs.append(x[at : at + group] * factor)
        lhs = jnp.concatenate(lhs, axis=0).astype(jnp.bfloat16)
        rhs = wide[pl.ds(q, padded, stride=block), :].astype(jnp.bfloat16)
        if keep:
            keep_ref[q] = rhs
        got = jnp.dot(lhs, rhs, preferred_element_type=jnp.float32)
        res[pl.ds(step * block + q, 4 * rows, stride=pairs), :] = got
        return carry

    lax.fori_loop(0, block, one, 0, unroll=UNROLL_FORWARD)

    @pl.when(step == pl.num_programs(0) - 1)
    def _():
        for n, slot in enumerate(made):
            place = slot_place(slot, direct)
            t, s = lax.div(place, 2) - t0, lax.rem(place, 2)
            base = pl.multiple_of((s * (2 * rows) + t * comps) * pairs, SUB)
            for f in range(comps // 2):
                parts = []
                for r in range(2):
                    for h in range(2):
                        parts.append(res[pl.ds(base + (h * rows + 2 * f + r) * pairs, pairs), :])
                out_refs[n][f] = jnp.concatenate(parts, axis=0).astype(jnp.bfloat16)


def grid_kernel(order_ref, cor_ref, weight_ref, syn_ref, ana_ref, *refs, scale):
    sources = order_ref.shape[0]
    in_refs, out_refs, (modes, force) = refs[:sources], refs[sources:-2], refs[-2:]
    fields, rows, lanes = in_refs[0].shape
    longitudes = syn_ref.shape[0]
    for n in range(sources):
        at = pl.multiple_of(order_ref[n] * rows, 16)
        for f in range(fields):
            modes[pl.ds(at, rows), f * lanes : (f + 1) * lanes] = in_refs[n][f]
    cor = cor_ref[...]
    weight = weight_ref[...]
    span = 128

    def synth(b, carry):
        at = pl.multiple_of(b * span, span)
        g = (
            jnp.dot(syn_ref[pl.ds(at, span), :], modes[...], preferred_element_type=jnp.float32)
            * scale
        )
        field = [g[:, f * lanes : (f + 1) * lanes] for f in range(fields)]
        mean = 0.5 * (field[4] + field[5])
        out = [None] * fields
        for a in range(2):
            spin = field[a] + cor
            div = field[2 + a]
            out[a] = -spin * div
            out[2 + a] = spin * field[a] - 0.5 * div * div
            out[4 + a] = -(field[4 + a] + mean) * div
        for f in range(fields):
            force[pl.ds(at, span), f * lanes : (f + 1) * lanes] = out[f].astype(jnp.bfloat16)
        return carry

    lax.fori_loop(0, longitudes // span, synth, 0)

    def analyse(d, carry):
        at = pl.multiple_of(d * rows, 16)
        w = jnp.dot(ana_ref[pl.ds(at, rows), :], force[...], preferred_element_type=jnp.float32)
        for f in range(fields):
            lane = slice(f * lanes, (f + 1) * lanes)
            modes[pl.ds(at, rows), lane] = (w[:, lane] * weight).astype(jnp.bfloat16)
        return carry

    lax.fori_loop(0, sources, analyse, 0)
    for n in range(sources):
        at = pl.multiple_of(order_ref[n] * rows, 16)
        for f in range(fields):
            out_refs[n][f] = modes[pl.ds(at, rows), f * lanes : (f + 1) * lanes]


def step_terms(degree, gm, hm, truncation):
    eig = wave_scale * (degree * (degree + 1)).astype(jnp.float32) / float(truncation * truncation)
    damping = 1.0 / (1.0 + diffusion * eig * eig)
    coupling = time_step * time_step * eig
    pm = [[gm[a][0] * hm[0][b] + gm[a][1] * hm[1][b] for b in range(2)] for a in range(2)]
    diag = [1.0 + coupling * pm[a][a] for a in range(2)]
    cross = [coupling * pm[0][1], coupling * pm[1][0]]
    inverse = 1.0 / (diag[0] * diag[1] - cross[0] * cross[1])
    solve = [
        [diag[1] * inverse, -cross[0] * inverse],
        [-cross[1] * inverse, diag[0] * inverse],
    ]
    push = [[time_step * eig * gm[a][b] for b in range(2)] for a in range(2)]
    return damping, solve, push


def semi_implicit_slabs(old, tend, terms, hm):
    damping, solve, push = terms
    out = [None] * 12
    for r in range(2):
        star = [old[c * 2 + r] + time_step * tend[c * 2 + r] for c in range(6)]
        right = [star[2 + a] + push[a][0] * star[4] + push[a][1] * star[5] for a in range(2)]
        div = [solve[a][0] * right[0] + solve[a][1] * right[1] for a in range(2)]
        for a in range(2):
            heat = (time_step * hm[a][0]) * div[0] + (time_step * hm[a][1]) * div[1]
            out[a * 2 + r] = damping * star[a]
            out[(2 + a) * 2 + r] = damping * div[a]
            out[(4 + a) * 2 + r] = damping * (star[4 + a] - heat)
    return out


def inverse_kernel(
    slot_ref,
    gravity_ref,
    stability_ref,
    *refs,
    truncation,
    pairs,
    real_pairs,
    chunks,
    last,
    stored,
    slots,
    count,
    direct,
):
    w_refs, refs = refs[: chunks * slots], refs[chunks * slots :]
    leg_refs, refs = refs[:chunks], refs[chunks:]
    spec_ref, refs = refs[0], refs[1:]
    patches = count if stored else 0
    fresh_refs, refs = refs[:patches], refs[patches:]
    mend_refs, refs = refs[:patches], refs[patches:]
    out_ref, ws, ten = refs[:3]
    if stored:
        wide = refs[3]
    step = pl.program_id(0)
    row_length = truncation + 1
    trajectories, comps, block, _ = out_ref.shape
    rows = trajectories * comps
    tiles = ten.shape[0]
    padded = tiles * LANES

    @pl.when(step == 0)
    def _():
        if stored:
            for k in range(chunks):
                wide[k, row_length * block :, :] = jnp.zeros(
                    (wide.shape[1] - row_length * block, LANES), jnp.float32
                )

        def fill(k, t, s, source):
            base = pl.multiple_of((s * (2 * rows) + t * comps) * pairs, SUB)
            for f in range(comps // 2):
                got = source(f).astype(jnp.float32)
                for r in range(2):
                    for h in range(2):
                        at = (r * 2 + h) * pairs
                        ws[k, pl.ds(base + (h * rows + 2 * f + r) * pairs, pairs), :] = got[
                            at : at + pairs, :
                        ]

        for k in range(chunks):
            for n in range(slots):
                place = slot_place(n, direct)
                fill(k, lax.div(place, 2), lax.rem(place, 2), lambda f: w_refs[k * slots + n][f])
        for i in range(patches):

            @pl.when(slot_ref[i] >= 0)
            def _():
                for s in range(2):
                    fill(0, slot_ref[i], s, lambda f: mend_refs[i][s, f])

    if stored:
        for k in range(chunks):
            wide[k, : row_length * block, :] = (
                leg_refs[k][...].astype(jnp.float32).reshape(row_length * block, LANES)
            )
    first_pair = lax.axis_index("space") * real_pairs + step * block

    def one(q, carry):
        at = pl.ds(step * block + q, 4 * rows, stride=pairs)
        lhs = jnp.concatenate([ws[k, at, :].astype(jnp.bfloat16) for k in range(chunks)], axis=1)
        if not stored:
            rhs = jnp.concatenate([leg_refs[k][q] for k in range(chunks)], axis=1)
        else:
            at = pl.ds(q, padded, stride=block)
            rhs = jnp.concatenate(
                [wide[k, at, :].astype(jnp.bfloat16) for k in range(chunks)], axis=1
            )
        got = lax.dot_general(
            lhs, rhs, (((1,), (1,)), ((), ())), preferred_element_type=jnp.float32
        )
        leading, odd, _ = layout_terms(first_pair + q, 1, 0, padded, truncation)
        north = jnp.where(leading, got[:rows], got[rows : 2 * rows])
        south = jnp.where(leading, got[2 * rows : 3 * rows], got[3 * rows :])
        total = north + jnp.where(odd, -south, south)
        for k in range(tiles):
            ten[k, pl.ds(q, rows, stride=block), :] = total[:, k * LANES : (k + 1) * LANES]
        return carry

    lax.fori_loop(0, block, one, 0, unroll=UNROLL_INVERSE)

    if last:
        gm = [[gravity_ref[a, b] for b in range(2)] for a in range(2)]
        hm = [[stability_ref[a, b] for b in range(2)] for a in range(2)]
    for k in range(tiles):
        width = min(LANES, row_length - k * LANES)
        lanes = slice(k * LANES, k * LANES + width)
        if last:
            _, _, degree = layout_terms(first_pair, block, k * LANES, width, truncation)
            terms = step_terms(degree, gm, hm, truncation)

        def body(t, carry):
            tend = []
            for c in range(comps):
                at = pl.multiple_of((t * comps + c) * block, SUB)
                value = ten[k, pl.ds(at, block), :][:, :width]
                tend.append(value)
            old = [spec_ref[t, c, :, lanes] for c in range(comps)]
            if last:
                tend = semi_implicit_slabs(old, tend, terms, hm)
            else:
                for i in range(patches):
                    mine = slot_ref[i] == t
                    old = [jnp.where(mine, fresh_refs[i][c, :, lanes], old[c]) for c in range(comps)]
                tend = [old[c] + time_step * tend[c] for c in range(comps)]
            for c in range(comps):
                out_ref[t, c, :, lanes] = tend[c]
            return carry

        lax.fori_loop(0, trajectories, body, 0)


def fourier_tables(pair_count, groups, truncation, longitudes):
    half_turn = longitudes // 2
    order = jnp.arange(pair_count + 1, dtype=jnp.int32)[None, :, None]
    column = jnp.arange(half_turn, dtype=jnp.int32)[None, None, :]
    quarter = jnp.arange(2, dtype=jnp.int32)[:, None, None] * (longitudes // 4)
    phase = (order * column + quarter) % longitudes
    angle = phase.astype(jnp.float32) * (2.0 * math.pi / longitudes)
    base = lax.optimization_barrier(jnp.cos(angle).astype(jnp.bfloat16))
    low = base[:, :pair_count]
    flip = (1 - 2 * (column % 2)) * (1 - 2 * jnp.arange(2, dtype=jnp.int32)[:, None, None])
    high = base[:, 1:] * flip.astype(jnp.bfloat16)
    pair = jnp.arange(pair_count, dtype=jnp.int32)[None, :, None]
    low_sign = (1 - 2 * (pair % 2)).astype(jnp.bfloat16)
    high_sign = (1 - 2 * ((truncation - 1 - pair) % 2)).astype(jnp.bfloat16)
    low = jnp.concatenate([low, low * low_sign], axis=2)
    high = jnp.concatenate([high, high * high_sign], axis=2)
    table = jnp.stack([low, high], axis=1)
    table = table.reshape(2, 2, groups, pair_count // groups, longitudes)
    return jnp.transpose(table, (2, 0, 1, 3, 4)).reshape(4 * pair_count, longitudes)


def far_members(members):
    return [(a, b) for a in range(members) for b in range(a + 1, members) if a ^ b != 1]


def pick_kernel(clones_ref, spec_ref, row_ref, slot_ref, *route_refs, local):
    row_ref[...] = spec_ref[...].astype(jnp.bfloat16)
    members, member = lax.axis_size("member"), lax.axis_index("member")
    for i, route_ref in enumerate(route_refs):
        source = lax.div(clones_ref[i, 1], local)
        target = lax.div(clones_ref[i, 0], local)
        route = jnp.where(source == target, 0, 1)
        low, high = jnp.minimum(source, target), jnp.maximum(source, target)
        for k, (a, b) in enumerate(far_members(members)):
            route = jnp.where(jnp.logical_and(low == a, high == b), 2 + k, route)
        route_ref[0] = route
        slot_ref[i] = jnp.where(target == member, clones_ref[i, 0] - target * local, -1)


def pick_clones(spectra, clones):
    local, comps, pairs, row_length = spectra.shape
    count = clones.shape[0]
    smem = pl.BlockSpec(memory_space=pltpu.SMEM)
    block = (1, comps, pairs, row_length)
    got = pl.pallas_call(
        functools.partial(pick_kernel, local=local),
        out_shape=[
            jax.ShapeDtypeStruct((count,) + block[1:], jnp.bfloat16),
            jax.ShapeDtypeStruct((count,), jnp.int32),
        ]
        + [jax.ShapeDtypeStruct((1,), jnp.int32)] * count,
        grid_spec=pltpu.PrefetchScalarGridSpec(
            num_scalar_prefetch=1,
            grid=(count,),
            in_specs=[pl.BlockSpec(block, lambda i, c: (lax.rem(c[i, 1], local), 0, 0, 0))],
            out_specs=[pl.BlockSpec(block, lambda i, c: (i, 0, 0, 0))] + [smem] * (1 + count),
        ),
        cost_estimate=pl.CostEstimate(
            flops=0, bytes_accessed=6 * 1024 * 1024, transcendentals=0
        ),
        name="pick",
    )(clones, spectra)
    return got[0], got[1], [r.reshape(()) for r in got[2:]]


def choose_kernel(clones_ref, *refs, local, slots, direct):
    in_refs, out_refs = refs[:slots], refs[slots:]
    for i, out_ref in enumerate(out_refs):
        t = lax.rem(clones_ref[i, 1], local)
        for n in range(slots):
            place = slot_place(n, direct)

            @pl.when(lax.div(place, 2) == t)
            def _():
                out_ref[lax.rem(place, 2)] = in_refs[n][...]


def choose_rows(parts, clones, local, direct):
    vmem = pl.BlockSpec(memory_space=pltpu.VMEM)
    return pl.pallas_call(
        functools.partial(choose_kernel, local=local, slots=len(parts), direct=direct),
        out_shape=[jax.ShapeDtypeStruct((2,) + parts[0].shape, parts[0].dtype)] * clones.shape[0],
        in_specs=[pl.BlockSpec(memory_space=pltpu.SMEM)] + [vmem] * len(parts),
        out_specs=[vmem] * clones.shape[0],
        cost_estimate=pl.CostEstimate(
            flops=0, bytes_accessed=4 * 1024 * 1024, transcendentals=0
        ),
        name="choose",
    )(clones, *parts)


def send_clone(row, route):
    members = lax.axis_size("member")

    def swap(pairs):
        both = pairs + [(b, a) for a, b in pairs]
        return lambda v: lax.ppermute(v, "member", both)

    branches = [lambda v: v, swap([(a, a + 1) for a in range(0, members, 2)])]
    branches += [swap([pair]) for pair in far_members(members)]
    return lax.switch(route, branches, row)


def share_row(row, owner):
    members = lax.axis_size("member")
    differs = jnp.bitwise_xor(owner, lax.axis_index("member").astype(jnp.int32))
    bit = 1
    while bit < members:
        other = lax.ppermute(row, "member", [(m, m ^ bit) for m in range(members)])
        row = jnp.where(jnp.bitwise_and(differs, bit) != 0, other, row)
        bit *= 2
    return row


def shards(spectra, legendre, sin_lat, gravity, stability, clones):
    trajectories, comps, pairs, row_length = spectra.shape
    truncation = row_length - 1
    half_lat = legendre.shape[2]
    longitudes = LONGITUDES_PER_WAVE * truncation
    space = lax.axis_size("space")
    position = lax.axis_index("space")
    fields = comps // 2
    split = space // (2 * trajectories)
    lane_count = LANES // split
    chunk_count = half_lat // LANES
    padded_pairs = -(-pairs // SUB) * SUB
    steps = padded_pairs // SUB
    tiles = -(-row_length // LANES)
    extra = padded_pairs - pairs
    rows = trajectories * comps

    count = clones.shape[0]
    slots = 2 * trajectories
    direct = split == 1
    state = spectra
    if extra:
        state = jnp.pad(state, ((0, 0), (0, 0), (0, extra), (0, 0)))
    order = jnp.arange(space, dtype=jnp.int32)
    if direct:
        order = jnp.bitwise_xor(position.astype(jnp.int32), order)
    columns = jnp.transpose(legendre, (1, 0, 2))
    if extra:
        columns = jnp.pad(columns, ((0, 0), (0, extra), (0, 0)))

    smem = pl.BlockSpec(memory_space=pltpu.SMEM)
    state_spec = pl.BlockSpec((trajectories, comps, SUB, row_length), lambda i: (0, 0, i, 0))
    fresh_spec = pl.BlockSpec((comps, SUB, row_length), lambda i: (0, i, 0))
    kept_spec = pl.BlockSpec((SUB, tiles * LANES, LANES), lambda i: (i, 0, 0))
    part_shape = (fields, 4 * padded_pairs, LANES)
    part_spec = pl.BlockSpec(part_shape, lambda i: (0, 0, 0))
    mend_spec = pl.BlockSpec((2,) + part_shape, lambda i: (0, 0, 0, 0))

    def leg_spec(k):
        return pl.BlockSpec((row_length, SUB, LANES), lambda i: (0, i, k))

    mib = 1024 * 1024

    def forward(k, made, span, clone_slot, patches):
        keep = k > 0
        kept_shape = jax.ShapeDtypeStruct((padded_pairs, tiles * LANES, LANES), jnp.bfloat16)
        return pl.pallas_call(
            functools.partial(
                forward_kernel, truncation=truncation, pairs=padded_pairs, keep=keep,
                real_pairs=pairs, count=len(patches), made=made, span=span, direct=direct,
            ),
            out_shape=[jax.ShapeDtypeStruct(part_shape, jnp.bfloat16)] * len(made)
            + [kept_shape] * keep,
            grid=(steps,),
            in_specs=[smem] * bool(patches)
            + [state_spec, leg_spec(k)]
            + [fresh_spec] * len(patches),
            out_specs=[part_spec] * len(made) + [kept_spec] * keep,
            scratch_shapes=[
                pltpu.VMEM((tiles * LANES * SUB, LANES), jnp.float32),
                pltpu.VMEM((tiles, span * comps * SUB, LANES), jnp.float32),
                pltpu.VMEM((4 * span * comps * padded_pairs, LANES), jnp.float32),
            ],
            compiler_params=pltpu.CompilerParams(vmem_limit_bytes=60 * mib),
            cost_estimate=pl.CostEstimate(
                flops=8 * span * comps * padded_pairs * row_length * LANES,
                bytes_accessed=16 * 1024 * 1024,
                transcendentals=0,
            ),
            name="forward",
        )(*([clone_slot] if patches else []), state, columns, *patches)

    def to_wire(x):
        if extra:
            x = x.reshape(slots, fields, 4, padded_pairs, LANES)[:, :, :, :pairs]
        x = x.reshape(slots, fields, 4 * pairs, split, lane_count)
        return jnp.transpose(x, (0, 3, 1, 2, 4)).reshape(space, fields, 4 * pairs, lane_count)

    def from_wire(x):
        x = x.reshape(slots, split, fields, 4, pairs, lane_count)
        x = jnp.transpose(x, (0, 2, 3, 4, 1, 5)).reshape(slots, fields, 4, pairs, LANES)
        if extra:
            x = jnp.pad(x, ((0, 0), (0, 0), (0, 0), (0, extra), (0, 0)))
        return x.reshape((slots,) + part_shape)

    def exchange(x):
        return lax.all_to_all(x, "space", split_axis=0, concat_axis=0, tiled=True)

    def swap(parts):
        got = list(parts)
        for n in reversed(range(1, space)):
            got[n] = lax.ppermute(parts[n], "space", [(d, d ^ n) for d in range(space)])
        return got

    def spread(parts):
        if direct:
            return swap(parts)
        x = exchange(to_wire(jnp.stack(parts)))
        x = jnp.pad(x, ((0, 0), (0, 0), (0, 0), (0, LANES - lane_count)))
        return [x[d] for d in range(space)]

    def collect(parts):
        if direct:
            return swap(parts)
        x = from_wire(exchange(jnp.stack(parts)[..., :lane_count]))
        return [x[n] for n in range(slots)]

    analysis = lax.optimization_barrier(
        fourier_tables(pairs * space, space, truncation, longitudes)
    )
    synthesis = analysis.T
    south = position // split % 2
    hemisphere = jnp.where(south == 0, sin_lat, -sin_lat)
    weights_all = math.pi * jnp.sqrt(1.0 - hemisphere * hemisphere) / (2 * half_lat)
    vmem = pl.BlockSpec(memory_space=pltpu.VMEM)
    modes = 4 * pairs * space

    def grid(k, parts):
        first = k * LANES + position % split * lane_count
        mu = lax.dynamic_slice_in_dim(hemisphere, first, lane_count)
        weight = lax.dynamic_slice_in_dim(weights_all, first, lane_count)
        short = LANES - lane_count
        if short:
            mu = jnp.pad(mu, (0, short))
            weight = jnp.pad(weight, (0, short))
        return pl.pallas_call(
            functools.partial(grid_kernel, scale=1.0 / truncation),
            out_shape=[jax.ShapeDtypeStruct(x.shape, jnp.bfloat16) for x in parts],
            in_specs=[smem] + [vmem] * (4 + space),
            out_specs=[vmem] * space,
            scratch_shapes=[
                pltpu.VMEM((modes, fields * LANES), jnp.bfloat16),
                pltpu.VMEM((longitudes, fields * LANES), jnp.bfloat16),
            ],
            compiler_params=pltpu.CompilerParams(vmem_limit_bytes=60 * mib),
            cost_estimate=pl.CostEstimate(
                flops=4 * modes * longitudes * fields * LANES,
                bytes_accessed=12 * 1024 * 1024,
                transcendentals=0,
            ),
            name="grid",
        )(order, (2.0 * mu)[None], weight[None], synthesis, analysis, *parts)

    def inverse(ws, legs, start, patches, mends, last):
        chunks = len(ws)
        stored = bool(patches)
        wide_scratch = pltpu.VMEM((chunks, tiles * LANES * SUB, LANES), jnp.float32)
        return pl.pallas_call(
            functools.partial(
                inverse_kernel,
                truncation=truncation,
                pairs=padded_pairs,
                chunks=chunks,
                last=last,
                stored=stored,
                slots=slots,
                count=count,
                real_pairs=pairs,
                direct=direct,
            ),
            out_shape=jax.ShapeDtypeStruct(state.shape, jnp.float32),
            grid=(steps,),
            in_specs=[smem] * 3
            + [part_spec] * (chunks * slots)
            + ([leg_spec(k) for k in range(chunks)] if stored else [kept_spec] * chunks)
            + [state_spec]
            + [fresh_spec] * len(patches)
            + [mend_spec] * len(mends),
            out_specs=state_spec,
            scratch_shapes=[
                pltpu.VMEM((chunks, 4 * rows * padded_pairs, LANES), jnp.float32),
                pltpu.VMEM((tiles, rows * SUB, LANES), jnp.float32),
            ]
            + ([wide_scratch] if stored else []),
            compiler_params=pltpu.CompilerParams(vmem_limit_bytes=60 * mib),
            cost_estimate=pl.CostEstimate(
                flops=8 * rows * padded_pairs * row_length * LANES * chunks,
                bytes_accessed=20 * 1024 * 1024,
                transcendentals=0,
            ),
            name="inverse",
        )(slot, gravity, stability, *[x for w in ws for x in w], *legs, start, *patches, *mends)

    everything = tuple(range(slots))
    if direct and trajectories % 2 == 0:
        near, far = everything[: slots // 2], everything[slots // 2 :]
        first = list(forward(0, far, trajectories // 2, None, []))
        second = list(forward(0, near, trajectories // 2, None, []))
        made = [second + first]
    else:
        made = [list(forward(0, everything, trajectories, None, []))]

    turn, made[0][0] = lax.optimization_barrier((clones, made[0][0]))
    picked, slot, route = pick_clones(spectra, turn)
    narrow = [send_clone(picked[i], route[i]) for i in range(count)]
    if extra:
        narrow = [jnp.pad(x, ((0, 0), (0, extra), (0, 0))) for x in narrow]
    turn = slot
    for k in range(1, chunk_count):
        made.append(list(forward(k, everything, trajectories, turn, narrow)))
        turn, made[k][0] = lax.optimization_barrier((slot, made[k][0]))
    kept = [x[-1] for x in made[1:]]
    sent = []
    for x in made:
        sent.append(spread(x[:slots]))
    back = []
    for k in range(chunk_count):
        got = grid(k, sent[k])
        if k == 0:
            later, got = lax.optimization_barrier((clones[:, 1], got))
        back.append(collect(got))
    fresh = [
        share_row(
            lax.dynamic_index_in_dim(spectra, lax.rem(later[i], trajectories), 0, keepdims=False),
            lax.div(later[i], trajectories),
        )
        for i in range(count)
    ]
    if extra:
        fresh = [jnp.pad(x, ((0, 0), (0, extra), (0, 0))) for x in fresh]
    back[0][0], fresh = lax.optimization_barrier((back[0][0], fresh))
    chosen = choose_rows(back[0], clones, trajectories, direct)
    mends = [send_clone(chosen[i], route[i]) for i in range(count)]
    start = inverse(back[:1], [columns], state, fresh, mends, False)
    for k in range(1, chunk_count - 1):
        start = inverse(back[k : k + 1], kept[k - 1 : k], start, [], [], False)
    out = inverse(back[-1:], kept[-1:], start, [], [], True)
    return out[:, :, :pairs] if extra else out


def solution(mesh):
    placed = (P("member", None, "space", None), P("space", None, None), P(), P(), P(), P())
    return jax.shard_map(
        shards,
        mesh=mesh,
        in_specs=placed,
        out_specs=P("member", None, "space", None),
        check_vma=False,
    )
```

profile of v0, /device:TPU:1, one launch (start us, length us, event | category | flops | bytes accessed | tf_op | source)
XLA Modules:
  0.0 449.8 jit_solution(14971519394702138296)
XLA Ops:
  0.0 9.9 %forward.7 = (bf16[6,160,128]{2,1,0:T(8,128)(2,1)}, bf16[6,160,128]{2,1,0:T(8,128)(2,1)}, bf16[6,160,128]{2,1,0:T(8,128)(2,1)}, bf16[6,160,128]{2,1,0:T(8,128)(2,1)}) custom-call(f32[4,12,40,641]{3,2,1,0:T(8,128)} %refs_9_.1, bf16[641,40,384]{2,1,0:T(8,128)(2,1)} %bitcast.31), custom_call_target="tpu_custom_call" | custom-call | flops 630128640 | bytes 16777216 | tf_op jit(solution)/shard_map/forward/pallas_call | solution.py:495
  17.4 9.9 %forward.4 = (bf16[6,160,128]{2,1,0:T(8,128)(2,1)}, bf16[6,160,128]{2,1,0:T(8,128)(2,1)}, bf16[6,160,128]{2,1,0:T(8,128)(2,1)}, bf16[6,160,128]{2,1,0:T(8,128)(2,1)}) custom-call(f32[4,12,40,641]{3,2,1,0:T(8,128)} %refs_9_.1, bf16[641,40,384]{2,1,0:T(8,128)(2,1)} %bitcast.32), custom_call_target="tpu_custom_call" | custom-call | flops 630128640 | bytes 16777216 | tf_op jit(solution)/shard_map/forward/pallas_call | solution.py:495
  28.6 6.8 %fusion.3 = bf16[2,321,640]{2,1,0:T(8,128)(2,1)S(1)} fusion(s32[2]{0:T(128)S(1)} %iota_multiply_fusion.1, s32[321,640]{1,0:T(8,128)S(1)} %iota_multiply_fusion), kind=kLoop, calls=%fused_computation.5 | loop fusion | flops 4108800 | bytes 1643528 | tf_op jit(solution)/shard_map/convert_element_type | solution.py:342
  41.3 4.8 %collective-permute-done.52.refs_5_ = bf16[6,160,128]{2,1,0:T(8,128)(2,1)S(1)} collective-permute-done((bf16[6,160,128]{2,1,0:T(8,128)(2,1)}, bf16[6,160,128]{2,1,0:T(8,128)(2,1)S(1)}, u32[]{:S(2)}, u32[]{:S(2)}) %collective-permute-start.52) | collective-permute-done | bytes 245792 | tf_op jit(solution)/shard_map/ppermute | solution.py:540
  50.4 3.7 copy.11.syn_ref
  57.2 14.4 %grid.5 = (bf16[6,160,128]{2,1,0:T(8,128)(2,1)}, bf16[6,160,128]{2,1,0:T(8,128)(2,1)}, bf16[6,160,128]{2,1,0:T(8,128)(2,1)}, bf16[6,160,128]{2,1,0:T(8,128)(2,1)...) custom-call(s32[8]{0:T(128)} %iota_xor_fusion.order_ref, ...), custom_call_target="tpu_custom_call" | custom-call | flops 5033164800 | bytes 12582912 | tf_op jit(solution)/shard_map/grid/pallas_call | solution.py:574
  89.2 4.3 collective-permute-start.60
  96.1 60.9 %conditional.5 = (bf16[12,40,641]{2,1,0:T(8,128)(2,1)S(1)}) conditional(s32[]{:T(128)} %bitcast.10, bf16[12,40,641]{2,1,0:T(8,128)(2,1)S(1)} %get-tuple-element.209, bf16[12,40,641]{2,1,0:T(8,128)(2,1)S(1)} %get-tuple-element.209, bf16[12,40,641]{2,1,0:T(8,128)(2,1)S(1)} %get-tuple-element.209, ...), branch_computations={%region_6.7_spmd, %region_7.8_spmd, %region_8.9_spmd, %region_9.10... | conditional | bytes 3692208 | solution.py:435
  98.7 58.2 %collective-permute-done.9 = bf16[12,40,641]{2,1,0:T(8,128)(2,1)S(1)} collective-permute-done((bf16[12,40,641]{2,1,0:T(8,128)(2,1)S(1)}, bf16[12,40,641]{2,1,0:T(8,128)(2,1)S(1)}, u32[]{:S(2)}, u32[]{:S(2)}) %collective-permute-start.9) | collective-permute-done | bytes 615392 | tf_op jit(solution)/shard_map/cond/branch_5_fun/ppermute | solution.py:431
  157.9 13.1 %forward.5 = (bf16[6,160,128]{2,1,0:T(8,128)(2,1)}, bf16[6,160,128]{2,1,0:T(8,128)(2,1)}, bf16[6,160,128]{2,1,0:T(8,128)(2,1)}, bf16[6,160,128]{2,1,0:T(8,128)(2...) custom-call(s32[2]{0:T(128)} %get-tuple-element.137.refs_0_.slot_ref, ...), custom_call_target="tpu_custom_call" | custom-call | flops 1260257280 | bytes 16777216 | tf_op jit(solution)/shard_map/forward/pallas_call | solution.py:495
  171.0 4.4 collective-permute-start.61
  184.4 5.3 %collective-permute-start.35 = (bf16[6,160,128]{2,1,0:T(8,128)(2,1)}, bf16[6,160,128]{2,1,0:T(8,128)(2,1)}, u32[]{:S(2)}, u32[]{:S(2)}) collective-permute-start(bf16[6,160,128]{2,1,0:T(8,128)(2,1)} %get-tuple-element.158), channel_id=1, source_target_pairs={{0,2},{1,3},{2,0},{3,1},{4,6},{5,7},{6,4},{7,5},{8,10},{9,11},{10,... | collective-permute-start | bytes 737288 | tf_op jit(solution)/shard_map/ppermute | solution.py:540
  192.6 11.4 %collective-permute-start.37 = (bf16[6,160,128]{2,1,0:T(8,128)(2,1)}, bf16[6,160,128]{2,1,0:T(8,128)(2,1)}, u32[]{:S(2)}, u32[]{:S(2)}) collective-permute-start(bf16[6,160,128]{2,1,0:T(8,128)(2,1)} %get-tuple-element.160), channel_id=1, source_target_pairs={{0,4},{1,5},{2,6},{3,7},{4,0},{5,1},{6,2},{7,3},{8,12},{9,13},{10,... | collective-permute-start | bytes 737288 | tf_op jit(solution)/shard_map/ppermute | solution.py:540
  206.7 8.7 %collective-permute-done.65.refs_7_ = bf16[6,160,128]{2,1,0:T(8,128)(2,1)S(1)} collective-permute-done((bf16[6,160,128]{2,1,0:T(8,128)(2,1)S(1)}, bf16[6,160,128]{2,1,0:T(8,128)(2,1)S(1)}, u32[]{:S(2)}, u32[]{:S(2)}) %collective-permute-start.65) | collective-permute-done | bytes 245792 | tf_op jit(solution)/shard_map/ppermute | solution.py:540
  218.7 45.6 %conditional.7 = (bf16[2,6,160,128]{3,2,1,0:T(8,128)(2,1)S(1)}) conditional(s32[]{:T(128)} %bitcast.10, bf16[2,6,160,128]{3,2,1,0:T(8,128)(2,1)S(1)} %get-tuple-element.202, bf16[2,6,160,128]{3,2,1,0:T(8,128)(2,1)S(1)} %get-tuple-element.202, bf16[2,6,160,128]{3,2,1,0:T(8,128)(2,1)S(1)} %get-tuple-element.202, ...), branch_computations={%region_18.19_spmd, %region_19.20_spmd, %region_20.21_spmd, %regio... | conditional | bytes 2949168 | solution.py:435
  218.8 39.3 %collective-permute-start.19 = (bf16[2,6,160,128]{3,2,1,0:T(8,128)(2,1)S(1)}, bf16[2,6,160,128]{3,2,1,0:T(8,128)(2,1)S(1)}, u32[]{:S(2)}, u32[]{:S(2)}) collective-permute-start(bf16[2,6,160,128]{3,2,1,0:T(8,128)(2,1)S(1)} %param.23), channel_id=1, source_target_pairs={{8,24},{24,8},{9,25},{25,9},{10,26},{26,10},{11,27},{27,11},{12,28... | collective-permute-start | bytes 1474568 | tf_op jit(solution)/shard_map/cond/branch_5_fun/ppermute | solution.py:431
  258.1 6.2 %collective-permute-done.19 = bf16[2,6,160,128]{3,2,1,0:T(8,128)(2,1)S(1)} collective-permute-done((bf16[2,6,160,128]{3,2,1,0:T(8,128)(2,1)S(1)}, bf16[2,6,160,128]{3,2,1,0:T(8,128)(2,1)S(1)}, u32[]{:S(2)}, u32[]{:S(2)}) %collective-permute-start.19) | collective-permute-done | bytes 491552 | tf_op jit(solution)/shard_map/cond/branch_5_fun/ppermute | solution.py:431
  264.3 8.0 %collective-permute-start.38 = (bf16[6,160,128]{2,1,0:T(8,128)(2,1)S(1)}, bf16[6,160,128]{2,1,0:T(8,128)(2,1)S(1)}, u32[]{:S(2)}, u32[]{:S(2)}) collective-permute-start(bf16[6,160,128]{2,1,0:T(8,128)(2,1)S(1)} %copy-done.25), channel_id=1, source_target_pairs={{0,5},{1,4},{2,7},{3,6},{4,1},{5,0},{6,3},{7,2},{8,13},{9,12},{10,... | collective-permute-start | bytes 737288 | tf_op jit(solution)/shard_map/ppermute | solution.py:540
  272.3 13.0 %forward.6 = (bf16[6,160,128]{2,1,0:T(8,128)(2,1)}, bf16[6,160,128]{2,1,0:T(8,128)(2,1)}, bf16[6,160,128]{2,1,0:T(8,128)(2,1)}, bf16[6,160,128]{2,1,0:T(8,128)(2...) custom-call(s32[2]{0:T(128)} %get-tuple-element.137.refs_0_.slot_ref, ...), custom_call_target="tpu_custom_call" | custom-call | flops 1260257280 | bytes 16777216 | tf_op jit(solution)/shard_map/forward/pallas_call | solution.py:495
  285.3 5.5 %collective-permute-start.39 = (bf16[6,160,128]{2,1,0:T(8,128)(2,1)S(1)}, bf16[6,160,128]{2,1,0:T(8,128)(2,1)S(1)}, u32[]{:S(2)}, u32[]{:S(2)}) collective-permute-start(bf16[6,160,128]{2,1,0:T(8,128)(2,1)S(1)} %copy-done.24), channel_id=1, source_target_pairs={{0,6},{1,7},{2,4},{3,5},{4,2},{5,3},{6,0},{7,1},{8,14},{9,15},{10,... | collective-permute-start | bytes 737288 | tf_op jit(solution)/shard_map/ppermute | solution.py:540
  299.1 4.7 %collective-permute-done.40.refs_7_ = bf16[6,160,128]{2,1,0:T(8,128)(2,1)S(1)} collective-permute-done((bf16[6,160,128]{2,1,0:T(8,128)(2,1)S(1)}, bf16[6,160,128]{2,1,0:T(8,128)(2,1)S(1)}, u32[]{:S(2)}, u32[]{:S(2)}) %collective-permute-start.40) | collective-permute-done | bytes 245792 | tf_op jit(solution)/shard_map/ppermute | solution.py:540
  303.8 18.7 %collective-permute-start.24 = (bf16[6,160,128]{2,1,0:T(8,128)(2,1)}, bf16[6,160,128]{2,1,0:T(8,128)(2,1)S(1)}, u32[]{:S(2)}, u32[]{:S(2)}) collective-permute-start(bf16[6,160,128]{2,1,0:T(8,128)(2,1)} %get-tuple-element.144), channel_id=1, source_target_pairs={{0,5},{1,4},{2,7},{3,6},{4,1},{5,0},{6,3},{7,2},{8,13},{9,12},{10,... | collective-permute-start | bytes 737288 | tf_op jit(solution)/shard_map/ppermute | solution.py:540
  325.0 14.3 %grid.4 = (bf16[6,160,128]{2,1,0:T(8,128)(2,1)}, bf16[6,160,128]{2,1,0:T(8,128)(2,1)}, bf16[6,160,128]{2,1,0:T(8,128)(2,1)}, bf16[6,160,128]{2,1,0:T(8,128)(2,1)...) custom-call(s32[8]{0:T(128)} %iota_xor_fusion.order_ref, ...), custom_call_target="tpu_custom_call" | custom-call | flops 5033164800 | bytes 12582912 | tf_op jit(solution)/shard_map/grid/pallas_call | solution.py:574
  343.5 5.2 %collective-permute-start.44 = (bf16[6,160,128]{2,1,0:T(8,128)(2,1)}, bf16[6,160,128]{2,1,0:T(8,128)(2,1)S(1)}, u32[]{:S(2)}, u32[]{:S(2)}) collective-permute-start(bf16[6,160,128]{2,1,0:T(8,128)(2,1)} %get-tuple-element.168), channel_id=1, source_target_pairs={{0,4},{1,5},{2,6},{3,7},{4,0},{5,1},{6,2},{7,3},{8,12},{9,13},{10,... | collective-permute-start | bytes 737288 | tf_op jit(solution)/shard_map/ppermute | solution.py:540
  349.4 10.7 %collective-permute-start.45 = (bf16[6,160,128]{2,1,0:T(8,128)(2,1)}, bf16[6,160,128]{2,1,0:T(8,128)(2,1)S(1)}, u32[]{:S(2)}, u32[]{:S(2)}) collective-permute-start(bf16[6,160,128]{2,1,0:T(8,128)(2,1)} %get-tuple-element.169), channel_id=1, source_target_pairs={{0,5},{1,4},{2,7},{3,6},{4,1},{5,0},{6,3},{7,2},{8,13},{9,12},{10,... | collective-permute-start | bytes 737288 | tf_op jit(solution)/shard_map/ppermute | solution.py:540
  360.2 14.4 %grid.3 = (bf16[6,160,128]{2,1,0:T(8,128)(2,1)}, bf16[6,160,128]{2,1,0:T(8,128)(2,1)}, bf16[6,160,128]{2,1,0:T(8,128)(2,1)}, bf16[6,160,128]{2,1,0:T(8,128)(2,1)...) custom-call(s32[8]{0:T(128)} %iota_xor_fusion.order_ref, ...), custom_call_target="tpu_custom_call" | custom-call | flops 5033164800 | bytes 12582912 | tf_op jit(solution)/shard_map/grid/pallas_call | solution.py:574
  380.5 3.8 collective-permute-done.46.refs_6_
  384.2 7.2 %collective-permute-start.30 = (bf16[6,160,128]{2,1,0:T(8,128)(2,1)}, bf16[6,160,128]{2,1,0:T(8,128)(2,1)S(1)}, u32[]{:S(2)}, u32[]{:S(2)}) collective-permute-start(bf16[6,160,128]{2,1,0:T(8,128)(2,1)} %get-tuple-element.151), channel_id=1, source_target_pairs={{0,4},{1,5},{2,6},{3,7},{4,0},{5,1},{6,2},{7,3},{8,12},{9,13},{10,... | collective-permute-start | bytes 737288 | tf_op jit(solution)/shard_map/ppermute | solution.py:540
  391.5 14.7 %collective-permute-start.31 = (bf16[6,160,128]{2,1,0:T(8,128)(2,1)}, bf16[6,160,128]{2,1,0:T(8,128)(2,1)S(1)}, u32[]{:S(2)}, u32[]{:S(2)}) collective-permute-start(bf16[6,160,128]{2,1,0:T(8,128)(2,1)} %get-tuple-element.152), channel_id=1, source_target_pairs={{0,5},{1,4},{2,7},{3,6},{4,1},{5,0},{6,3},{7,2},{8,13},{9,12},{10,... | collective-permute-start | bytes 737288 | tf_op jit(solution)/shard_map/ppermute | solution.py:540
  410.2 14.6 %inverse.3.refs_9_ = f32[4,12,40,641]{3,2,1,0:T(8,128)} custom-call(s32[2]{0:T(128)} %get-tuple-element.137.refs_0_.slot_ref, f32[2,2]{1,0:T(2,128)} %gravity_ref.5, f32[2,2]{1,0:T(2,128)} %stability_ref.5, bf16[6,160,128]{2,1,0:T(8,128)(2,1)} %get-tuple-element.191.refs_0_, bf16[6,160,128]{2,1,0:T(8,128)(2,1)} %copy-done.1, bf16[6,160,128]{2,1,0:T(8,128)(2,1)} %copy-done.2, ...), custom_call_target="tpu_custom_call" | custom-call | flops 1260257280 | bytes 20971520 | tf_op jit(solution)/shard_map/inverse/pallas_call | solution.py:596
  424.9 11.7 %inverse.4.refs_9_ = f32[4,12,40,641]{3,2,1,0:T(8,128)} custom-call(s32[2]{0:T(128)} %get-tuple-element.137.refs_0_.slot_ref, f32[2,2]{1,0:T(2,128)} %gravity_ref.5, f32[2,2]{1,0:T(2,128)} %stability_ref.5, bf16[6,160,128]{2,1,0:T(8,128)(2,1)} %get-tuple-element.164.refs_0_, bf16[6,160,128]{2,1,0:T(8,128)(2,1)} %copy-done.8, bf16[6,160,128]{2,1,0:T(8,128)(2,1)} %copy-done.9, ...), custom_call_target="tpu_custom_call" | custom-call | flops 1260257280 | bytes 20971520 | tf_op jit(solution)/shard_map/inverse/pallas_call | solution.py:596
  437.5 12.3 %inverse.5 = f32[4,12,40,641]{3,2,1,0:T(8,128)} custom-call(s32[2]{0:T(128)} %get-tuple-element.137.refs_0_.slot_ref, f32[2,2]{1,0:T(2,128)} %gravity_ref.5, f32[2,2]{1,0:T(2,128)} %stability_ref.5, bf16[6,160,128]{2,1,0:T(8,128)(2,1)} %get-tuple-element.147.refs_0_, bf16[6,160,128]{2,1,0:T(8,128)(2,1)} %copy-done.13, bf16[6,160,128]{2,1,0:T(8,128)(2,1)} %copy-done.14, ...), custom_call_target="tpu_custom_call" | custom-call | flops 1260257280 | bytes 20971520 | tf_op jit(solution)/shard_map/inverse/pallas_call | solution.py:596
  (194 shorter events, 86.7 us)
Async XLA Ops:
  9.9 30.1 %collective-permute-start.51 = (bf16[6,160,128]{2,1,0:T(8,128)(2,1)}, bf16[6,160,128]{2,1,0:T(8,128)(2,1)S(1)}, u32[]{:S(2)}, u32[]{:S(2)}) collective-permute-start(bf16[6,160,128]{2,1,0:T(8,128)(2,1)} %get-tuple-element.177), channel_id=1, source_target_pairs={{0,4},{1,5},{2,6},{3,7},{4,0},{5,1},{6,2},{7,3},{8,12},{9,13},{10,... | collective-permute-start | bytes 737288 | tf_op jit(solution)/shard_map/ppermute | solution.py:540
  13.1 33.0 %collective-permute-start.52 = (bf16[6,160,128]{2,1,0:T(8,128)(2,1)}, bf16[6,160,128]{2,1,0:T(8,128)(2,1)S(1)}, u32[]{:S(2)}, u32[]{:S(2)}) collective-permute-start(bf16[6,160,128]{2,1,0:T(8,128)(2,1)} %get-tuple-element.178), channel_id=1, source_target_pairs={{0,5},{1,4},{2,7},{3,6},{4,1},{5,0},{6,3},{7,2},{8,13},{9,12},{10,... | collective-permute-start | bytes 737288 | tf_op jit(solution)/shard_map/ppermute | solution.py:540
  14.1 40.6 %collective-permute-start.53 = (bf16[6,160,128]{2,1,0:T(8,128)(2,1)}, bf16[6,160,128]{2,1,0:T(8,128)(2,1)}, u32[]{:S(2)}, u32[]{:S(2)}) collective-permute-start(bf16[6,160,128]{2,1,0:T(8,128)(2,1)} %get-tuple-element.179), channel_id=1, source_target_pairs={{0,6},{1,7},{2,4},{3,5},{4,2},{5,3},{6,0},{7,1},{8,14},{9,15},{10,... | collective-permute-start | bytes 737288 | tf_op jit(solution)/shard_map/ppermute | solution.py:540
  17.4 37.3 %collective-permute-start.54 = (bf16[6,160,128]{2,1,0:T(8,128)(2,1)}, bf16[6,160,128]{2,1,0:T(8,128)(2,1)}, u32[]{:S(2)}, u32[]{:S(2)}) collective-permute-start(bf16[6,160,128]{2,1,0:T(8,128)(2,1)} %get-tuple-element.180), channel_id=1, source_target_pairs={{0,7},{1,6},{2,5},{3,4},{4,3},{5,2},{6,1},{7,0},{8,15},{9,14},{10,... | collective-permute-start | bytes 737288 | tf_op jit(solution)/shard_map/ppermute | solution.py:540
  83.2 94.5 %collective-permute-start.58 = (f32[12,40,641]{2,1,0:T(8,128)}, f32[12,40,641]{2,1,0:T(8,128)}, u32[]{:S(2)}, u32[]{:S(2)}) collective-permute-start(f32[12,40,641]{2,1,0:T(8,128)} %broadcast_select_fusion), channel_id=1, source_target_pairs={{0,16},{8,24},{16,0},{24,8},{1,17},{9,25},{17,1},{25,9},{2,18},{10... | collective-permute-start | bytes 3692168 | tf_op jit(solution)/shard_map/ppermute | solution.py:443
  84.6 119.4 %collective-permute-start.56 = (f32[12,40,641]{2,1,0:T(8,128)S(1)}, f32[12,40,641]{2,1,0:T(8,128)}, u32[]{:S(2)}, u32[]{:S(2)}) collective-permute-start(f32[12,40,641]{2,1,0:T(8,128)S(1)} %broadcast_select_fusion.2), channel_id=1, source_target_pairs={{0,16},{8,24},{16,0},{24,8},{1,17},{9,25},{17,1},{25,9},{2,18},{10... | collective-permute-start | bytes 3692168 | tf_op jit(solution)/shard_map/ppermute | solution.py:443
  88.9 86.5 %collective-permute-start.59 = (bf16[6,160,128]{2,1,0:T(8,128)(2,1)}, bf16[6,160,128]{2,1,0:T(8,128)(2,1)S(1)}, u32[]{:S(2)}, u32[]{:S(2)}) collective-permute-start(bf16[6,160,128]{2,1,0:T(8,128)(2,1)} %get-tuple-element.192), channel_id=1, source_target_pairs={{0,1},{1,0},{2,3},{3,2},{4,5},{5,4},{6,7},{7,6},{8,9},{9,8},{10,11... | collective-permute-start | bytes 737288 | tf_op jit(solution)/shard_map/ppermute | solution.py:540
  89.2 86.9 %collective-permute-start.60 = (bf16[6,160,128]{2,1,0:T(8,128)(2,1)}, bf16[6,160,128]{2,1,0:T(8,128)(2,1)S(1)}, u32[]{:S(2)}, u32[]{:S(2)}) collective-permute-start(bf16[6,160,128]{2,1,0:T(8,128)(2,1)} %get-tuple-element.193), channel_id=1, source_target_pairs={{0,2},{1,3},{2,0},{3,1},{4,6},{5,7},{6,4},{7,5},{8,10},{9,11},{10,... | collective-permute-start | bytes 737288 | tf_op jit(solution)/shard_map/ppermute | solution.py:540
  96.1 60.8 %collective-permute-start.9 = (bf16[12,40,641]{2,1,0:T(8,128)(2,1)S(1)}, bf16[12,40,641]{2,1,0:T(8,128)(2,1)S(1)}, u32[]{:S(2)}, u32[]{:S(2)}) collective-permute-start(bf16[12,40,641]{2,1,0:T(8,128)(2,1)S(1)} %param.11), channel_id=1, source_target_pairs={{8,24},{24,8},{9,25},{25,9},{10,26},{26,10},{11,27},{27,11},{12,28... | collective-permute-start | bytes 1846088 | tf_op jit(solution)/shard_map/cond/branch_5_fun/ppermute | solution.py:431
  183.1 102.2 %collective-permute-start.34 = (bf16[6,160,128]{2,1,0:T(8,128)(2,1)}, bf16[6,160,128]{2,1,0:T(8,128)(2,1)S(1)}, u32[]{:S(2)}, u32[]{:S(2)}) collective-permute-start(bf16[6,160,128]{2,1,0:T(8,128)(2,1)} %get-tuple-element.157), channel_id=1, source_target_pairs={{0,1},{1,0},{2,3},{3,2},{4,5},{5,4},{6,7},{7,6},{8,9},{9,8},{10,11... | collective-permute-start | bytes 737288 | tf_op jit(solution)/shard_map/ppermute | solution.py:540
  184.4 106.4 %collective-permute-start.35 = (bf16[6,160,128]{2,1,0:T(8,128)(2,1)}, bf16[6,160,128]{2,1,0:T(8,128)(2,1)}, u32[]{:S(2)}, u32[]{:S(2)}) collective-permute-start(bf16[6,160,128]{2,1,0:T(8,128)(2,1)} %get-tuple-element.158), channel_id=1, source_target_pairs={{0,2},{1,3},{2,0},{3,1},{4,6},{5,7},{6,4},{7,5},{8,10},{9,11},{10,... | collective-permute-start | bytes 737288 | tf_op jit(solution)/shard_map/ppermute | solution.py:540
  192.5 99.8 %collective-permute-start.36 = (bf16[6,160,128]{2,1,0:T(8,128)(2,1)}, bf16[6,160,128]{2,1,0:T(8,128)(2,1)}, u32[]{:S(2)}, u32[]{:S(2)}) collective-permute-start(bf16[6,160,128]{2,1,0:T(8,128)(2,1)} %get-tuple-element.159), channel_id=1, source_target_pairs={{0,3},{1,2},{2,1},{3,0},{4,7},{5,6},{6,5},{7,4},{8,11},{9,10},{10,... | collective-permute-start | bytes 737288 | tf_op jit(solution)/shard_map/ppermute | solution.py:540
  192.6 99.7 %collective-permute-start.37 = (bf16[6,160,128]{2,1,0:T(8,128)(2,1)}, bf16[6,160,128]{2,1,0:T(8,128)(2,1)}, u32[]{:S(2)}, u32[]{:S(2)}) collective-permute-start(bf16[6,160,128]{2,1,0:T(8,128)(2,1)} %get-tuple-element.160), channel_id=1, source_target_pairs={{0,4},{1,5},{2,6},{3,7},{4,0},{5,1},{6,2},{7,3},{8,12},{9,13},{10,... | collective-permute-start | bytes 737288 | tf_op jit(solution)/shard_map/ppermute | solution.py:540
  218.8 45.5 %collective-permute-start.19 = (bf16[2,6,160,128]{3,2,1,0:T(8,128)(2,1)S(1)}, bf16[2,6,160,128]{3,2,1,0:T(8,128)(2,1)S(1)}, u32[]{:S(2)}, u32[]{:S(2)}) collective-permute-start(bf16[2,6,160,128]{3,2,1,0:T(8,128)(2,1)S(1)} %param.23), channel_id=1, source_target_pairs={{8,24},{24,8},{9,25},{25,9},{10,26},{26,10},{11,27},{27,11},{12,28... | collective-permute-start | bytes 1474568 | tf_op jit(solution)/shard_map/cond/branch_5_fun/ppermute | solution.py:431
  264.3 28.0 %collective-permute-start.38 = (bf16[6,160,128]{2,1,0:T(8,128)(2,1)S(1)}, bf16[6,160,128]{2,1,0:T(8,128)(2,1)S(1)}, u32[]{:S(2)}, u32[]{:S(2)}) collective-permute-start(bf16[6,160,128]{2,1,0:T(8,128)(2,1)S(1)} %copy-done.25), channel_id=1, source_target_pairs={{0,5},{1,4},{2,7},{3,6},{4,1},{5,0},{6,3},{7,2},{8,13},{9,12},{10,... | collective-permute-start | bytes 737288 | tf_op jit(solution)/shard_map/ppermute | solution.py:540
  292.3 30.3 %collective-permute-start.20 = (bf16[6,160,128]{2,1,0:T(8,128)(2,1)}, bf16[6,160,128]{2,1,0:T(8,128)(2,1)S(1)}, u32[]{:S(2)}, u32[]{:S(2)}) collective-permute-start(bf16[6,160,128]{2,1,0:T(8,128)(2,1)} %get-tuple-element.140), channel_id=1, source_target_pairs={{0,1},{1,0},{2,3},{3,2},{4,5},{5,4},{6,7},{7,6},{8,9},{9,8},{10,11... | collective-permute-start | bytes 737288 | tf_op jit(solution)/shard_map/ppermute | solution.py:540
  292.3 30.4 %collective-permute-start.21 = (bf16[6,160,128]{2,1,0:T(8,128)(2,1)}, bf16[6,160,128]{2,1,0:T(8,128)(2,1)S(1)}, u32[]{:S(2)}, u32[]{:S(2)}) collective-permute-start(bf16[6,160,128]{2,1,0:T(8,128)(2,1)} %get-tuple-element.141), channel_id=1, source_target_pairs={{0,2},{1,3},{2,0},{3,1},{4,6},{5,7},{6,4},{7,5},{8,10},{9,11},{10,... | collective-permute-start | bytes 737288 | tf_op jit(solution)/shard_map/ppermute | solution.py:540
  292.4 47.0 %collective-permute-start.22 = (bf16[6,160,128]{2,1,0:T(8,128)(2,1)}, bf16[6,160,128]{2,1,0:T(8,128)(2,1)S(1)}, u32[]{:S(2)}, u32[]{:S(2)}) collective-permute-start(bf16[6,160,128]{2,1,0:T(8,128)(2,1)} %get-tuple-element.142), channel_id=1, source_target_pairs={{0,3},{1,2},{2,1},{3,0},{4,7},{5,6},{6,5},{7,4},{8,11},{9,10},{10,... | collective-permute-start | bytes 737288 | tf_op jit(solution)/shard_map/ppermute | solution.py:540
  297.2 44.3 %collective-permute-start.23 = (bf16[6,160,128]{2,1,0:T(8,128)(2,1)}, bf16[6,160,128]{2,1,0:T(8,128)(2,1)S(1)}, u32[]{:S(2)}, u32[]{:S(2)}) collective-permute-start(bf16[6,160,128]{2,1,0:T(8,128)(2,1)} %get-tuple-element.143), channel_id=1, source_target_pairs={{0,4},{1,5},{2,6},{3,7},{4,0},{5,1},{6,2},{7,3},{8,12},{9,13},{10,... | collective-permute-start | bytes 737288 | tf_op jit(solution)/shard_map/ppermute | solution.py:540
  303.8 37.7 %collective-permute-start.24 = (bf16[6,160,128]{2,1,0:T(8,128)(2,1)}, bf16[6,160,128]{2,1,0:T(8,128)(2,1)S(1)}, u32[]{:S(2)}, u32[]{:S(2)}) collective-permute-start(bf16[6,160,128]{2,1,0:T(8,128)(2,1)} %get-tuple-element.144), channel_id=1, source_target_pairs={{0,5},{1,4},{2,7},{3,6},{4,1},{5,0},{6,3},{7,2},{8,13},{9,12},{10,... | collective-permute-start | bytes 737288 | tf_op jit(solution)/shard_map/ppermute | solution.py:540
  339.4 35.2 %collective-permute-start.41 = (bf16[6,160,128]{2,1,0:T(8,128)(2,1)}, bf16[6,160,128]{2,1,0:T(8,128)(2,1)S(1)}, u32[]{:S(2)}, u32[]{:S(2)}) collective-permute-start(bf16[6,160,128]{2,1,0:T(8,128)(2,1)} %get-tuple-element.165), channel_id=1, source_target_pairs={{0,1},{1,0},{2,3},{3,2},{4,5},{5,4},{6,7},{7,6},{8,9},{9,8},{10,11... | collective-permute-start | bytes 737288 | tf_op jit(solution)/shard_map/ppermute | solution.py:540
  341.5 33.2 %collective-permute-start.42 = (bf16[6,160,128]{2,1,0:T(8,128)(2,1)}, bf16[6,160,128]{2,1,0:T(8,128)(2,1)S(1)}, u32[]{:S(2)}, u32[]{:S(2)}) collective-permute-start(bf16[6,160,128]{2,1,0:T(8,128)(2,1)} %get-tuple-element.166), channel_id=1, source_target_pairs={{0,2},{1,3},{2,0},{3,1},{4,6},{5,7},{6,4},{7,5},{8,10},{9,11},{10,... | collective-permute-start | bytes 737288 | tf_op jit(solution)/shard_map/ppermute | solution.py:540
  341.5 35.9 %collective-permute-start.43 = (bf16[6,160,128]{2,1,0:T(8,128)(2,1)}, bf16[6,160,128]{2,1,0:T(8,128)(2,1)S(1)}, u32[]{:S(2)}, u32[]{:S(2)}) collective-permute-start(bf16[6,160,128]{2,1,0:T(8,128)(2,1)} %get-tuple-element.167), channel_id=1, source_target_pairs={{0,3},{1,2},{2,1},{3,0},{4,7},{5,6},{6,5},{7,4},{8,11},{9,10},{10,... | collective-permute-start | bytes 737288 | tf_op jit(solution)/shard_map/ppermute | solution.py:540
  343.5 35.7 %collective-permute-start.44 = (bf16[6,160,128]{2,1,0:T(8,128)(2,1)}, bf16[6,160,128]{2,1,0:T(8,128)(2,1)S(1)}, u32[]{:S(2)}, u32[]{:S(2)}) collective-permute-start(bf16[6,160,128]{2,1,0:T(8,128)(2,1)} %get-tuple-element.168), channel_id=1, source_target_pairs={{0,4},{1,5},{2,6},{3,7},{4,0},{5,1},{6,2},{7,3},{8,12},{9,13},{10,... | collective-permute-start | bytes 737288 | tf_op jit(solution)/shard_map/ppermute | solution.py:540
  349.4 29.8 %collective-permute-start.45 = (bf16[6,160,128]{2,1,0:T(8,128)(2,1)}, bf16[6,160,128]{2,1,0:T(8,128)(2,1)S(1)}, u32[]{:S(2)}, u32[]{:S(2)}) collective-permute-start(bf16[6,160,128]{2,1,0:T(8,128)(2,1)} %get-tuple-element.169), channel_id=1, source_target_pairs={{0,5},{1,4},{2,7},{3,6},{4,1},{5,0},{6,3},{7,2},{8,13},{9,12},{10,... | collective-permute-start | bytes 737288 | tf_op jit(solution)/shard_map/ppermute | solution.py:540
  377.4 28.7 %collective-permute-start.27 = (bf16[6,160,128]{2,1,0:T(8,128)(2,1)}, bf16[6,160,128]{2,1,0:T(8,128)(2,1)S(1)}, u32[]{:S(2)}, u32[]{:S(2)}) collective-permute-start(bf16[6,160,128]{2,1,0:T(8,128)(2,1)} %get-tuple-element.148), channel_id=1, source_target_pairs={{0,1},{1,0},{2,3},{3,2},{4,5},{5,4},{6,7},{7,6},{8,9},{9,8},{10,11... | collective-permute-start | bytes 737288 | tf_op jit(solution)/shard_map/ppermute | solution.py:540
  379.2 29.2 %collective-permute-start.28 = (bf16[6,160,128]{2,1,0:T(8,128)(2,1)}, bf16[6,160,128]{2,1,0:T(8,128)(2,1)S(1)}, u32[]{:S(2)}, u32[]{:S(2)}) collective-permute-start(bf16[6,160,128]{2,1,0:T(8,128)(2,1)} %get-tuple-element.149), channel_id=1, source_target_pairs={{0,2},{1,3},{2,0},{3,1},{4,6},{5,7},{6,4},{7,5},{8,10},{9,11},{10,... | collective-permute-start | bytes 737288 | tf_op jit(solution)/shard_map/ppermute | solution.py:540
  379.2 57.4 %collective-permute-start.29 = (bf16[6,160,128]{2,1,0:T(8,128)(2,1)}, bf16[6,160,128]{2,1,0:T(8,128)(2,1)S(1)}, u32[]{:S(2)}, u32[]{:S(2)}) collective-permute-start(bf16[6,160,128]{2,1,0:T(8,128)(2,1)} %get-tuple-element.150), channel_id=1, source_target_pairs={{0,3},{1,2},{2,1},{3,0},{4,7},{5,6},{6,5},{7,4},{8,11},{9,10},{10,... | collective-permute-start | bytes 737288 | tf_op jit(solution)/shard_map/ppermute | solution.py:540
  384.2 52.4 %collective-permute-start.30 = (bf16[6,160,128]{2,1,0:T(8,128)(2,1)}, bf16[6,160,128]{2,1,0:T(8,128)(2,1)S(1)}, u32[]{:S(2)}, u32[]{:S(2)}) collective-permute-start(bf16[6,160,128]{2,1,0:T(8,128)(2,1)} %get-tuple-element.151), channel_id=1, source_target_pairs={{0,4},{1,5},{2,6},{3,7},{4,0},{5,1},{6,2},{7,3},{8,12},{9,13},{10,... | collective-permute-start | bytes 737288 | tf_op jit(solution)/shard_map/ppermute | solution.py:540
  391.5 45.2 %collective-permute-start.31 = (bf16[6,160,128]{2,1,0:T(8,128)(2,1)}, bf16[6,160,128]{2,1,0:T(8,128)(2,1)S(1)}, u32[]{:S(2)}, u32[]{:S(2)}) collective-permute-start(bf16[6,160,128]{2,1,0:T(8,128)(2,1)} %get-tuple-element.152), channel_id=1, source_target_pairs={{0,5},{1,4},{2,7},{3,6},{4,1},{5,0},{6,3},{7,2},{8,13},{9,12},{10,... | collective-permute-start | bytes 737288 | tf_op jit(solution)/shard_map/ppermute | solution.py:540
  406.1 30.5 %collective-permute-start.32 = (bf16[6,160,128]{2,1,0:T(8,128)(2,1)}, bf16[6,160,128]{2,1,0:T(8,128)(2,1)}, u32[]{:S(2)}, u32[]{:S(2)}) collective-permute-start(bf16[6,160,128]{2,1,0:T(8,128)(2,1)} %get-tuple-element.153), channel_id=1, source_target_pairs={{0,6},{1,7},{2,4},{3,5},{4,2},{5,3},{6,0},{7,1},{8,14},{9,15},{10,... | collective-permute-start | bytes 737288 | tf_op jit(solution)/shard_map/ppermute | solution.py:540
  408.4 28.3 %collective-permute-start.33 = (bf16[6,160,128]{2,1,0:T(8,128)(2,1)}, bf16[6,160,128]{2,1,0:T(8,128)(2,1)}, u32[]{:S(2)}, u32[]{:S(2)}) collective-permute-start(bf16[6,160,128]{2,1,0:T(8,128)(2,1)} %get-tuple-element.154), channel_id=1, source_target_pairs={{0,7},{1,6},{2,5},{3,4},{4,3},{5,2},{6,1},{7,0},{8,15},{9,14},{10,... | collective-permute-start | bytes 737288 | tf_op jit(solution)/shard_map/ppermute | solution.py:540
  (59 other events, 1037.1 us)
where the time goes:
time: 451 us; the launch traced here: 450 us
  starting transfers between devices  182 us (40%)
  Pallas kernels  133 us (29%)
  waiting for transfers between devices  98.4 us (22%)
  other arithmetic  17.7 us (4%)
  local copies, waits for them, and re-layouts  13.3 us (3%)
  between operations  5.3 us (1%)
    ppermute x42, starting transfers between devices, swap(): got[n] = lax.ppermute(parts[n], 'space', [(d, d ^ n) for d in range(space)])  135 us
    ppermute x4, waiting for transfers between devices, swap(): return lambda v: lax.ppermute(v, 'member', both)  64.4 us
    pallas_call x4, Pallas kernels, forward(): pl.pallas_call(functools.partial(forward_kernel, truncation=truncation, p...  45.9 us
    ppermute x4, starting transfers between devices, swap(): return lambda v: lax.ppermute(v, 'member', both)  43.2 us
    pallas_call x3, Pallas kernels, grid(): pl.pallas_call(functools.partial(grid_kernel, scale=1.0 / truncation), ou...  43.1 us
    pallas_call x3, Pallas kernels, inverse(): pl.pallas_call(functools.partial(inverse_kernel, truncation=truncation, p...  38.6 us
    ppermute x42, waiting for transfers between devices, swap(): got[n] = lax.ppermute(parts[n], 'space', [(d, d ^ n) for d in range(space)])  31.1 us
  transfers between devices with their start and end apart: 50, of which 11 were waited for; matrix products, arithmetic and copies ran while one was open for 6% of the time, Pallas kernels for 21%

commit v1 on v0

--- a/solution.py
+++ b/solution.py
@@ -630,15 +630,16 @@
         )(slot, gravity, stability, *[x for w in ws for x in w], *legs, start, *patches, *mends)
 
     everything = tuple(range(slots))
-    if direct and trajectories % 2 == 0:
-        near, far = everything[: slots // 2], everything[slots // 2 :]
+    halved = direct and trajectories % 2 == 0
+    near, far = everything[: slots // 2], everything[slots // 2 :]
+    if halved:
         first = list(forward(0, far, trajectories // 2, None, []))
         second = list(forward(0, near, trajectories // 2, None, []))
-        made = [second + first]
     else:
-        made = [list(forward(0, everything, trajectories, None, []))]
-
-    turn, made[0][0] = lax.optimization_barrier((clones, made[0][0]))
+        first = list(forward(0, everything, trajectories, None, []))
+
+    turn, first[0] = lax.optimization_barrier((clones, first[0]))
+    made = [second + first if halved else first]
     picked, slot, route = pick_clones(spectra, turn)
     narrow = [send_clone(picked[i], route[i]) for i in range(count)]
     if extra:

time: 451 us -> 458 us (1.016)
  starting transfers between devices: 182 us -> 193 us
  waiting for transfers between devices: 98.4 us -> 93.7 us
    ppermute x42, starting transfers between devices: 135 us -> 146 us  [swap(): got[n] = lax.ppermute(parts[n], 'space', [(d, d ^ n) for d in range(space)])]
    ppermute x4, waiting for transfers between devices: 64.4 us -> 59.2 us  [swap(): return lambda v: lax.ppermute(v, 'member', both)]
  transfers between devices with their start and end apart: 50 -> 50, of which waited for: 11 -> 10; matrix products, arithmetic and copies ran while one was open for 6% -> 6% of each run, Pallas kernels for 21% -> 21%
where the time goes in v1:
time: 458 us; the launch traced here: 457 us
  starting transfers between devices  193 us (42%)
  Pallas kernels  133 us (29%)
  waiting for transfers between devices  93.7 us (20%)
  other arithmetic  17.7 us (4%)
  local copies, waits for them, and re-layouts  14 us (3%)
  between operations  5.28 us (1%)
    ppermute x42, starting transfers between devices, swap(): got[n] = lax.ppermute(parts[n], 'space', [(d, d ^ n) for d in range(space)])  146 us
    ppermute x4, waiting for transfers between devices, swap(): return lambda v: lax.ppermute(v, 'member', both)  59.2 us
    pallas_call x4, Pallas kernels, forward(): pl.pallas_call(functools.partial(forward_kernel, truncation=truncation, p...  45.9 us
    pallas_call x3, Pallas kernels, grid(): pl.pallas_call(functools.partial(grid_kernel, scale=1.0 / truncation), ou...  43.1 us
    ppermute x4, starting transfers between devices, swap(): return lambda v: lax.ppermute(v, 'member', both)  41.9 us
    pallas_call x3, Pallas kernels, inverse(): pl.pallas_call(functools.partial(inverse_kernel, truncation=truncation, p...  38.6 us
    ppermute x42, waiting for transfers between devices, swap(): got[n] = lax.ppermute(parts[n], 'space', [(d, d ^ n) for d in range(space)])  31.6 us
  transfers between devices with their start and end apart: 50, of which 10 were waited for; matrix products, arithmetic and copies ran while one was open for 6% of the time, Pallas kernels for 21%

profile of v1, /device:TPU:1, one launch (start us, length us, event | category | flops | bytes accessed | tf_op | source)
XLA Modules:
  0.0 456.8 jit_solution(13070125729893622526)
XLA Ops:
  0.0 9.9 %forward.7 = (bf16[6,160,128]{2,1,0:T(8,128)(2,1)}, bf16[6,160,128]{2,1,0:T(8,128)(2,1)}, bf16[6,160,128]{2,1,0:T(8,128)(2,1)}, bf16[6,160,128]{2,1,0:T(8,128)(2,1)}) custom-call(f32[4,12,40,641]{3,2,1,0:T(8,128)} %refs_9_.1, bf16[641,40,384]{2,1,0:T(8,128)(2,1)} %bitcast.31), custom_call_target="tpu_custom_call" | custom-call | flops 630128640 | bytes 16777216 | tf_op jit(solution)/shard_map/forward/pallas_call | solution.py:495
  13.3 10.0 %forward.4 = (bf16[6,160,128]{2,1,0:T(8,128)(2,1)}, bf16[6,160,128]{2,1,0:T(8,128)(2,1)}, bf16[6,160,128]{2,1,0:T(8,128)(2,1)}, bf16[6,160,128]{2,1,0:T(8,128)(2,1)}) custom-call(f32[4,12,40,641]{3,2,1,0:T(8,128)} %refs_9_.1, bf16[641,40,384]{2,1,0:T(8,128)(2,1)} %bitcast.32), custom_call_target="tpu_custom_call" | custom-call | flops 630128640 | bytes 16777216 | tf_op jit(solution)/shard_map/forward/pallas_call | solution.py:495
  26.8 6.8 %fusion.3 = bf16[2,321,640]{2,1,0:T(8,128)(2,1)S(1)} fusion(s32[2]{0:T(128)S(1)} %iota_multiply_fusion.1, s32[321,640]{1,0:T(8,128)S(1)} %iota_multiply_fusion), kind=kLoop, calls=%fused_computation.5 | loop fusion | flops 4108800 | bytes 1643528 | tf_op jit(solution)/shard_map/convert_element_type | solution.py:342
  43.5 3.7 copy.11.syn_ref
  47.8 4.6 %collective-permute-done.51.refs_4_ = bf16[6,160,128]{2,1,0:T(8,128)(2,1)} collective-permute-done((bf16[6,160,128]{2,1,0:T(8,128)(2,1)}, bf16[6,160,128]{2,1,0:T(8,128)(2,1)}, u32[]{:S(2)}, u32[]{:S(2)}) %collective-permute-start.51) | collective-permute-done | bytes 245792 | tf_op jit(solution)/shard_map/ppermute | solution.py:540
  52.4 6.3 %collective-permute-done.52.refs_5_ = bf16[6,160,128]{2,1,0:T(8,128)(2,1)} collective-permute-done((bf16[6,160,128]{2,1,0:T(8,128)(2,1)}, bf16[6,160,128]{2,1,0:T(8,128)(2,1)}, u32[]{:S(2)}, u32[]{:S(2)}) %collective-permute-start.52) | collective-permute-done | bytes 245792 | tf_op jit(solution)/shard_map/ppermute | solution.py:540
  58.7 14.4 %grid.5 = (bf16[6,160,128]{2,1,0:T(8,128)(2,1)}, bf16[6,160,128]{2,1,0:T(8,128)(2,1)}, bf16[6,160,128]{2,1,0:T(8,128)(2,1)}, bf16[6,160,128]{2,1,0:T(8,128)(2,1)...) custom-call(s32[8]{0:T(128)} %iota_xor_fusion.order_ref, ...), custom_call_target="tpu_custom_call" | custom-call | flops 5033164800 | bytes 12582912 | tf_op jit(solution)/shard_map/grid/pallas_call | solution.py:574
  92.3 9.9 %collective-permute-start.60 = (bf16[6,160,128]{2,1,0:T(8,128)(2,1)}, bf16[6,160,128]{2,1,0:T(8,128)(2,1)S(1)}, u32[]{:S(2)}, u32[]{:S(2)}) collective-permute-start(bf16[6,160,128]{2,1,0:T(8,128)(2,1)} %get-tuple-element.193), channel_id=1, source_target_pairs={{0,2},{1,3},{2,0},{3,1},{4,6},{5,7},{6,4},{7,5},{8,10},{9,11},{10,... | collective-permute-start | bytes 737288 | tf_op jit(solution)/shard_map/ppermute | solution.py:540
  104.7 55.4 %conditional.5 = (bf16[12,40,641]{2,1,0:T(8,128)(2,1)S(1)}) conditional(s32[]{:T(128)} %bitcast.10, bf16[12,40,641]{2,1,0:T(8,128)(2,1)S(1)} %get-tuple-element.209, bf16[12,40,641]{2,1,0:T(8,128)(2,1)S(1)} %get-tuple-element.209, bf16[12,40,641]{2,1,0:T(8,128)(2,1)S(1)} %get-tuple-element.209, ...), branch_computations={%region_6.7_spmd, %region_7.8_spmd, %region_8.9_spmd, %region_9.10... | conditional | bytes 3692208 | solution.py:435
  107.3 52.7 %collective-permute-done.9 = bf16[12,40,641]{2,1,0:T(8,128)(2,1)S(1)} collective-permute-done((bf16[12,40,641]{2,1,0:T(8,128)(2,1)S(1)}, bf16[12,40,641]{2,1,0:T(8,128)(2,1)S(1)}, u32[]{:S(2)}, u32[]{:S(2)}) %collective-permute-start.9) | collective-permute-done | bytes 615392 | tf_op jit(solution)/shard_map/cond/branch_5_fun/ppermute | solution.py:431
  161.1 13.1 %forward.5 = (bf16[6,160,128]{2,1,0:T(8,128)(2,1)}, bf16[6,160,128]{2,1,0:T(8,128)(2,1)}, bf16[6,160,128]{2,1,0:T(8,128)(2,1)}, bf16[6,160,128]{2,1,0:T(8,128)(2...) custom-call(s32[2]{0:T(128)} %get-tuple-element.137.refs_0_.slot_ref, ...), custom_call_target="tpu_custom_call" | custom-call | flops 1260257280 | bytes 16777216 | tf_op jit(solution)/shard_map/forward/pallas_call | solution.py:495
  174.2 9.9 %collective-permute-start.61 = (bf16[6,160,128]{2,1,0:T(8,128)(2,1)}, bf16[6,160,128]{2,1,0:T(8,128)(2,1)S(1)}, u32[]{:S(2)}, u32[]{:S(2)}) collective-permute-start(bf16[6,160,128]{2,1,0:T(8,128)(2,1)} %get-tuple-element.194), channel_id=1, source_target_pairs={{0,3},{1,2},{2,1},{3,0},{4,7},{5,6},{6,5},{7,4},{8,11},{9,10},{10,... | collective-permute-start | bytes 737288 | tf_op jit(solution)/shard_map/ppermute | solution.py:540
  193.4 5.3 %collective-permute-start.35 = (bf16[6,160,128]{2,1,0:T(8,128)(2,1)}, bf16[6,160,128]{2,1,0:T(8,128)(2,1)}, u32[]{:S(2)}, u32[]{:S(2)}) collective-permute-start(bf16[6,160,128]{2,1,0:T(8,128)(2,1)} %get-tuple-element.158), channel_id=1, source_target_pairs={{0,2},{1,3},{2,0},{3,1},{4,6},{5,7},{6,4},{7,5},{8,10},{9,11},{10,... | collective-permute-start | bytes 737288 | tf_op jit(solution)/shard_map/ppermute | solution.py:540
  202.6 14.0 %collective-permute-start.37 = (bf16[6,160,128]{2,1,0:T(8,128)(2,1)}, bf16[6,160,128]{2,1,0:T(8,128)(2,1)}, u32[]{:S(2)}, u32[]{:S(2)}) collective-permute-start(bf16[6,160,128]{2,1,0:T(8,128)(2,1)} %get-tuple-element.160), channel_id=1, source_target_pairs={{0,4},{1,5},{2,6},{3,7},{4,0},{5,1},{6,2},{7,3},{8,12},{9,13},{10,... | collective-permute-start | bytes 737288 | tf_op jit(solution)/shard_map/ppermute | solution.py:540
  219.3 6.4 %collective-permute-done.65.refs_7_ = bf16[6,160,128]{2,1,0:T(8,128)(2,1)S(1)} collective-permute-done((bf16[6,160,128]{2,1,0:T(8,128)(2,1)S(1)}, bf16[6,160,128]{2,1,0:T(8,128)(2,1)S(1)}, u32[]{:S(2)}, u32[]{:S(2)}) %collective-permute-start.65) | collective-permute-done | bytes 245792 | tf_op jit(solution)/shard_map/ppermute | solution.py:540
  229.0 44.5 %conditional.7 = (bf16[2,6,160,128]{3,2,1,0:T(8,128)(2,1)S(1)}) conditional(s32[]{:T(128)} %bitcast.10, bf16[2,6,160,128]{3,2,1,0:T(8,128)(2,1)S(1)} %get-tuple-element.202, bf16[2,6,160,128]{3,2,1,0:T(8,128)(2,1)S(1)} %get-tuple-element.202, bf16[2,6,160,128]{3,2,1,0:T(8,128)(2,1)S(1)} %get-tuple-element.202, ...), branch_computations={%region_18.19_spmd, %region_19.20_spmd, %region_20.21_spmd, %regio... | conditional | bytes 2949168 | solution.py:435
  229.1 37.9 %collective-permute-start.19 = (bf16[2,6,160,128]{3,2,1,0:T(8,128)(2,1)S(1)}, bf16[2,6,160,128]{3,2,1,0:T(8,128)(2,1)S(1)}, u32[]{:S(2)}, u32[]{:S(2)}) collective-permute-start(bf16[2,6,160,128]{3,2,1,0:T(8,128)(2,1)S(1)} %param.23), channel_id=1, source_target_pairs={{8,24},{24,8},{9,25},{25,9},{10,26},{26,10},{11,27},{27,11},{12,28... | collective-permute-start | bytes 1474568 | tf_op jit(solution)/shard_map/cond/branch_5_fun/ppermute | solution.py:431
  267.0 6.5 %collective-permute-done.19 = bf16[2,6,160,128]{3,2,1,0:T(8,128)(2,1)S(1)} collective-permute-done((bf16[2,6,160,128]{3,2,1,0:T(8,128)(2,1)S(1)}, bf16[2,6,160,128]{3,2,1,0:T(8,128)(2,1)S(1)}, u32[]{:S(2)}, u32[]{:S(2)}) %collective-permute-start.19) | collective-permute-done | bytes 491552 | tf_op jit(solution)/shard_map/cond/branch_5_fun/ppermute | solution.py:431
  273.6 6.9 %collective-permute-start.38 = (bf16[6,160,128]{2,1,0:T(8,128)(2,1)S(1)}, bf16[6,160,128]{2,1,0:T(8,128)(2,1)S(1)}, u32[]{:S(2)}, u32[]{:S(2)}) collective-permute-start(bf16[6,160,128]{2,1,0:T(8,128)(2,1)S(1)} %copy-done.25), channel_id=1, source_target_pairs={{0,5},{1,4},{2,7},{3,6},{4,1},{5,0},{6,3},{7,2},{8,13},{9,12},{10,... | collective-permute-start | bytes 737288 | tf_op jit(solution)/shard_map/ppermute | solution.py:540
  280.5 13.0 %forward.6 = (bf16[6,160,128]{2,1,0:T(8,128)(2,1)}, bf16[6,160,128]{2,1,0:T(8,128)(2,1)}, bf16[6,160,128]{2,1,0:T(8,128)(2,1)}, bf16[6,160,128]{2,1,0:T(8,128)(2...) custom-call(s32[2]{0:T(128)} %get-tuple-element.137.refs_0_.slot_ref, ...), custom_call_target="tpu_custom_call" | custom-call | flops 1260257280 | bytes 16777216 | tf_op jit(solution)/shard_map/forward/pallas_call | solution.py:495
  293.5 5.7 %collective-permute-start.39 = (bf16[6,160,128]{2,1,0:T(8,128)(2,1)S(1)}, bf16[6,160,128]{2,1,0:T(8,128)(2,1)S(1)}, u32[]{:S(2)}, u32[]{:S(2)}) collective-permute-start(bf16[6,160,128]{2,1,0:T(8,128)(2,1)S(1)} %copy-done.24), channel_id=1, source_target_pairs={{0,6},{1,7},{2,4},{3,5},{4,2},{5,3},{6,0},{7,1},{8,14},{9,15},{10,... | collective-permute-start | bytes 737288 | tf_op jit(solution)/shard_map/ppermute | solution.py:540
  306.8 4.5 collective-permute-done.40.refs_7_
  311.2 19.2 %collective-permute-start.24 = (bf16[6,160,128]{2,1,0:T(8,128)(2,1)}, bf16[6,160,128]{2,1,0:T(8,128)(2,1)S(1)}, u32[]{:S(2)}, u32[]{:S(2)}) collective-permute-start(bf16[6,160,128]{2,1,0:T(8,128)(2,1)} %get-tuple-element.144), channel_id=1, source_target_pairs={{0,5},{1,4},{2,7},{3,6},{4,1},{5,0},{6,3},{7,2},{8,13},{9,12},{10,... | collective-permute-start | bytes 737288 | tf_op jit(solution)/shard_map/ppermute | solution.py:540
  333.4 14.3 %grid.4 = (bf16[6,160,128]{2,1,0:T(8,128)(2,1)}, bf16[6,160,128]{2,1,0:T(8,128)(2,1)}, bf16[6,160,128]{2,1,0:T(8,128)(2,1)}, bf16[6,160,128]{2,1,0:T(8,128)(2,1)...) custom-call(s32[8]{0:T(128)} %iota_xor_fusion.order_ref, ...), custom_call_target="tpu_custom_call" | custom-call | flops 5033164800 | bytes 12582912 | tf_op jit(solution)/shard_map/grid/pallas_call | solution.py:574
  351.3 5.2 %collective-permute-start.44 = (bf16[6,160,128]{2,1,0:T(8,128)(2,1)}, bf16[6,160,128]{2,1,0:T(8,128)(2,1)S(1)}, u32[]{:S(2)}, u32[]{:S(2)}) collective-permute-start(bf16[6,160,128]{2,1,0:T(8,128)(2,1)} %get-tuple-element.168), channel_id=1, source_target_pairs={{0,4},{1,5},{2,6},{3,7},{4,0},{5,1},{6,2},{7,3},{8,12},{9,13},{10,... | collective-permute-start | bytes 737288 | tf_op jit(solution)/shard_map/ppermute | solution.py:540
  357.2 10.4 %collective-permute-start.45 = (bf16[6,160,128]{2,1,0:T(8,128)(2,1)}, bf16[6,160,128]{2,1,0:T(8,128)(2,1)S(1)}, u32[]{:S(2)}, u32[]{:S(2)}) collective-permute-start(bf16[6,160,128]{2,1,0:T(8,128)(2,1)} %get-tuple-element.169), channel_id=1, source_target_pairs={{0,5},{1,4},{2,7},{3,6},{4,1},{5,0},{6,3},{7,2},{8,13},{9,12},{10,... | collective-permute-start | bytes 737288 | tf_op jit(solution)/shard_map/ppermute | solution.py:540
  367.6 14.4 %grid.3 = (bf16[6,160,128]{2,1,0:T(8,128)(2,1)}, bf16[6,160,128]{2,1,0:T(8,128)(2,1)}, bf16[6,160,128]{2,1,0:T(8,128)(2,1)}, bf16[6,160,128]{2,1,0:T(8,128)(2,1)...) custom-call(s32[8]{0:T(128)} %iota_xor_fusion.order_ref, ...), custom_call_target="tpu_custom_call" | custom-call | flops 5033164800 | bytes 12582912 | tf_op jit(solution)/shard_map/grid/pallas_call | solution.py:574
  391.7 6.2 %collective-permute-start.30 = (bf16[6,160,128]{2,1,0:T(8,128)(2,1)}, bf16[6,160,128]{2,1,0:T(8,128)(2,1)S(1)}, u32[]{:S(2)}, u32[]{:S(2)}) collective-permute-start(bf16[6,160,128]{2,1,0:T(8,128)(2,1)} %get-tuple-element.151), channel_id=1, source_target_pairs={{0,4},{1,5},{2,6},{3,7},{4,0},{5,1},{6,2},{7,3},{8,12},{9,13},{10,... | collective-permute-start | bytes 737288 | tf_op jit(solution)/shard_map/ppermute | solution.py:540
  398.0 16.4 %collective-permute-start.31 = (bf16[6,160,128]{2,1,0:T(8,128)(2,1)}, bf16[6,160,128]{2,1,0:T(8,128)(2,1)S(1)}, u32[]{:S(2)}, u32[]{:S(2)}) collective-permute-start(bf16[6,160,128]{2,1,0:T(8,128)(2,1)} %get-tuple-element.152), channel_id=1, source_target_pairs={{0,5},{1,4},{2,7},{3,6},{4,1},{5,0},{6,3},{7,2},{8,13},{9,12},{10,... | collective-permute-start | bytes 737288 | tf_op jit(solution)/shard_map/ppermute | solution.py:540
  417.2 14.6 %inverse.3.refs_9_ = f32[4,12,40,641]{3,2,1,0:T(8,128)} custom-call(s32[2]{0:T(128)} %get-tuple-element.137.refs_0_.slot_ref, f32[2,2]{1,0:T(2,128)} %gravity_ref.5, f32[2,2]{1,0:T(2,128)} %stability_ref.5, bf16[6,160,128]{2,1,0:T(8,128)(2,1)} %get-tuple-element.191.refs_0_, bf16[6,160,128]{2,1,0:T(8,128)(2,1)} %copy-done.1, bf16[6,160,128]{2,1,0:T(8,128)(2,1)} %copy-done.2, ...), custom_call_target="tpu_custom_call" | custom-call | flops 1260257280 | bytes 20971520 | tf_op jit(solution)/shard_map/inverse/pallas_call | solution.py:596
  431.9 11.7 %inverse.4.refs_9_ = f32[4,12,40,641]{3,2,1,0:T(8,128)} custom-call(s32[2]{0:T(128)} %get-tuple-element.137.refs_0_.slot_ref, f32[2,2]{1,0:T(2,128)} %gravity_ref.5, f32[2,2]{1,0:T(2,128)} %stability_ref.5, bf16[6,160,128]{2,1,0:T(8,128)(2,1)} %get-tuple-element.164.refs_0_, bf16[6,160,128]{2,1,0:T(8,128)(2,1)} %copy-done.8, bf16[6,160,128]{2,1,0:T(8,128)(2,1)} %copy-done.9, ...), custom_call_target="tpu_custom_call" | custom-call | flops 1260257280 | bytes 20971520 | tf_op jit(solution)/shard_map/inverse/pallas_call | solution.py:596
  444.5 12.3 %inverse.5 = f32[4,12,40,641]{3,2,1,0:T(8,128)} custom-call(s32[2]{0:T(128)} %get-tuple-element.137.refs_0_.slot_ref, f32[2,2]{1,0:T(2,128)} %gravity_ref.5, f32[2,2]{1,0:T(2,128)} %stability_ref.5, bf16[6,160,128]{2,1,0:T(8,128)(2,1)} %get-tuple-element.147.refs_0_, bf16[6,160,128]{2,1,0:T(8,128)(2,1)} %copy-done.13, bf16[6,160,128]{2,1,0:T(8,128)(2,1)} %copy-done.14, ...), custom_call_target="tpu_custom_call" | custom-call | flops 1260257280 | bytes 20971520 | tf_op jit(solution)/shard_map/inverse/pallas_call | solution.py:596
  (194 shorter events, 86.8 us)
Async XLA Ops:
  12.0 28.0 %collective-permute-start.49 = (bf16[6,160,128]{2,1,0:T(8,128)(2,1)}, bf16[6,160,128]{2,1,0:T(8,128)(2,1)S(1)}, u32[]{:S(2)}, u32[]{:S(2)}) collective-permute-start(bf16[6,160,128]{2,1,0:T(8,128)(2,1)} %get-tuple-element.175), channel_id=1, source_target_pairs={{0,2},{1,3},{2,0},{3,1},{4,6},{5,7},{6,4},{7,5},{8,10},{9,11},{10,... | collective-permute-start | bytes 737288 | tf_op jit(solution)/shard_map/ppermute | solution.py:540
  13.3 34.5 %collective-permute-start.50 = (bf16[6,160,128]{2,1,0:T(8,128)(2,1)}, bf16[6,160,128]{2,1,0:T(8,128)(2,1)}, u32[]{:S(2)}, u32[]{:S(2)}) collective-permute-start(bf16[6,160,128]{2,1,0:T(8,128)(2,1)} %get-tuple-element.176), channel_id=1, source_target_pairs={{0,3},{1,2},{2,1},{3,0},{4,7},{5,6},{6,5},{7,4},{8,11},{9,10},{10,... | collective-permute-start | bytes 737288 | tf_op jit(solution)/shard_map/ppermute | solution.py:540
  23.2 29.1 %collective-permute-start.51 = (bf16[6,160,128]{2,1,0:T(8,128)(2,1)}, bf16[6,160,128]{2,1,0:T(8,128)(2,1)}, u32[]{:S(2)}, u32[]{:S(2)}) collective-permute-start(bf16[6,160,128]{2,1,0:T(8,128)(2,1)} %get-tuple-element.177), channel_id=1, source_target_pairs={{0,4},{1,5},{2,6},{3,7},{4,0},{5,1},{6,2},{7,3},{8,12},{9,13},{10,... | collective-permute-start | bytes 737288 | tf_op jit(solution)/shard_map/ppermute | solution.py:540
  25.6 33.1 %collective-permute-start.52 = (bf16[6,160,128]{2,1,0:T(8,128)(2,1)}, bf16[6,160,128]{2,1,0:T(8,128)(2,1)}, u32[]{:S(2)}, u32[]{:S(2)}) collective-permute-start(bf16[6,160,128]{2,1,0:T(8,128)(2,1)} %get-tuple-element.178), channel_id=1, source_target_pairs={{0,5},{1,4},{2,7},{3,6},{4,1},{5,0},{6,3},{7,2},{8,13},{9,12},{10,... | collective-permute-start | bytes 737288 | tf_op jit(solution)/shard_map/ppermute | solution.py:540
  86.3 100.9 %collective-permute-start.58 = (f32[12,40,641]{2,1,0:T(8,128)}, f32[12,40,641]{2,1,0:T(8,128)}, u32[]{:S(2)}, u32[]{:S(2)}) collective-permute-start(f32[12,40,641]{2,1,0:T(8,128)} %broadcast_select_fusion), channel_id=1, source_target_pairs={{0,16},{8,24},{16,0},{24,8},{1,17},{9,25},{17,1},{25,9},{2,18},{10... | collective-permute-start | bytes 3692168 | tf_op jit(solution)/shard_map/ppermute | solution.py:443
  87.7 128.9 %collective-permute-start.56 = (f32[12,40,641]{2,1,0:T(8,128)S(1)}, f32[12,40,641]{2,1,0:T(8,128)}, u32[]{:S(2)}, u32[]{:S(2)}) collective-permute-start(f32[12,40,641]{2,1,0:T(8,128)S(1)} %broadcast_select_fusion.2), channel_id=1, source_target_pairs={{0,16},{8,24},{16,0},{24,8},{1,17},{9,25},{17,1},{25,9},{2,18},{10... | collective-permute-start | bytes 3692168 | tf_op jit(solution)/shard_map/ppermute | solution.py:443
  92.0 92.0 %collective-permute-start.59 = (bf16[6,160,128]{2,1,0:T(8,128)(2,1)}, bf16[6,160,128]{2,1,0:T(8,128)(2,1)S(1)}, u32[]{:S(2)}, u32[]{:S(2)}) collective-permute-start(bf16[6,160,128]{2,1,0:T(8,128)(2,1)} %get-tuple-element.192), channel_id=1, source_target_pairs={{0,1},{1,0},{2,3},{3,2},{4,5},{5,4},{6,7},{7,6},{8,9},{9,8},{10,11... | collective-permute-start | bytes 737288 | tf_op jit(solution)/shard_map/ppermute | solution.py:540
  92.3 93.8 %collective-permute-start.60 = (bf16[6,160,128]{2,1,0:T(8,128)(2,1)}, bf16[6,160,128]{2,1,0:T(8,128)(2,1)S(1)}, u32[]{:S(2)}, u32[]{:S(2)}) collective-permute-start(bf16[6,160,128]{2,1,0:T(8,128)(2,1)} %get-tuple-element.193), channel_id=1, source_target_pairs={{0,2},{1,3},{2,0},{3,1},{4,6},{5,7},{6,4},{7,5},{8,10},{9,11},{10,... | collective-permute-start | bytes 737288 | tf_op jit(solution)/shard_map/ppermute | solution.py:540
  104.8 55.3 %collective-permute-start.9 = (bf16[12,40,641]{2,1,0:T(8,128)(2,1)S(1)}, bf16[12,40,641]{2,1,0:T(8,128)(2,1)S(1)}, u32[]{:S(2)}, u32[]{:S(2)}) collective-permute-start(bf16[12,40,641]{2,1,0:T(8,128)(2,1)S(1)} %param.11), channel_id=1, source_target_pairs={{8,24},{24,8},{9,25},{25,9},{10,26},{26,10},{11,27},{27,11},{12,28... | collective-permute-start | bytes 1846088 | tf_op jit(solution)/shard_map/cond/branch_5_fun/ppermute | solution.py:431
  193.1 100.3 %collective-permute-start.34 = (bf16[6,160,128]{2,1,0:T(8,128)(2,1)}, bf16[6,160,128]{2,1,0:T(8,128)(2,1)S(1)}, u32[]{:S(2)}, u32[]{:S(2)}) collective-permute-start(bf16[6,160,128]{2,1,0:T(8,128)(2,1)} %get-tuple-element.157), channel_id=1, source_target_pairs={{0,1},{1,0},{2,3},{3,2},{4,5},{5,4},{6,7},{7,6},{8,9},{9,8},{10,11... | collective-permute-start | bytes 737288 | tf_op jit(solution)/shard_map/ppermute | solution.py:540
  193.4 105.8 %collective-permute-start.35 = (bf16[6,160,128]{2,1,0:T(8,128)(2,1)}, bf16[6,160,128]{2,1,0:T(8,128)(2,1)}, u32[]{:S(2)}, u32[]{:S(2)}) collective-permute-start(bf16[6,160,128]{2,1,0:T(8,128)(2,1)} %get-tuple-element.158), channel_id=1, source_target_pairs={{0,2},{1,3},{2,0},{3,1},{4,6},{5,7},{6,4},{7,5},{8,10},{9,11},{10,... | collective-permute-start | bytes 737288 | tf_op jit(solution)/shard_map/ppermute | solution.py:540
  201.9 97.8 %collective-permute-start.36 = (bf16[6,160,128]{2,1,0:T(8,128)(2,1)}, bf16[6,160,128]{2,1,0:T(8,128)(2,1)}, u32[]{:S(2)}, u32[]{:S(2)}) collective-permute-start(bf16[6,160,128]{2,1,0:T(8,128)(2,1)} %get-tuple-element.159), channel_id=1, source_target_pairs={{0,3},{1,2},{2,1},{3,0},{4,7},{5,6},{6,5},{7,4},{8,11},{9,10},{10,... | collective-permute-start | bytes 737288 | tf_op jit(solution)/shard_map/ppermute | solution.py:540
  202.6 97.9 %collective-permute-start.37 = (bf16[6,160,128]{2,1,0:T(8,128)(2,1)}, bf16[6,160,128]{2,1,0:T(8,128)(2,1)}, u32[]{:S(2)}, u32[]{:S(2)}) collective-permute-start(bf16[6,160,128]{2,1,0:T(8,128)(2,1)} %get-tuple-element.160), channel_id=1, source_target_pairs={{0,4},{1,5},{2,6},{3,7},{4,0},{5,1},{6,2},{7,3},{8,12},{9,13},{10,... | collective-permute-start | bytes 737288 | tf_op jit(solution)/shard_map/ppermute | solution.py:540
  229.1 44.4 %collective-permute-start.19 = (bf16[2,6,160,128]{3,2,1,0:T(8,128)(2,1)S(1)}, bf16[2,6,160,128]{3,2,1,0:T(8,128)(2,1)S(1)}, u32[]{:S(2)}, u32[]{:S(2)}) collective-permute-start(bf16[2,6,160,128]{3,2,1,0:T(8,128)(2,1)S(1)} %param.23), channel_id=1, source_target_pairs={{8,24},{24,8},{9,25},{25,9},{10,26},{26,10},{11,27},{27,11},{12,28... | collective-permute-start | bytes 1474568 | tf_op jit(solution)/shard_map/cond/branch_5_fun/ppermute | solution.py:431
  273.6 26.9 %collective-permute-start.38 = (bf16[6,160,128]{2,1,0:T(8,128)(2,1)S(1)}, bf16[6,160,128]{2,1,0:T(8,128)(2,1)S(1)}, u32[]{:S(2)}, u32[]{:S(2)}) collective-permute-start(bf16[6,160,128]{2,1,0:T(8,128)(2,1)S(1)} %copy-done.25), channel_id=1, source_target_pairs={{0,5},{1,4},{2,7},{3,6},{4,1},{5,0},{6,3},{7,2},{8,13},{9,12},{10,... | collective-permute-start | bytes 737288 | tf_op jit(solution)/shard_map/ppermute | solution.py:540
  299.7 30.8 %collective-permute-start.20 = (bf16[6,160,128]{2,1,0:T(8,128)(2,1)}, bf16[6,160,128]{2,1,0:T(8,128)(2,1)S(1)}, u32[]{:S(2)}, u32[]{:S(2)}) collective-permute-start(bf16[6,160,128]{2,1,0:T(8,128)(2,1)} %get-tuple-element.140), channel_id=1, source_target_pairs={{0,1},{1,0},{2,3},{3,2},{4,5},{5,4},{6,7},{7,6},{8,9},{9,8},{10,11... | collective-permute-start | bytes 737288 | tf_op jit(solution)/shard_map/ppermute | solution.py:540
  300.5 30.0 %collective-permute-start.21 = (bf16[6,160,128]{2,1,0:T(8,128)(2,1)}, bf16[6,160,128]{2,1,0:T(8,128)(2,1)S(1)}, u32[]{:S(2)}, u32[]{:S(2)}) collective-permute-start(bf16[6,160,128]{2,1,0:T(8,128)(2,1)} %get-tuple-element.141), channel_id=1, source_target_pairs={{0,2},{1,3},{2,0},{3,1},{4,6},{5,7},{6,4},{7,5},{8,10},{9,11},{10,... | collective-permute-start | bytes 737288 | tf_op jit(solution)/shard_map/ppermute | solution.py:540
  300.5 47.2 %collective-permute-start.22 = (bf16[6,160,128]{2,1,0:T(8,128)(2,1)}, bf16[6,160,128]{2,1,0:T(8,128)(2,1)S(1)}, u32[]{:S(2)}, u32[]{:S(2)}) collective-permute-start(bf16[6,160,128]{2,1,0:T(8,128)(2,1)} %get-tuple-element.142), channel_id=1, source_target_pairs={{0,3},{1,2},{2,1},{3,0},{4,7},{5,6},{6,5},{7,4},{8,11},{9,10},{10,... | collective-permute-start | bytes 737288 | tf_op jit(solution)/shard_map/ppermute | solution.py:540
  305.5 43.8 %collective-permute-start.23 = (bf16[6,160,128]{2,1,0:T(8,128)(2,1)}, bf16[6,160,128]{2,1,0:T(8,128)(2,1)S(1)}, u32[]{:S(2)}, u32[]{:S(2)}) collective-permute-start(bf16[6,160,128]{2,1,0:T(8,128)(2,1)} %get-tuple-element.143), channel_id=1, source_target_pairs={{0,4},{1,5},{2,6},{3,7},{4,0},{5,1},{6,2},{7,3},{8,12},{9,13},{10,... | collective-permute-start | bytes 737288 | tf_op jit(solution)/shard_map/ppermute | solution.py:540
  311.2 38.1 %collective-permute-start.24 = (bf16[6,160,128]{2,1,0:T(8,128)(2,1)}, bf16[6,160,128]{2,1,0:T(8,128)(2,1)S(1)}, u32[]{:S(2)}, u32[]{:S(2)}) collective-permute-start(bf16[6,160,128]{2,1,0:T(8,128)(2,1)} %get-tuple-element.144), channel_id=1, source_target_pairs={{0,5},{1,4},{2,7},{3,6},{4,1},{5,0},{6,3},{7,2},{8,13},{9,12},{10,... | collective-permute-start | bytes 737288 | tf_op jit(solution)/shard_map/ppermute | solution.py:540
  347.7 34.3 %collective-permute-start.41 = (bf16[6,160,128]{2,1,0:T(8,128)(2,1)}, bf16[6,160,128]{2,1,0:T(8,128)(2,1)S(1)}, u32[]{:S(2)}, u32[]{:S(2)}) collective-permute-start(bf16[6,160,128]{2,1,0:T(8,128)(2,1)} %get-tuple-element.165), channel_id=1, source_target_pairs={{0,1},{1,0},{2,3},{3,2},{4,5},{5,4},{6,7},{7,6},{8,9},{9,8},{10,11... | collective-permute-start | bytes 737288 | tf_op jit(solution)/shard_map/ppermute | solution.py:540
  349.4 33.4 %collective-permute-start.42 = (bf16[6,160,128]{2,1,0:T(8,128)(2,1)}, bf16[6,160,128]{2,1,0:T(8,128)(2,1)S(1)}, u32[]{:S(2)}, u32[]{:S(2)}) collective-permute-start(bf16[6,160,128]{2,1,0:T(8,128)(2,1)} %get-tuple-element.166), channel_id=1, source_target_pairs={{0,2},{1,3},{2,0},{3,1},{4,6},{5,7},{6,4},{7,5},{8,10},{9,11},{10,... | collective-permute-start | bytes 737288 | tf_op jit(solution)/shard_map/ppermute | solution.py:540
  349.4 36.3 %collective-permute-start.43 = (bf16[6,160,128]{2,1,0:T(8,128)(2,1)}, bf16[6,160,128]{2,1,0:T(8,128)(2,1)S(1)}, u32[]{:S(2)}, u32[]{:S(2)}) collective-permute-start(bf16[6,160,128]{2,1,0:T(8,128)(2,1)} %get-tuple-element.167), channel_id=1, source_target_pairs={{0,3},{1,2},{2,1},{3,0},{4,7},{5,6},{6,5},{7,4},{8,11},{9,10},{10,... | collective-permute-start | bytes 737288 | tf_op jit(solution)/shard_map/ppermute | solution.py:540
  351.3 35.3 %collective-permute-start.44 = (bf16[6,160,128]{2,1,0:T(8,128)(2,1)}, bf16[6,160,128]{2,1,0:T(8,128)(2,1)S(1)}, u32[]{:S(2)}, u32[]{:S(2)}) collective-permute-start(bf16[6,160,128]{2,1,0:T(8,128)(2,1)} %get-tuple-element.168), channel_id=1, source_target_pairs={{0,4},{1,5},{2,6},{3,7},{4,0},{5,1},{6,2},{7,3},{8,12},{9,13},{10,... | collective-permute-start | bytes 737288 | tf_op jit(solution)/shard_map/ppermute | solution.py:540
  357.2 29.4 %collective-permute-start.45 = (bf16[6,160,128]{2,1,0:T(8,128)(2,1)}, bf16[6,160,128]{2,1,0:T(8,128)(2,1)S(1)}, u32[]{:S(2)}, u32[]{:S(2)}) collective-permute-start(bf16[6,160,128]{2,1,0:T(8,128)(2,1)} %get-tuple-element.169), channel_id=1, source_target_pairs={{0,5},{1,4},{2,7},{3,6},{4,1},{5,0},{6,3},{7,2},{8,13},{9,12},{10,... | collective-permute-start | bytes 737288 | tf_op jit(solution)/shard_map/ppermute | solution.py:540
  385.7 28.7 %collective-permute-start.27 = (bf16[6,160,128]{2,1,0:T(8,128)(2,1)}, bf16[6,160,128]{2,1,0:T(8,128)(2,1)S(1)}, u32[]{:S(2)}, u32[]{:S(2)}) collective-permute-start(bf16[6,160,128]{2,1,0:T(8,128)(2,1)} %get-tuple-element.148), channel_id=1, source_target_pairs={{0,1},{1,0},{2,3},{3,2},{4,5},{5,4},{6,7},{7,6},{8,9},{9,8},{10,11... | collective-permute-start | bytes 737288 | tf_op jit(solution)/shard_map/ppermute | solution.py:540
  386.7 30.1 %collective-permute-start.28 = (bf16[6,160,128]{2,1,0:T(8,128)(2,1)}, bf16[6,160,128]{2,1,0:T(8,128)(2,1)S(1)}, u32[]{:S(2)}, u32[]{:S(2)}) collective-permute-start(bf16[6,160,128]{2,1,0:T(8,128)(2,1)} %get-tuple-element.149), channel_id=1, source_target_pairs={{0,2},{1,3},{2,0},{3,1},{4,6},{5,7},{6,4},{7,5},{8,10},{9,11},{10,... | collective-permute-start | bytes 737288 | tf_op jit(solution)/shard_map/ppermute | solution.py:540
  386.7 56.9 %collective-permute-start.29 = (bf16[6,160,128]{2,1,0:T(8,128)(2,1)}, bf16[6,160,128]{2,1,0:T(8,128)(2,1)S(1)}, u32[]{:S(2)}, u32[]{:S(2)}) collective-permute-start(bf16[6,160,128]{2,1,0:T(8,128)(2,1)} %get-tuple-element.150), channel_id=1, source_target_pairs={{0,3},{1,2},{2,1},{3,0},{4,7},{5,6},{6,5},{7,4},{8,11},{9,10},{10,... | collective-permute-start | bytes 737288 | tf_op jit(solution)/shard_map/ppermute | solution.py:540
  391.7 51.9 %collective-permute-start.30 = (bf16[6,160,128]{2,1,0:T(8,128)(2,1)}, bf16[6,160,128]{2,1,0:T(8,128)(2,1)S(1)}, u32[]{:S(2)}, u32[]{:S(2)}) collective-permute-start(bf16[6,160,128]{2,1,0:T(8,128)(2,1)} %get-tuple-element.151), channel_id=1, source_target_pairs={{0,4},{1,5},{2,6},{3,7},{4,0},{5,1},{6,2},{7,3},{8,12},{9,13},{10,... | collective-permute-start | bytes 737288 | tf_op jit(solution)/shard_map/ppermute | solution.py:540
  398.0 45.7 %collective-permute-start.31 = (bf16[6,160,128]{2,1,0:T(8,128)(2,1)}, bf16[6,160,128]{2,1,0:T(8,128)(2,1)S(1)}, u32[]{:S(2)}, u32[]{:S(2)}) collective-permute-start(bf16[6,160,128]{2,1,0:T(8,128)(2,1)} %get-tuple-element.152), channel_id=1, source_target_pairs={{0,5},{1,4},{2,7},{3,6},{4,1},{5,0},{6,3},{7,2},{8,13},{9,12},{10,... | collective-permute-start | bytes 737288 | tf_op jit(solution)/shard_map/ppermute | solution.py:540
  414.4 29.3 %collective-permute-start.32 = (bf16[6,160,128]{2,1,0:T(8,128)(2,1)}, bf16[6,160,128]{2,1,0:T(8,128)(2,1)}, u32[]{:S(2)}, u32[]{:S(2)}) collective-permute-start(bf16[6,160,128]{2,1,0:T(8,128)(2,1)} %get-tuple-element.153), channel_id=1, source_target_pairs={{0,6},{1,7},{2,4},{3,5},{4,2},{5,3},{6,0},{7,1},{8,14},{9,15},{10,... | collective-permute-start | bytes 737288 | tf_op jit(solution)/shard_map/ppermute | solution.py:540
  416.8 26.9 %collective-permute-start.33 = (bf16[6,160,128]{2,1,0:T(8,128)(2,1)}, bf16[6,160,128]{2,1,0:T(8,128)(2,1)}, u32[]{:S(2)}, u32[]{:S(2)}) collective-permute-start(bf16[6,160,128]{2,1,0:T(8,128)(2,1)} %get-tuple-element.154), channel_id=1, source_target_pairs={{0,7},{1,6},{2,5},{3,4},{4,3},{5,2},{6,1},{7,0},{8,15},{9,14},{10,... | collective-permute-start | bytes 737288 | tf_op jit(solution)/shard_map/ppermute | solution.py:540
  (59 other events, 1067.1 us)

commit v2 on v1

--- a/solution.py
+++ b/solution.py
@@ -223,14 +223,15 @@
     stored,
     slots,
     count,
+    patches,
     direct,
 ):
     w_refs, refs = refs[: chunks * slots], refs[chunks * slots :]
     leg_refs, refs = refs[:chunks], refs[chunks:]
     spec_ref, refs = refs[0], refs[1:]
-    patches = count if stored else 0
-    fresh_refs, refs = refs[:patches], refs[patches:]
-    mend_refs, refs = refs[:patches], refs[patches:]
+    mended = count if stored else 0
+    fresh_refs, refs = refs[: 2 * patches], refs[2 * patches :]
+    mend_refs, refs = refs[:mended], refs[mended:]
     out_ref, ws, ten = refs[:3]
     if stored:
         wide = refs[3]
@@ -264,7 +265,7 @@
             for n in range(slots):
                 place = slot_place(n, direct)
                 fill(k, lax.div(place, 2), lax.rem(place, 2), lambda f: w_refs[k * slots + n][f])
-        for i in range(patches):
+        for i in range(mended):
 
             @pl.when(slot_ref[i] >= 0)
             def _():
@@ -318,12 +319,18 @@
                 value = ten[k, pl.ds(at, block), :][:, :width]
                 tend.append(value)
             old = [spec_ref[t, c, :, lanes] for c in range(comps)]
+            for i in range(mended):
+                mine = slot_ref[i] == t
+                old = [jnp.where(mine, 0.0, old[c]) for c in range(comps)]
+            for i in range(patches):
+                here = jnp.logical_and(slot_ref[i] == t, slot_ref[count + i] == 0)
+                there = jnp.logical_and(slot_ref[i] == t, slot_ref[count + i] != 0)
+                for c in range(comps):
+                    old[c] = old[c] + jnp.where(here, fresh_refs[2 * i][c, :, lanes], 0.0)
+                    old[c] = old[c] + jnp.where(there, fresh_refs[2 * i + 1][c, :, lanes], 0.0)
             if last:
                 tend = semi_implicit_slabs(old, tend, terms, hm)
             else:
-                for i in range(patches):
-                    mine = slot_ref[i] == t
-                    old = [jnp.where(mine, fresh_refs[i][c, :, lanes], old[c]) for c in range(comps)]
                 tend = [old[c] + time_step * tend[c] for c in range(comps)]
             for c in range(comps):
                 out_ref[t, c, :, lanes] = tend[c]
@@ -369,6 +376,9 @@
             route = jnp.where(jnp.logical_and(low == a, high == b), 2 + k, route)
         route_ref[0] = route
         slot_ref[i] = jnp.where(target == member, clones_ref[i, 0] - target * local, -1)
+        slot_ref[len(route_refs) + i] = jnp.bitwise_and(
+            jnp.bitwise_xor(source, member), members // 2
+        )
 
 
 def pick_clones(spectra, clones):
@@ -380,7 +390,7 @@
         functools.partial(pick_kernel, local=local),
         out_shape=[
             jax.ShapeDtypeStruct((count,) + block[1:], jnp.bfloat16),
-            jax.ShapeDtypeStruct((count,), jnp.int32),
+            jax.ShapeDtypeStruct((2 * count,), jnp.int32),
         ]
         + [jax.ShapeDtypeStruct((1,), jnp.int32)] * count,
         grid_spec=pltpu.PrefetchScalarGridSpec(
@@ -439,11 +449,12 @@
     members = lax.axis_size("member")
     differs = jnp.bitwise_xor(owner, lax.axis_index("member").astype(jnp.int32))
     bit = 1
-    while bit < members:
+    while True:
         other = lax.ppermute(row, "member", [(m, m ^ bit) for m in range(members)])
+        if 2 * bit >= members:
+            return [row, other]
         row = jnp.where(jnp.bitwise_and(differs, bit) != 0, other, row)
         bit *= 2
-    return row
 
 
 def shards(spectra, legendre, sin_lat, gravity, stability, clones):
@@ -591,7 +602,7 @@
 
     def inverse(ws, legs, start, patches, mends, last):
         chunks = len(ws)
-        stored = bool(patches)
+        stored = bool(mends)
         wide_scratch = pltpu.VMEM((chunks, tiles * LANES * SUB, LANES), jnp.float32)
         return pl.pallas_call(
             functools.partial(
@@ -603,6 +614,7 @@
                 stored=stored,
                 slots=slots,
                 count=count,
+                patches=len(patches) // 2,
                 real_pairs=pairs,
                 direct=direct,
             ),
@@ -648,6 +660,7 @@
     for k in range(1, chunk_count):
         made.append(list(forward(k, everything, trajectories, turn, narrow)))
         turn, made[k][0] = lax.optimization_barrier((slot, made[k][0]))
+    later, made[-1][0] = lax.optimization_barrier((clones[:, 1], made[-1][0]))
     kept = [x[-1] for x in made[1:]]
     sent = []
     for x in made:
@@ -655,8 +668,6 @@
     back = []
     for k in range(chunk_count):
         got = grid(k, sent[k])
-        if k == 0:
-            later, got = lax.optimization_barrier((clones[:, 1], got))
         back.append(collect(got))
     fresh = [
         share_row(
@@ -665,15 +676,16 @@
         )
         for i in range(count)
     ]
+    fresh = [x for pair in fresh for x in pair]
     if extra:
         fresh = [jnp.pad(x, ((0, 0), (0, extra), (0, 0))) for x in fresh]
-    back[0][0], fresh = lax.optimization_barrier((back[0][0], fresh))
     chosen = choose_rows(back[0], clones, trajectories, direct)
     mends = [send_clone(chosen[i], route[i]) for i in range(count)]
-    start = inverse(back[:1], [columns], state, fresh, mends, False)
+    start = inverse(back[:1], [columns], state, [], mends, False)
     for k in range(1, chunk_count - 1):
-        start = inverse(back[k : k + 1], kept[k - 1 : k], start, [], [], False)
-    out = inverse(back[-1:], kept[-1:], start, [], [], True)
+        start = inverse(back[k : k + 1], kept[k - 1 : k], start, fresh, [], False)
+        fresh = []
+    out = inverse(back[-1:], kept[-1:], start, fresh, [], True)
     return out[:, :, :pairs] if extra else out
 
 

time: 458 us -> 397 us (0.87)
  the two profiles are of different devices: /device:TPU:1 before, /device:TPU:10 now
where the time goes in v2:
time: 397 us; the launch traced here: 396 us
  Pallas kernels  135 us (34%)
  starting transfers between devices  118 us (30%)
  waiting for transfers between devices  107 us (27%)
  local copies, waits for them, and re-layouts  16.5 us (4%)
  other arithmetic  14.1 us (4%)
  between operations  5.35 us (1%)
    ppermute x42, waiting for transfers between devices, swap(): got[n] = lax.ppermute(parts[n], 'space', [(d, d ^ n) for d in range(space)])  107 us
    ppermute x42, starting transfers between devices, swap(): got[n] = lax.ppermute(parts[n], 'space', [(d, d ^ n) for d in range(space)])  73.6 us
    pallas_call x4, Pallas kernels, forward(): pl.pallas_call(functools.partial(forward_kernel, truncation=truncation, p...  45.7 us
    pallas_call x3, Pallas kernels, grid(): pl.pallas_call(functools.partial(grid_kernel, scale=1.0 / truncation), ou...  43.1 us
    ppermute x4, starting transfers between devices, share_row(): other = lax.ppermute(row, 'member', [(m, m ^ bit) for m in range(members)])  41.1 us
    pallas_call x3, Pallas kernels, inverse(): pl.pallas_call(functools.partial(inverse_kernel, truncation=truncation, p...  39.8 us
  transfers between devices with their start and end apart: 50, of which 18 were waited for; matrix products, arithmetic and copies ran while one was open for 6% of the time, Pallas kernels for 28%

profile of v2, /device:TPU:10, one launch (start us, length us, event | category | flops | bytes accessed | tf_op | source)
XLA Modules:
  0.0 396.2 jit_solution(9076165312526107950)
XLA Ops:
  0.0 9.9 %forward.7 = (bf16[6,160,128]{2,1,0:T(8,128)(2,1)}, bf16[6,160,128]{2,1,0:T(8,128)(2,1)}, bf16[6,160,128]{2,1,0:T(8,128)(2,1)}, bf16[6,160,128]{2,1,0:T(8,128)(2,1)}) custom-call(f32[4,12,40,641]{3,2,1,0:T(8,128)} %refs_9_.1, bf16[641,40,384]{2,1,0:T(8,128)(2,1)} %bitcast.31), custom_call_target="tpu_custom_call" | custom-call | flops 630128640 | bytes 16777216 | tf_op jit(solution)/shard_map/forward/pallas_call | solution.py:506
  13.4 9.9 %forward.4 = (bf16[6,160,128]{2,1,0:T(8,128)(2,1)}, bf16[6,160,128]{2,1,0:T(8,128)(2,1)}, bf16[6,160,128]{2,1,0:T(8,128)(2,1)}, bf16[6,160,128]{2,1,0:T(8,128)(2,1)}) custom-call(f32[4,12,40,641]{3,2,1,0:T(8,128)} %refs_9_.1, bf16[641,40,384]{2,1,0:T(8,128)(2,1)} %bitcast.32), custom_call_target="tpu_custom_call" | custom-call | flops 630128640 | bytes 16777216 | tf_op jit(solution)/shard_map/forward/pallas_call | solution.py:506
  35.6 6.8 %fusion.3 = bf16[2,321,640]{2,1,0:T(8,128)(2,1)S(1)} fusion(s32[2]{0:T(128)S(1)} %iota_multiply_fusion.1, s32[321,640]{1,0:T(8,128)S(1)} %iota_multiply_fusion), kind=kLoop, calls=%fused_computation.5 | loop fusion | flops 4108800 | bytes 1643528 | tf_op jit(solution)/shard_map/convert_element_type | solution.py:349
  42.4 13.0 %forward.5 = (bf16[6,160,128]{2,1,0:T(8,128)(2,1)}, bf16[6,160,128]{2,1,0:T(8,128)(2,1)}, bf16[6,160,128]{2,1,0:T(8,128)(2,1)}, bf16[6,160,128]{2,1,0:T(8,128)(2...) custom-call(s32[4]{0:T(128)} %get-tuple-element.127.refs_0_.slot_ref, ...), custom_call_target="tpu_custom_call" | custom-call | flops 1260257280 | bytes 16777216 | tf_op jit(solution)/shard_map/forward/pallas_call | solution.py:506
  55.3 13.0 %forward.6 = (bf16[6,160,128]{2,1,0:T(8,128)(2,1)}, bf16[6,160,128]{2,1,0:T(8,128)(2,1)}, bf16[6,160,128]{2,1,0:T(8,128)(2,1)}, bf16[6,160,128]{2,1,0:T(8,128)(2...) custom-call(s32[4]{0:T(128)} %get-tuple-element.127.refs_0_.slot_ref, ...), custom_call_target="tpu_custom_call" | custom-call | flops 1260257280 | bytes 16777216 | tf_op jit(solution)/shard_map/forward/pallas_call | solution.py:506
  78.0 3.8 dynamic-slice_bitcast_fusion
  81.8 21.8 %collective-permute-start.64 = (f32[12,40,641]{2,1,0:T(8,128)}, f32[12,40,641]{2,1,0:T(8,128)}, u32[]{:S(2)}, u32[]{:S(2)}) collective-permute-start(f32[12,40,641]{2,1,0:T(8,128)} %get-tuple-element.187), channel_id=1, source_target_pairs={{0,8},{8,0},{16,24},{24,16},{1,9},{9,1},{17,25},{25,17},{2,10},{10... | collective-permute-start | bytes 3692168 | tf_op jit(solution)/shard_map/ppermute | solution.py:453
  108.1 14.4 %grid.5 = (bf16[6,160,128]{2,1,0:T(8,128)(2,1)}, bf16[6,160,128]{2,1,0:T(8,128)(2,1)}, bf16[6,160,128]{2,1,0:T(8,128)(2,1)}, bf16[6,160,128]{2,1,0:T(8,128)(2,1)...) custom-call(s32[8]{0:T(128)} %iota_xor_fusion.order_ref, ...), custom_call_target="tpu_custom_call" | custom-call | flops 5033164800 | bytes 12582912 | tf_op jit(solution)/shard_map/grid/pallas_call | solution.py:585
  129.1 5.8 %collective-permute-start.58 = (bf16[6,160,128]{2,1,0:T(8,128)(2,1)}, bf16[6,160,128]{2,1,0:T(8,128)(2,1)S(1)}, u32[]{:S(2)}, u32[]{:S(2)}) collective-permute-start(bf16[6,160,128]{2,1,0:T(8,128)(2,1)} %get-tuple-element.176), channel_id=1, source_target_pairs={{0,4},{1,5},{2,6},{3,7},{4,0},{5,1},{6,2},{7,3},{8,12},{9,13},{10,... | collective-permute-start | bytes 737288 | tf_op jit(solution)/shard_map/ppermute | solution.py:551
  136.9 5.4 %collective-permute-done.57.refs_3_ = bf16[6,160,128]{2,1,0:T(8,128)(2,1)S(1)} collective-permute-done((bf16[6,160,128]{2,1,0:T(8,128)(2,1)}, bf16[6,160,128]{2,1,0:T(8,128)(2,1)S(1)}, u32[]{:S(2)}, u32[]{:S(2)}) %collective-permute-start.57) | collective-permute-done | bytes 245792 | tf_op jit(solution)/shard_map/ppermute | solution.py:551
  142.4 14.3 %collective-permute-done.58.refs_4_ = bf16[6,160,128]{2,1,0:T(8,128)(2,1)S(1)} collective-permute-done((bf16[6,160,128]{2,1,0:T(8,128)(2,1)}, bf16[6,160,128]{2,1,0:T(8,128)(2,1)S(1)}, u32[]{:S(2)}, u32[]{:S(2)}) %collective-permute-start.58) | collective-permute-done | bytes 245792 | tf_op jit(solution)/shard_map/ppermute | solution.py:551
  157.8 9.4 %collective-permute-done.59.refs_5_ = bf16[6,160,128]{2,1,0:T(8,128)(2,1)S(1)} collective-permute-done((bf16[6,160,128]{2,1,0:T(8,128)(2,1)}, bf16[6,160,128]{2,1,0:T(8,128)(2,1)S(1)}, u32[]{:S(2)}, u32[]{:S(2)}) %collective-permute-start.59) | collective-permute-done | bytes 245792 | tf_op jit(solution)/shard_map/ppermute | solution.py:551
  168.7 4.8 %collective-permute-done.60.refs_6_ = bf16[6,160,128]{2,1,0:T(8,128)(2,1)S(1)} collective-permute-done((bf16[6,160,128]{2,1,0:T(8,128)(2,1)}, bf16[6,160,128]{2,1,0:T(8,128)(2,1)S(1)}, u32[]{:S(2)}, u32[]{:S(2)}) %collective-permute-start.60) | collective-permute-done | bytes 245792 | tf_op jit(solution)/shard_map/ppermute | solution.py:551
  173.5 4.6 %collective-permute-done.61.refs_7_ = bf16[6,160,128]{2,1,0:T(8,128)(2,1)S(1)} collective-permute-done((bf16[6,160,128]{2,1,0:T(8,128)(2,1)}, bf16[6,160,128]{2,1,0:T(8,128)(2,1)S(1)}, u32[]{:S(2)}, u32[]{:S(2)}) %collective-permute-start.61) | collective-permute-done | bytes 245792 | tf_op jit(solution)/shard_map/ppermute | solution.py:551
  194.0 8.6 %collective-permute-done.37.refs_4_ = bf16[6,160,128]{2,1,0:T(8,128)(2,1)S(1)} collective-permute-done((bf16[6,160,128]{2,1,0:T(8,128)(2,1)}, bf16[6,160,128]{2,1,0:T(8,128)(2,1)S(1)}, u32[]{:S(2)}, u32[]{:S(2)}) %collective-permute-start.37) | collective-permute-done | bytes 245792 | tf_op jit(solution)/shard_map/ppermute | solution.py:551
  208.5 4.6 %collective-permute-done.39.refs_6_ = bf16[6,160,128]{2,1,0:T(8,128)(2,1)S(1)} collective-permute-done((bf16[6,160,128]{2,1,0:T(8,128)(2,1)}, bf16[6,160,128]{2,1,0:T(8,128)(2,1)S(1)}, u32[]{:S(2)}, u32[]{:S(2)}) %collective-permute-start.39) | collective-permute-done | bytes 245792 | tf_op jit(solution)/shard_map/ppermute | solution.py:551
  215.0 4.9 %collective-permute-start.23 = (bf16[6,160,128]{2,1,0:T(8,128)(2,1)S(1)}, bf16[6,160,128]{2,1,0:T(8,128)(2,1)S(1)}, u32[]{:S(2)}, u32[]{:S(2)}) collective-permute-start(bf16[6,160,128]{2,1,0:T(8,128)(2,1)S(1)} %copy-done.27), channel_id=1, source_target_pairs={{0,4},{1,5},{2,6},{3,7},{4,0},{5,1},{6,2},{7,3},{8,12},{9,13},{10,... | collective-permute-start | bytes 737288 | tf_op jit(solution)/shard_map/ppermute | solution.py:551
  221.5 6.1 %collective-permute-done.40.refs_7_ = bf16[6,160,128]{2,1,0:T(8,128)(2,1)S(1)} collective-permute-done((bf16[6,160,128]{2,1,0:T(8,128)(2,1)S(1)}, bf16[6,160,128]{2,1,0:T(8,128)(2,1)S(1)}, u32[]{:S(2)}, u32[]{:S(2)}) %collective-permute-start.40) | collective-permute-done | bytes 245792 | tf_op jit(solution)/shard_map/ppermute | solution.py:551
  231.7 14.7 %collective-permute-start.65 = (f32[12,40,641]{2,1,0:T(8,128)S(1)}, f32[12,40,641]{2,1,0:T(8,128)}, u32[]{:S(2)}, u32[]{:S(2)}) collective-permute-start(f32[12,40,641]{2,1,0:T(8,128)S(1)} %broadcast_select_fusion.refs_12_), channel_id=1, source_target_pairs={{0,16},{8,24},{16,0},{24,8},{1,17},{9,25},{17,1},{25,9},{2,18},{10... | collective-permute-start | bytes 3692168 | tf_op jit(solution)/shard_map/ppermute | solution.py:453
  246.5 4.6 %collective-permute-start.63 = (f32[12,40,641]{2,1,0:T(8,128)S(1)}, f32[12,40,641]{2,1,0:T(8,128)}, u32[]{:S(2)}, u32[]{:S(2)}) collective-permute-start(f32[12,40,641]{2,1,0:T(8,128)S(1)} %broadcast_select_fusion.1.refs_10_), channel_id=1, source_target_pairs={{0,16},{8,24},{16,0},{24,8},{1,17},{9,25},{17,1},{25,9},{2,18},{10... | collective-permute-start | bytes 3692168 | tf_op jit(solution)/shard_map/ppermute | solution.py:453
  251.1 14.4 %grid.4 = (bf16[6,160,128]{2,1,0:T(8,128)(2,1)}, bf16[6,160,128]{2,1,0:T(8,128)(2,1)}, bf16[6,160,128]{2,1,0:T(8,128)(2,1)}, bf16[6,160,128]{2,1,0:T(8,128)(2,1)...) custom-call(s32[8]{0:T(128)} %iota_xor_fusion.order_ref, ...), custom_call_target="tpu_custom_call" | custom-call | flops 5033164800 | bytes 12582912 | tf_op jit(solution)/shard_map/grid/pallas_call | solution.py:585
  265.6 20.1 %collective-permute-start.42 = (bf16[6,160,128]{2,1,0:T(8,128)(2,1)}, bf16[6,160,128]{2,1,0:T(8,128)(2,1)S(1)}, u32[]{:S(2)}, u32[]{:S(2)}) collective-permute-start(bf16[6,160,128]{2,1,0:T(8,128)(2,1)} %get-tuple-element.157), channel_id=1, source_target_pairs={{0,2},{1,3},{2,0},{3,1},{4,6},{5,7},{6,4},{7,5},{8,10},{9,11},{10,... | collective-permute-start | bytes 737288 | tf_op jit(solution)/shard_map/ppermute | solution.py:551
  285.8 5.4 %collective-permute-done.42.refs_2_ = bf16[6,160,128]{2,1,0:T(8,128)(2,1)S(1)} collective-permute-done((bf16[6,160,128]{2,1,0:T(8,128)(2,1)}, bf16[6,160,128]{2,1,0:T(8,128)(2,1)S(1)}, u32[]{:S(2)}, u32[]{:S(2)}) %collective-permute-start.42) | collective-permute-done | bytes 245792 | tf_op jit(solution)/shard_map/ppermute | solution.py:551
  291.2 8.0 %collective-permute-done.43.refs_3_ = bf16[6,160,128]{2,1,0:T(8,128)(2,1)S(1)} collective-permute-done((bf16[6,160,128]{2,1,0:T(8,128)(2,1)}, bf16[6,160,128]{2,1,0:T(8,128)(2,1)S(1)}, u32[]{:S(2)}, u32[]{:S(2)}) %collective-permute-start.43) | collective-permute-done | bytes 245792 | tf_op jit(solution)/shard_map/ppermute | solution.py:551
  300.0 14.3 %grid.3 = (bf16[6,160,128]{2,1,0:T(8,128)(2,1)}, bf16[6,160,128]{2,1,0:T(8,128)(2,1)}, bf16[6,160,128]{2,1,0:T(8,128)(2,1)}, bf16[6,160,128]{2,1,0:T(8,128)(2,1)...) custom-call(s32[8]{0:T(128)} %iota_xor_fusion.order_ref, ...), custom_call_target="tpu_custom_call" | custom-call | flops 5033164800 | bytes 12582912 | tf_op jit(solution)/shard_map/grid/pallas_call | solution.py:585
  317.2 12.1 %collective-permute-done.46.refs_6_ = bf16[6,160,128]{2,1,0:T(8,128)(2,1)} collective-permute-done((bf16[6,160,128]{2,1,0:T(8,128)(2,1)}, bf16[6,160,128]{2,1,0:T(8,128)(2,1)}, u32[]{:S(2)}, u32[]{:S(2)}) %collective-permute-start.46) | collective-permute-done | bytes 245792 | tf_op jit(solution)/shard_map/ppermute | solution.py:551
  329.3 6.7 %collective-permute-done.47.refs_7_ = bf16[6,160,128]{2,1,0:T(8,128)(2,1)S(1)} collective-permute-done((bf16[6,160,128]{2,1,0:T(8,128)(2,1)}, bf16[6,160,128]{2,1,0:T(8,128)(2,1)S(1)}, u32[]{:S(2)}, u32[]{:S(2)}) %collective-permute-start.47) | collective-permute-done | bytes 245792 | tf_op jit(solution)/shard_map/ppermute | solution.py:551
  342.0 13.2 %inverse.3.refs_9_ = f32[4,12,40,641]{3,2,1,0:T(8,128)} custom-call(s32[4]{0:T(128)} %get-tuple-element.127.refs_0_.slot_ref, f32[2,2]{1,0:T(2,128)} %gravity_ref.5, f32[2,2]{1,0:T(2,128)} %stability_ref.5, bf16[6,160,128]{2,1,0:T(8,128)(2,1)} %get-tuple-element.172.refs_0_, bf16[6,160,128]{2,1,0:T(8,128)(2,1)} %copy-done.6, bf16[6,160,128]{2,1,0:T(8,128)(2,1)} %copy-done.7, ...), custom_call_target="tpu_custom_call" | custom-call | flops 1260257280 | bytes 20971520 | tf_op jit(solution)/shard_map/inverse/pallas_call | solution.py:607
  355.2 14.3 %inverse.4.refs_9_ = f32[4,12,40,641]{3,2,1,0:T(8,128)} custom-call(s32[4]{0:T(128)} %get-tuple-element.127.refs_0_.slot_ref, f32[2,2]{1,0:T(2,128)} %gravity_ref.5, f32[2,2]{1,0:T(2,128)} %stability_ref.5, bf16[6,160,128]{2,1,0:T(8,128)(2,1)} %get-tuple-element.155.refs_0_, bf16[6,160,128]{2,1,0:T(8,128)(2,1)} %copy-done.15, ...), custom_call_target="tpu_custom_call" | custom-call | flops 1260257280 | bytes 20971520 | tf_op jit(solution)/shard_map/inverse/pallas_call | solution.py:607
  370.2 7.1 %collective-permute-done.32.refs_6_ = bf16[6,160,128]{2,1,0:T(8,128)(2,1)S(1)} collective-permute-done((bf16[6,160,128]{2,1,0:T(8,128)(2,1)}, bf16[6,160,128]{2,1,0:T(8,128)(2,1)S(1)}, u32[]{:S(2)}, u32[]{:S(2)}) %collective-permute-start.32) | collective-permute-done | bytes 245792 | tf_op jit(solution)/shard_map/ppermute | solution.py:551
  377.2 6.0 %collective-permute-done.33.refs_7_ = bf16[6,160,128]{2,1,0:T(8,128)(2,1)S(1)} collective-permute-done((bf16[6,160,128]{2,1,0:T(8,128)(2,1)}, bf16[6,160,128]{2,1,0:T(8,128)(2,1)S(1)}, u32[]{:S(2)}, u32[]{:S(2)}) %collective-permute-start.33) | collective-permute-done | bytes 245792 | tf_op jit(solution)/shard_map/ppermute | solution.py:551
  383.9 12.3 %inverse.5 = f32[4,12,40,641]{3,2,1,0:T(8,128)} custom-call(s32[4]{0:T(128)} %get-tuple-element.127.refs_0_.slot_ref, f32[2,2]{1,0:T(2,128)} %gravity_ref.5, f32[2,2]{1,0:T(2,128)} %stability_ref.5, bf16[6,160,128]{2,1,0:T(8,128)(2,1)} %get-tuple-element.138.refs_0_, bf16[6,160,128]{2,1,0:T(8,128)(2,1)} %copy-done.18, bf16[6,160,128]{2,1,0:T(8,128)(2,1)} %copy-done.19, ...), custom_call_target="tpu_custom_call" | custom-call | flops 1260257280 | bytes 20971520 | tf_op jit(solution)/shard_map/inverse/pallas_call | solution.py:607
  (194 shorter events, 80.6 us)
Async XLA Ops:
  9.9 66.0 %collective-permute-start.48 = (bf16[6,160,128]{2,1,0:T(8,128)(2,1)}, bf16[6,160,128]{2,1,0:T(8,128)(2,1)S(1)}, u32[]{:S(2)}, u32[]{:S(2)}) collective-permute-start(bf16[6,160,128]{2,1,0:T(8,128)(2,1)} %get-tuple-element.165), channel_id=1, source_target_pairs={{0,1},{1,0},{2,3},{3,2},{4,5},{5,4},{6,7},{7,6},{8,9},{9,8},{10,11... | collective-permute-start | bytes 737288 | tf_op jit(solution)/shard_map/ppermute | solution.py:551
  11.4 66.1 %collective-permute-start.49 = (bf16[6,160,128]{2,1,0:T(8,128)(2,1)}, bf16[6,160,128]{2,1,0:T(8,128)(2,1)}, u32[]{:S(2)}, u32[]{:S(2)}) collective-permute-start(bf16[6,160,128]{2,1,0:T(8,128)(2,1)} %get-tuple-element.166), channel_id=1, source_target_pairs={{0,2},{1,3},{2,0},{3,1},{4,6},{5,7},{6,4},{7,5},{8,10},{9,11},{10,... | collective-permute-start | bytes 737288 | tf_op jit(solution)/shard_map/ppermute | solution.py:551
  11.9 69.9 %collective-permute-start.50 = (bf16[6,160,128]{2,1,0:T(8,128)(2,1)}, bf16[6,160,128]{2,1,0:T(8,128)(2,1)}, u32[]{:S(2)}, u32[]{:S(2)}) collective-permute-start(bf16[6,160,128]{2,1,0:T(8,128)(2,1)} %get-tuple-element.167), channel_id=1, source_target_pairs={{0,3},{1,2},{2,1},{3,0},{4,7},{5,6},{6,5},{7,4},{8,11},{9,10},{10,... | collective-permute-start | bytes 737288 | tf_op jit(solution)/shard_map/ppermute | solution.py:551
  23.3 84.8 %collective-permute-start.51 = (bf16[6,160,128]{2,1,0:T(8,128)(2,1)}, bf16[6,160,128]{2,1,0:T(8,128)(2,1)}, u32[]{:S(2)}, u32[]{:S(2)}) collective-permute-start(bf16[6,160,128]{2,1,0:T(8,128)(2,1)} %get-tuple-element.168), channel_id=1, source_target_pairs={{0,4},{1,5},{2,6},{3,7},{4,0},{5,1},{6,2},{7,3},{8,12},{9,13},{10,... | collective-permute-start | bytes 737288 | tf_op jit(solution)/shard_map/ppermute | solution.py:551
  33.9 74.2 %collective-permute-start.52 = (bf16[6,160,128]{2,1,0:T(8,128)(2,1)}, bf16[6,160,128]{2,1,0:T(8,128)(2,1)}, u32[]{:S(2)}, u32[]{:S(2)}) collective-permute-start(bf16[6,160,128]{2,1,0:T(8,128)(2,1)} %get-tuple-element.169), channel_id=1, source_target_pairs={{0,5},{1,4},{2,7},{3,6},{4,1},{5,0},{6,3},{7,2},{8,13},{9,12},{10,... | collective-permute-start | bytes 737288 | tf_op jit(solution)/shard_map/ppermute | solution.py:551
  75.9 32.2 %collective-permute-start.53 = (bf16[6,160,128]{2,1,0:T(8,128)(2,1)}, bf16[6,160,128]{2,1,0:T(8,128)(2,1)}, u32[]{:S(2)}, u32[]{:S(2)}) collective-permute-start(bf16[6,160,128]{2,1,0:T(8,128)(2,1)} %get-tuple-element.170), channel_id=1, source_target_pairs={{0,6},{1,7},{2,4},{3,5},{4,2},{5,3},{6,0},{7,1},{8,14},{9,15},{10,... | collective-permute-start | bytes 737288 | tf_op jit(solution)/shard_map/ppermute | solution.py:551
  77.6 30.5 %collective-permute-start.54 = (bf16[6,160,128]{2,1,0:T(8,128)(2,1)}, bf16[6,160,128]{2,1,0:T(8,128)(2,1)}, u32[]{:S(2)}, u32[]{:S(2)}) collective-permute-start(bf16[6,160,128]{2,1,0:T(8,128)(2,1)} %get-tuple-element.171), channel_id=1, source_target_pairs={{0,7},{1,6},{2,5},{3,4},{4,3},{5,2},{6,1},{7,0},{8,15},{9,14},{10,... | collective-permute-start | bytes 737288 | tf_op jit(solution)/shard_map/ppermute | solution.py:551
  81.8 107.1 %collective-permute-start.64 = (f32[12,40,641]{2,1,0:T(8,128)}, f32[12,40,641]{2,1,0:T(8,128)}, u32[]{:S(2)}, u32[]{:S(2)}) collective-permute-start(f32[12,40,641]{2,1,0:T(8,128)} %get-tuple-element.187), channel_id=1, source_target_pairs={{0,8},{8,0},{16,24},{24,16},{1,9},{9,1},{17,25},{25,17},{2,10},{10... | collective-permute-start | bytes 3692168 | tf_op jit(solution)/shard_map/ppermute | solution.py:453
  108.1 105.7 %collective-permute-start.62 = (f32[12,40,641]{2,1,0:T(8,128)}, f32[12,40,641]{2,1,0:T(8,128)S(1)}, u32[]{:S(2)}, u32[]{:S(2)}) collective-permute-start(f32[12,40,641]{2,1,0:T(8,128)} %get-tuple-element.188), channel_id=1, source_target_pairs={{0,8},{8,0},{16,24},{24,16},{1,9},{9,1},{17,25},{25,17},{2,10},{10... | collective-permute-start | bytes 3692168 | tf_op jit(solution)/shard_map/ppermute | solution.py:453
  129.1 27.6 %collective-permute-start.58 = (bf16[6,160,128]{2,1,0:T(8,128)(2,1)}, bf16[6,160,128]{2,1,0:T(8,128)(2,1)S(1)}, u32[]{:S(2)}, u32[]{:S(2)}) collective-permute-start(bf16[6,160,128]{2,1,0:T(8,128)(2,1)} %get-tuple-element.176), channel_id=1, source_target_pairs={{0,4},{1,5},{2,6},{3,7},{4,0},{5,1},{6,2},{7,3},{8,12},{9,13},{10,... | collective-permute-start | bytes 737288 | tf_op jit(solution)/shard_map/ppermute | solution.py:551
  134.9 32.3 %collective-permute-start.59 = (bf16[6,160,128]{2,1,0:T(8,128)(2,1)}, bf16[6,160,128]{2,1,0:T(8,128)(2,1)S(1)}, u32[]{:S(2)}, u32[]{:S(2)}) collective-permute-start(bf16[6,160,128]{2,1,0:T(8,128)(2,1)} %get-tuple-element.177), channel_id=1, source_target_pairs={{0,5},{1,4},{2,7},{3,6},{4,1},{5,0},{6,3},{7,2},{8,13},{9,12},{10,... | collective-permute-start | bytes 737288 | tf_op jit(solution)/shard_map/ppermute | solution.py:551
  142.2 31.2 %collective-permute-start.60 = (bf16[6,160,128]{2,1,0:T(8,128)(2,1)}, bf16[6,160,128]{2,1,0:T(8,128)(2,1)S(1)}, u32[]{:S(2)}, u32[]{:S(2)}) collective-permute-start(bf16[6,160,128]{2,1,0:T(8,128)(2,1)} %get-tuple-element.178), channel_id=1, source_target_pairs={{0,6},{1,7},{2,4},{3,5},{4,2},{5,3},{6,0},{7,1},{8,14},{9,15},{10,... | collective-permute-start | bytes 737288 | tf_op jit(solution)/shard_map/ppermute | solution.py:551
  189.0 24.1 %collective-permute-start.39 = (bf16[6,160,128]{2,1,0:T(8,128)(2,1)}, bf16[6,160,128]{2,1,0:T(8,128)(2,1)S(1)}, u32[]{:S(2)}, u32[]{:S(2)}) collective-permute-start(bf16[6,160,128]{2,1,0:T(8,128)(2,1)} %get-tuple-element.153), channel_id=1, source_target_pairs={{0,6},{1,7},{2,4},{3,5},{4,2},{5,3},{6,0},{7,1},{8,14},{9,15},{10,... | collective-permute-start | bytes 737288 | tf_op jit(solution)/shard_map/ppermute | solution.py:551
  191.6 36.0 %collective-permute-start.40 = (bf16[6,160,128]{2,1,0:T(8,128)(2,1)S(1)}, bf16[6,160,128]{2,1,0:T(8,128)(2,1)S(1)}, u32[]{:S(2)}, u32[]{:S(2)}) collective-permute-start(bf16[6,160,128]{2,1,0:T(8,128)(2,1)S(1)} %copy-done.31), channel_id=1, source_target_pairs={{0,7},{1,6},{2,5},{3,4},{4,3},{5,2},{6,1},{7,0},{8,15},{9,14},{10,... | collective-permute-start | bytes 737288 | tf_op jit(solution)/shard_map/ppermute | solution.py:551
  203.3 24.4 %collective-permute-start.20 = (bf16[6,160,128]{2,1,0:T(8,128)(2,1)S(1)}, bf16[6,160,128]{2,1,0:T(8,128)(2,1)S(1)}, u32[]{:S(2)}, u32[]{:S(2)}) collective-permute-start(bf16[6,160,128]{2,1,0:T(8,128)(2,1)S(1)} %copy-done.30), channel_id=1, source_target_pairs={{0,1},{1,0},{2,3},{3,2},{4,5},{5,4},{6,7},{7,6},{8,9},{9,8},{10,11... | collective-permute-start | bytes 737288 | tf_op jit(solution)/shard_map/ppermute | solution.py:551
  205.9 25.2 %collective-permute-start.21 = (bf16[6,160,128]{2,1,0:T(8,128)(2,1)S(1)}, bf16[6,160,128]{2,1,0:T(8,128)(2,1)S(1)}, u32[]{:S(2)}, u32[]{:S(2)}) collective-permute-start(bf16[6,160,128]{2,1,0:T(8,128)(2,1)S(1)} %copy-done.29), channel_id=1, source_target_pairs={{0,2},{1,3},{2,0},{3,1},{4,6},{5,7},{6,4},{7,5},{8,10},{9,11},{10,... | collective-permute-start | bytes 737288 | tf_op jit(solution)/shard_map/ppermute | solution.py:551
  215.0 31.4 %collective-permute-start.23 = (bf16[6,160,128]{2,1,0:T(8,128)(2,1)S(1)}, bf16[6,160,128]{2,1,0:T(8,128)(2,1)S(1)}, u32[]{:S(2)}, u32[]{:S(2)}) collective-permute-start(bf16[6,160,128]{2,1,0:T(8,128)(2,1)S(1)} %copy-done.27), channel_id=1, source_target_pairs={{0,4},{1,5},{2,6},{3,7},{4,0},{5,1},{6,2},{7,3},{8,12},{9,13},{10,... | collective-permute-start | bytes 737288 | tf_op jit(solution)/shard_map/ppermute | solution.py:551
  227.6 37.9 %collective-permute-start.24 = (bf16[6,160,128]{2,1,0:T(8,128)(2,1)}, bf16[6,160,128]{2,1,0:T(8,128)(2,1)}, u32[]{:S(2)}, u32[]{:S(2)}) collective-permute-start(bf16[6,160,128]{2,1,0:T(8,128)(2,1)} %get-tuple-element.135), channel_id=1, source_target_pairs={{0,5},{1,4},{2,7},{3,6},{4,1},{5,0},{6,3},{7,2},{8,13},{9,12},{10,... | collective-permute-start | bytes 737288 | tf_op jit(solution)/shard_map/ppermute | solution.py:551
  227.6 37.9 %collective-permute-start.25 = (bf16[6,160,128]{2,1,0:T(8,128)(2,1)S(1)}, bf16[6,160,128]{2,1,0:T(8,128)(2,1)}, u32[]{:S(2)}, u32[]{:S(2)}) collective-permute-start(bf16[6,160,128]{2,1,0:T(8,128)(2,1)S(1)} %copy-done.26), channel_id=1, source_target_pairs={{0,6},{1,7},{2,4},{3,5},{4,2},{5,3},{6,0},{7,1},{8,14},{9,15},{10,... | collective-permute-start | bytes 737288 | tf_op jit(solution)/shard_map/ppermute | solution.py:551
  231.1 54.6 %collective-permute-start.26 = (bf16[6,160,128]{2,1,0:T(8,128)(2,1)S(1)}, bf16[6,160,128]{2,1,0:T(8,128)(2,1)}, u32[]{:S(2)}, u32[]{:S(2)}) collective-permute-start(bf16[6,160,128]{2,1,0:T(8,128)(2,1)S(1)} %copy-done.25), channel_id=1, source_target_pairs={{0,7},{1,6},{2,5},{3,4},{4,3},{5,2},{6,1},{7,0},{8,15},{9,14},{10,... | collective-permute-start | bytes 737288 | tf_op jit(solution)/shard_map/ppermute | solution.py:551
  231.7 106.7 %collective-permute-start.65 = (f32[12,40,641]{2,1,0:T(8,128)S(1)}, f32[12,40,641]{2,1,0:T(8,128)}, u32[]{:S(2)}, u32[]{:S(2)}) collective-permute-start(f32[12,40,641]{2,1,0:T(8,128)S(1)} %broadcast_select_fusion.refs_12_), channel_id=1, source_target_pairs={{0,16},{8,24},{16,0},{24,8},{1,17},{9,25},{17,1},{25,9},{2,18},{10... | collective-permute-start | bytes 3692168 | tf_op jit(solution)/shard_map/ppermute | solution.py:453
  246.5 94.9 %collective-permute-start.63 = (f32[12,40,641]{2,1,0:T(8,128)S(1)}, f32[12,40,641]{2,1,0:T(8,128)}, u32[]{:S(2)}, u32[]{:S(2)}) collective-permute-start(f32[12,40,641]{2,1,0:T(8,128)S(1)} %broadcast_select_fusion.1.refs_10_), channel_id=1, source_target_pairs={{0,16},{8,24},{16,0},{24,8},{1,17},{9,25},{17,1},{25,9},{2,18},{10... | collective-permute-start | bytes 3692168 | tf_op jit(solution)/shard_map/ppermute | solution.py:453
  265.6 25.6 %collective-permute-start.42 = (bf16[6,160,128]{2,1,0:T(8,128)(2,1)}, bf16[6,160,128]{2,1,0:T(8,128)(2,1)S(1)}, u32[]{:S(2)}, u32[]{:S(2)}) collective-permute-start(bf16[6,160,128]{2,1,0:T(8,128)(2,1)} %get-tuple-element.157), channel_id=1, source_target_pairs={{0,2},{1,3},{2,0},{3,1},{4,6},{5,7},{6,4},{7,5},{8,10},{9,11},{10,... | collective-permute-start | bytes 737288 | tf_op jit(solution)/shard_map/ppermute | solution.py:551
  285.7 28.6 %collective-permute-start.44 = (bf16[6,160,128]{2,1,0:T(8,128)(2,1)}, bf16[6,160,128]{2,1,0:T(8,128)(2,1)}, u32[]{:S(2)}, u32[]{:S(2)}) collective-permute-start(bf16[6,160,128]{2,1,0:T(8,128)(2,1)} %get-tuple-element.159), channel_id=1, source_target_pairs={{0,4},{1,5},{2,6},{3,7},{4,0},{5,1},{6,2},{7,3},{8,12},{9,13},{10,... | collective-permute-start | bytes 737288 | tf_op jit(solution)/shard_map/ppermute | solution.py:551
  291.2 23.4 %collective-permute-start.45 = (bf16[6,160,128]{2,1,0:T(8,128)(2,1)}, bf16[6,160,128]{2,1,0:T(8,128)(2,1)}, u32[]{:S(2)}, u32[]{:S(2)}) collective-permute-start(bf16[6,160,128]{2,1,0:T(8,128)(2,1)} %get-tuple-element.160), channel_id=1, source_target_pairs={{0,5},{1,4},{2,7},{3,6},{4,1},{5,0},{6,3},{7,2},{8,13},{9,12},{10,... | collective-permute-start | bytes 737288 | tf_op jit(solution)/shard_map/ppermute | solution.py:551
  299.2 30.1 %collective-permute-start.46 = (bf16[6,160,128]{2,1,0:T(8,128)(2,1)}, bf16[6,160,128]{2,1,0:T(8,128)(2,1)}, u32[]{:S(2)}, u32[]{:S(2)}) collective-permute-start(bf16[6,160,128]{2,1,0:T(8,128)(2,1)} %get-tuple-element.161), channel_id=1, source_target_pairs={{0,6},{1,7},{2,4},{3,5},{4,2},{5,3},{6,0},{7,1},{8,14},{9,15},{10,... | collective-permute-start | bytes 737288 | tf_op jit(solution)/shard_map/ppermute | solution.py:551
  314.3 21.7 %collective-permute-start.47 = (bf16[6,160,128]{2,1,0:T(8,128)(2,1)}, bf16[6,160,128]{2,1,0:T(8,128)(2,1)S(1)}, u32[]{:S(2)}, u32[]{:S(2)}) collective-permute-start(bf16[6,160,128]{2,1,0:T(8,128)(2,1)} %get-tuple-element.162), channel_id=1, source_target_pairs={{0,7},{1,6},{2,5},{3,4},{4,3},{5,2},{6,1},{7,0},{8,15},{9,14},{10,... | collective-permute-start | bytes 737288 | tf_op jit(solution)/shard_map/ppermute | solution.py:551
  336.0 33.5 %collective-permute-start.29 = (bf16[6,160,128]{2,1,0:T(8,128)(2,1)}, bf16[6,160,128]{2,1,0:T(8,128)(2,1)}, u32[]{:S(2)}, u32[]{:S(2)}) collective-permute-start(bf16[6,160,128]{2,1,0:T(8,128)(2,1)} %get-tuple-element.141), channel_id=1, source_target_pairs={{0,3},{1,2},{2,1},{3,0},{4,7},{5,6},{6,5},{7,4},{8,11},{9,10},{10,... | collective-permute-start | bytes 737288 | tf_op jit(solution)/shard_map/ppermute | solution.py:551
  336.0 33.5 %collective-permute-start.30 = (bf16[6,160,128]{2,1,0:T(8,128)(2,1)}, bf16[6,160,128]{2,1,0:T(8,128)(2,1)}, u32[]{:S(2)}, u32[]{:S(2)}) collective-permute-start(bf16[6,160,128]{2,1,0:T(8,128)(2,1)} %get-tuple-element.142), channel_id=1, source_target_pairs={{0,4},{1,5},{2,6},{3,7},{4,0},{5,1},{6,2},{7,3},{8,12},{9,13},{10,... | collective-permute-start | bytes 737288 | tf_op jit(solution)/shard_map/ppermute | solution.py:551
  337.1 33.0 %collective-permute-start.31 = (bf16[6,160,128]{2,1,0:T(8,128)(2,1)}, bf16[6,160,128]{2,1,0:T(8,128)(2,1)}, u32[]{:S(2)}, u32[]{:S(2)}) collective-permute-start(bf16[6,160,128]{2,1,0:T(8,128)(2,1)} %get-tuple-element.143), channel_id=1, source_target_pairs={{0,5},{1,4},{2,7},{3,6},{4,1},{5,0},{6,3},{7,2},{8,13},{9,12},{10,... | collective-permute-start | bytes 737288 | tf_op jit(solution)/shard_map/ppermute | solution.py:551
  338.5 38.8 %collective-permute-start.32 = (bf16[6,160,128]{2,1,0:T(8,128)(2,1)}, bf16[6,160,128]{2,1,0:T(8,128)(2,1)S(1)}, u32[]{:S(2)}, u32[]{:S(2)}) collective-permute-start(bf16[6,160,128]{2,1,0:T(8,128)(2,1)} %get-tuple-element.144), channel_id=1, source_target_pairs={{0,6},{1,7},{2,4},{3,5},{4,2},{5,3},{6,0},{7,1},{8,14},{9,15},{10,... | collective-permute-start | bytes 737288 | tf_op jit(solution)/shard_map/ppermute | solution.py:551
  341.4 41.9 %collective-permute-start.33 = (bf16[6,160,128]{2,1,0:T(8,128)(2,1)}, bf16[6,160,128]{2,1,0:T(8,128)(2,1)S(1)}, u32[]{:S(2)}, u32[]{:S(2)}) collective-permute-start(bf16[6,160,128]{2,1,0:T(8,128)(2,1)} %get-tuple-element.145), channel_id=1, source_target_pairs={{0,7},{1,6},{2,5},{3,4},{4,3},{5,2},{6,1},{7,0},{8,15},{9,14},{10,... | collective-permute-start | bytes 737288 | tf_op jit(solution)/shard_map/ppermute | solution.py:551
  (60 other events, 901.6 us)

commit v3 on v2

--- a/solution.py
+++ b/solution.py
@@ -221,14 +221,18 @@
     chunks,
     last,
     stored,
-    slots,
+    made,
     count,
     patches,
     direct,
+    prior=False,
 ):
+    slots = len(made)
     w_refs, refs = refs[: chunks * slots], refs[chunks * slots :]
     leg_refs, refs = refs[:chunks], refs[chunks:]
     spec_ref, refs = refs[0], refs[1:]
+    if prior:
+        refs = refs[1:]
     mended = count if stored else 0
     fresh_refs, refs = refs[: 2 * patches], refs[2 * patches :]
     mend_refs, refs = refs[:mended], refs[mended:]
@@ -241,6 +245,7 @@
     rows = trajectories * comps
     tiles = ten.shape[0]
     padded = tiles * LANES
+    t0 = lax.div(lax.div(slot_place(made[0], direct), 2), trajectories) * trajectories
 
     @pl.when(step == 0)
     def _():
@@ -262,9 +267,10 @@
                         ]
 
         for k in range(chunks):
-            for n in range(slots):
-                place = slot_place(n, direct)
-                fill(k, lax.div(place, 2), lax.rem(place, 2), lambda f: w_refs[k * slots + n][f])
+            for n, slot in enumerate(made):
+                place = slot_place(slot, direct)
+                t = lax.div(place, 2) - t0
+                fill(k, t, lax.rem(place, 2), lambda f: w_refs[k * slots + n][f])
         for i in range(mended):
 
             @pl.when(slot_ref[i] >= 0)
@@ -600,6 +606,51 @@
             name="grid",
         )(order, (2.0 * mu)[None], weight[None], synthesis, analysis, *parts)
 
+    everything = tuple(range(slots))
+
+    def finish(parts, leg, start, made, group, prior):
+        span = trajectories // 2
+        some_spec = pl.BlockSpec((span, comps, SUB, row_length), lambda i, g: (g[0], 0, i, 0))
+        kernel = functools.partial(
+            inverse_kernel,
+            truncation=truncation,
+            pairs=padded_pairs,
+            chunks=1,
+            last=True,
+            stored=False,
+            made=made,
+            count=count,
+            patches=0,
+            real_pairs=pairs,
+            direct=direct,
+            prior=bool(prior),
+        )
+        return pl.pallas_call(
+            lambda group_ref, *refs: kernel(*refs),
+            out_shape=jax.ShapeDtypeStruct(state.shape, jnp.float32),
+            grid_spec=pltpu.PrefetchScalarGridSpec(
+                num_scalar_prefetch=1,
+                grid=(steps,),
+                in_specs=[smem] * 3
+                + [pl.BlockSpec(part_shape, lambda i, g: (0, 0, 0))] * len(made)
+                + [pl.BlockSpec((SUB, tiles * LANES, LANES), lambda i, g: (i, 0, 0)), some_spec]
+                + [pl.BlockSpec(memory_space=pl.ANY)] * len(prior),
+                out_specs=some_spec,
+                scratch_shapes=[
+                    pltpu.VMEM((1, 4 * span * comps * padded_pairs, LANES), jnp.float32),
+                    pltpu.VMEM((tiles, span * comps * SUB, LANES), jnp.float32),
+                ],
+            ),
+            input_output_aliases={6 + len(made): 0} if prior else {},
+            compiler_params=pltpu.CompilerParams(vmem_limit_bytes=60 * mib),
+            cost_estimate=pl.CostEstimate(
+                flops=8 * span * comps * padded_pairs * row_length * LANES,
+                bytes_accessed=16 * mib,
+                transcendentals=0,
+            ),
+            name="finish",
+        )(group, slot, gravity, stability, *[parts[n] for n in made], leg, start, *prior)
+
     def inverse(ws, legs, start, patches, mends, last):
         chunks = len(ws)
         stored = bool(mends)
@@ -612,7 +663,7 @@
                 chunks=chunks,
                 last=last,
                 stored=stored,
-                slots=slots,
+                made=everything,
                 count=count,
                 patches=len(patches) // 2,
                 real_pairs=pairs,
@@ -641,7 +692,6 @@
             name="inverse",
         )(slot, gravity, stability, *[x for w in ws for x in w], *legs, start, *patches, *mends)
 
-    everything = tuple(range(slots))
     halved = direct and trajectories % 2 == 0
     near, far = everything[: slots // 2], everything[slots // 2 :]
     if halved:
@@ -685,7 +735,12 @@
     for k in range(1, chunk_count - 1):
         start = inverse(back[k : k + 1], kept[k - 1 : k], start, fresh, [], False)
         fresh = []
-    out = inverse(back[-1:], kept[-1:], start, fresh, [], True)
+    if halved:
+        side = lax.div(position.astype(jnp.int32), space // 2).reshape(1)
+        out = finish(back[-1], kept[-1], start, far, 1 - side, [])
+        out = finish(back[-1], kept[-1], start, near, side, [out])
+    else:
+        out = inverse(back[-1:], kept[-1:], start, fresh, [], True)
     return out[:, :, :pairs] if extra else out
 
 

time: 397 us -> 424 us (1.068)
  the two profiles are of different devices: /device:TPU:10 before, /device:TPU:0 now
where the time goes in v3:
time: 424 us; the launch traced here: 422 us
  Pallas kernels  141 us (33%)
  waiting for transfers between devices  130 us (31%)
  starting transfers between devices  116 us (27%)
  local copies, waits for them, and re-layouts  14.5 us (3%)
  other arithmetic  14 us (3%)
  between operations  5.67 us (1%)
    ppermute x42, waiting for transfers between devices, swap(): got[n] = lax.ppermute(parts[n], 'space', [(d, d ^ n) for d in range(space)])  111 us
    ppermute x42, starting transfers between devices, swap(): got[n] = lax.ppermute(parts[n], 'space', [(d, d ^ n) for d in range(space)])  99.9 us
    pallas_call x4, Pallas kernels, forward(): pl.pallas_call(functools.partial(forward_kernel, truncation=truncation, p...  45.9 us
    pallas_call x3, Pallas kernels, grid(): pl.pallas_call(functools.partial(grid_kernel, scale=1.0 / truncation), ou...  43 us
    pallas_call x2, Pallas kernels, inverse(): pl.pallas_call(functools.partial(inverse_kernel, truncation=truncation, p...  27.7 us
    ppermute x4, waiting for transfers between devices, swap(): return lambda v: lax.ppermute(v, 'member', both)  19.3 us
    pallas_call x2, Pallas kernels, finish(): pl.pallas_call(lambda group_ref, *refs: kernel(*refs), out_shape=jax.Shap...  18.6 us
    ppermute x4, starting transfers between devices, share_row(): other = lax.ppermute(row, 'member', [(m, m ^ bit) for m in range(members)])  10.5 us
  transfers between devices with their start and end apart: 50, of which 15 were waited for; matrix products, arithmetic and copies ran while one was open for 6% of the time, Pallas kernels for 29%

profile of v3, /device:TPU:0, one launch (start us, length us, event | category | flops | bytes accessed | tf_op | source)
XLA Modules:
  0.0 422.0 jit_solution(585845858745347912)
XLA Ops:
  0.0 9.9 %forward.7 = (bf16[6,160,128]{2,1,0:T(8,128)(2,1)}, bf16[6,160,128]{2,1,0:T(8,128)(2,1)}, bf16[6,160,128]{2,1,0:T(8,128)(2,1)}, bf16[6,160,128]{2,1,0:T(8,128)(2,1)}) custom-call(f32[4,12,40,641]{3,2,1,0:T(8,128)} %refs_9_.1, bf16[641,40,384]{2,1,0:T(8,128)(2,1)} %bitcast.32), custom_call_target="tpu_custom_call" | custom-call | flops 630128640 | bytes 16777216 | tf_op jit(solution)/shard_map/forward/pallas_call | solution.py:512
  14.5 9.9 %forward.4 = (bf16[6,160,128]{2,1,0:T(8,128)(2,1)}, bf16[6,160,128]{2,1,0:T(8,128)(2,1)}, bf16[6,160,128]{2,1,0:T(8,128)(2,1)}, bf16[6,160,128]{2,1,0:T(8,128)(2,1)}) custom-call(f32[4,12,40,641]{3,2,1,0:T(8,128)} %refs_9_.1, bf16[641,40,384]{2,1,0:T(8,128)(2,1)} %bitcast.33), custom_call_target="tpu_custom_call" | custom-call | flops 630128640 | bytes 16777216 | tf_op jit(solution)/shard_map/forward/pallas_call | solution.py:512
  33.5 12.9 %conditional.4 = (bf16[12,40,641]{2,1,0:T(8,128)(2,1)S(1)}) conditional(s32[]{:T(128)} %bitcast.9, bf16[12,40,641]{2,1,0:T(8,128)(2,1)S(1)} %get-tuple-element.190, bf16[12,40,641]{2,1,0:T(8,128)(2,1)S(1)} %get-tuple-element.190, bf16[12,40,641]{2,1,0:T(8,128)(2,1)S(1)} %get-tuple-element.190, ...), branch_computations={%region_0.1_spmd, %region_1.2_spmd, %region_2.3_spmd, %region_3.4_... | conditional | bytes 3692208 | solution.py:451
  35.4 10.9 %collective-permute-done.2 = bf16[12,40,641]{2,1,0:T(8,128)(2,1)S(1)} collective-permute-done((bf16[12,40,641]{2,1,0:T(8,128)(2,1)S(1)}, bf16[12,40,641]{2,1,0:T(8,128)(2,1)S(1)}, u32[]{:S(2)}, u32[]{:S(2)}) %collective-permute-start.2) | collective-permute-done | bytes 615392 | tf_op jit(solution)/shard_map/cond/branch_3_fun/ppermute | solution.py:447
  49.0 6.8 %fusion.3 = bf16[2,321,640]{2,1,0:T(8,128)(2,1)S(1)} fusion(s32[2]{0:T(128)S(1)} %iota_multiply_fusion.1, s32[321,640]{1,0:T(8,128)S(1)} %iota_multiply_fusion), kind=kLoop, calls=%fused_computation.5 | loop fusion | flops 4108800 | bytes 1643528 | tf_op jit(solution)/shard_map/convert_element_type | solution.py:355
  55.8 13.1 %forward.5 = (bf16[6,160,128]{2,1,0:T(8,128)(2,1)}, bf16[6,160,128]{2,1,0:T(8,128)(2,1)}, bf16[6,160,128]{2,1,0:T(8,128)(2,1)}, bf16[6,160,128]{2,1,0:T(8,128)(2...) custom-call(s32[4]{0:T(128)} %get-tuple-element.127.refs_0_.slot_ref, ...), custom_call_target="tpu_custom_call" | custom-call | flops 1260257280 | bytes 16777216 | tf_op jit(solution)/shard_map/forward/pallas_call | solution.py:512
  68.9 13.0 %forward.6 = (bf16[6,160,128]{2,1,0:T(8,128)(2,1)}, bf16[6,160,128]{2,1,0:T(8,128)(2,1)}, bf16[6,160,128]{2,1,0:T(8,128)(2,1)}, bf16[6,160,128]{2,1,0:T(8,128)(2...) custom-call(s32[4]{0:T(128)} %get-tuple-element.127.refs_0_.slot_ref, ...), custom_call_target="tpu_custom_call" | custom-call | flops 1260257280 | bytes 16777216 | tf_op jit(solution)/shard_map/forward/pallas_call | solution.py:512
  97.5 10.4 %collective-permute-start.58 = (f32[12,40,641]{2,1,0:T(8,128)}, f32[12,40,641]{2,1,0:T(8,128)}, u32[]{:S(2)}, u32[]{:S(2)}) collective-permute-start(f32[12,40,641]{2,1,0:T(8,128)} %get-tuple-element.188), channel_id=1, source_target_pairs={{0,8},{8,0},{16,24},{24,16},{1,9},{9,1},{17,25},{25,17},{2,10},{10... | collective-permute-start | bytes 3692168 | tf_op jit(solution)/shard_map/ppermute | solution.py:459
  112.5 14.3 %grid.5 = (bf16[6,160,128]{2,1,0:T(8,128)(2,1)}, bf16[6,160,128]{2,1,0:T(8,128)(2,1)}, bf16[6,160,128]{2,1,0:T(8,128)(2,1)}, bf16[6,160,128]{2,1,0:T(8,128)(2,1)...) custom-call(s32[8]{0:T(128)} %iota_xor_fusion.order_ref, ...), custom_call_target="tpu_custom_call" | custom-call | flops 5033164800 | bytes 12582912 | tf_op jit(solution)/shard_map/grid/pallas_call | solution.py:591
  130.4 5.1 %collective-permute-done.51.refs_1_ = bf16[6,160,128]{2,1,0:T(8,128)(2,1)S(1)} collective-permute-done((bf16[6,160,128]{2,1,0:T(8,128)(2,1)}, bf16[6,160,128]{2,1,0:T(8,128)(2,1)S(1)}, u32[]{:S(2)}, u32[]{:S(2)}) %collective-permute-start.51) | collective-permute-done | bytes 245792 | tf_op jit(solution)/shard_map/ppermute | solution.py:557
  138.4 5.9 %collective-permute-done.53.refs_3_ = bf16[6,160,128]{2,1,0:T(8,128)(2,1)S(1)} collective-permute-done((bf16[6,160,128]{2,1,0:T(8,128)(2,1)}, bf16[6,160,128]{2,1,0:T(8,128)(2,1)S(1)}, u32[]{:S(2)}, u32[]{:S(2)}) %collective-permute-start.53) | collective-permute-done | bytes 245792 | tf_op jit(solution)/shard_map/ppermute | solution.py:557
  146.0 15.3 %collective-permute-done.54.refs_4_ = bf16[6,160,128]{2,1,0:T(8,128)(2,1)S(1)} collective-permute-done((bf16[6,160,128]{2,1,0:T(8,128)(2,1)}, bf16[6,160,128]{2,1,0:T(8,128)(2,1)S(1)}, u32[]{:S(2)}, u32[]{:S(2)}) %collective-permute-start.54) | collective-permute-done | bytes 245792 | tf_op jit(solution)/shard_map/ppermute | solution.py:557
  163.8 7.6 %collective-permute-done.55.refs_5_ = bf16[6,160,128]{2,1,0:T(8,128)(2,1)S(1)} collective-permute-done((bf16[6,160,128]{2,1,0:T(8,128)(2,1)}, bf16[6,160,128]{2,1,0:T(8,128)(2,1)S(1)}, u32[]{:S(2)}, u32[]{:S(2)}) %collective-permute-start.55) | collective-permute-done | bytes 245792 | tf_op jit(solution)/shard_map/ppermute | solution.py:557
  181.1 11.3 %conditional.6 = (bf16[2,6,160,128]{3,2,1,0:T(8,128)(2,1)}) conditional(s32[]{:T(128)} %bitcast.9, bf16[2,6,160,128]{3,2,1,0:T(8,128)(2,1)} %get-tuple-element.176, bf16[2,6,160,128]{3,2,1,0:T(8,128)(2,1)} %get-tuple-element.176, bf16[2,6,160,128]{3,2,1,0:T(8,128)(2,1)} %get-tuple-element.176, ...), branch_computations={%region_12.13_spmd, %region_13.14_spmd, %region_14.15_spmd, %regio... | conditional | bytes 2949168 | solution.py:451
  183.1 8.4 %collective-permute-done.12 = bf16[2,6,160,128]{3,2,1,0:T(8,128)(2,1)S(1)} collective-permute-done((bf16[2,6,160,128]{3,2,1,0:T(8,128)(2,1)}, bf16[2,6,160,128]{3,2,1,0:T(8,128)(2,1)S(1)}, u32[]{:S(2)}, u32[]{:S(2)}) %collective-permute-start.12) | collective-permute-done | bytes 491552 | tf_op jit(solution)/shard_map/cond/branch_3_fun/ppermute | solution.py:447
  193.3 5.5 %collective-permute-start.22 = (bf16[6,160,128]{2,1,0:T(8,128)(2,1)}, bf16[6,160,128]{2,1,0:T(8,128)(2,1)}, u32[]{:S(2)}, u32[]{:S(2)}) collective-permute-start(bf16[6,160,128]{2,1,0:T(8,128)(2,1)} %get-tuple-element.133), channel_id=1, source_target_pairs={{0,3},{1,2},{2,1},{3,0},{4,7},{5,6},{6,5},{7,4},{8,11},{9,10},{10,... | collective-permute-start | bytes 737288 | tf_op jit(solution)/shard_map/ppermute | solution.py:557
  223.5 5.1 %collective-permute-done.34.refs_5_ = bf16[6,160,128]{2,1,0:T(8,128)(2,1)S(1)} collective-permute-done((bf16[6,160,128]{2,1,0:T(8,128)(2,1)S(1)}, bf16[6,160,128]{2,1,0:T(8,128)(2,1)S(1)}, u32[]{:S(2)}, u32[]{:S(2)}) %collective-permute-start.34) | collective-permute-done | bytes 245792 | tf_op jit(solution)/shard_map/ppermute | solution.py:557
  232.2 6.2 %collective-permute-done.36.refs_7_ = bf16[6,160,128]{2,1,0:T(8,128)(2,1)S(1)} collective-permute-done((bf16[6,160,128]{2,1,0:T(8,128)(2,1)S(1)}, bf16[6,160,128]{2,1,0:T(8,128)(2,1)S(1)}, u32[]{:S(2)}, u32[]{:S(2)}) %collective-permute-start.36) | collective-permute-done | bytes 245792 | tf_op jit(solution)/shard_map/ppermute | solution.py:557
  239.1 14.4 %grid.4 = (bf16[6,160,128]{2,1,0:T(8,128)(2,1)}, bf16[6,160,128]{2,1,0:T(8,128)(2,1)}, bf16[6,160,128]{2,1,0:T(8,128)(2,1)}, bf16[6,160,128]{2,1,0:T(8,128)(2,1)...) custom-call(s32[8]{0:T(128)} %iota_xor_fusion.order_ref, ...), custom_call_target="tpu_custom_call" | custom-call | flops 5033164800 | bytes 12582912 | tf_op jit(solution)/shard_map/grid/pallas_call | solution.py:591
  253.5 22.2 %collective-permute-done.24.refs_5_ = bf16[6,160,128]{2,1,0:T(8,128)(2,1)} collective-permute-done((bf16[6,160,128]{2,1,0:T(8,128)(2,1)}, bf16[6,160,128]{2,1,0:T(8,128)(2,1)}, u32[]{:S(2)}, u32[]{:S(2)}) %collective-permute-start.24) | collective-permute-done | bytes 245792 | tf_op jit(solution)/shard_map/ppermute | solution.py:557
  277.5 7.7 %collective-permute-start.38 = (bf16[6,160,128]{2,1,0:T(8,128)(2,1)}, bf16[6,160,128]{2,1,0:T(8,128)(2,1)}, u32[]{:S(2)}, u32[]{:S(2)}) collective-permute-start(bf16[6,160,128]{2,1,0:T(8,128)(2,1)} %get-tuple-element.153), channel_id=1, source_target_pairs={{0,2},{1,3},{2,0},{3,1},{4,6},{5,7},{6,4},{7,5},{8,10},{9,11},{10,... | collective-permute-start | bytes 737288 | tf_op jit(solution)/shard_map/ppermute | solution.py:557
  288.0 9.4 %collective-permute-start.40 = (bf16[6,160,128]{2,1,0:T(8,128)(2,1)}, bf16[6,160,128]{2,1,0:T(8,128)(2,1)}, u32[]{:S(2)}, u32[]{:S(2)}) collective-permute-start(bf16[6,160,128]{2,1,0:T(8,128)(2,1)} %get-tuple-element.155), channel_id=1, source_target_pairs={{0,4},{1,5},{2,6},{3,7},{4,0},{5,1},{6,2},{7,3},{8,12},{9,13},{10,... | collective-permute-start | bytes 737288 | tf_op jit(solution)/shard_map/ppermute | solution.py:557
  298.8 14.3 %grid.3 = (bf16[6,160,128]{2,1,0:T(8,128)(2,1)}, bf16[6,160,128]{2,1,0:T(8,128)(2,1)}, bf16[6,160,128]{2,1,0:T(8,128)(2,1)}, bf16[6,160,128]{2,1,0:T(8,128)(2,1)...) custom-call(s32[8]{0:T(128)} %iota_xor_fusion.order_ref, ...), custom_call_target="tpu_custom_call" | custom-call | flops 5033164800 | bytes 12582912 | tf_op jit(solution)/shard_map/grid/pallas_call | solution.py:591
  313.1 8.7 %collective-permute-done.40.refs_4_ = bf16[6,160,128]{2,1,0:T(8,128)(2,1)} collective-permute-done((bf16[6,160,128]{2,1,0:T(8,128)(2,1)}, bf16[6,160,128]{2,1,0:T(8,128)(2,1)}, u32[]{:S(2)}, u32[]{:S(2)}) %collective-permute-start.40) | collective-permute-done | bytes 245792 | tf_op jit(solution)/shard_map/ppermute | solution.py:557
  322.9 6.2 %collective-permute-start.62 = (bf16[6,160,128]{2,1,0:T(8,128)(2,1)}, bf16[6,160,128]{2,1,0:T(8,128)(2,1)}, u32[]{:S(2)}, u32[]{:S(2)}) collective-permute-start(bf16[6,160,128]{2,1,0:T(8,128)(2,1)} %get-tuple-element.179), channel_id=1, source_target_pairs={{0,4},{1,5},{2,6},{3,7},{4,0},{5,1},{6,2},{7,3},{8,12},{9,13},{10,... | collective-permute-start | bytes 737288 | tf_op jit(solution)/shard_map/ppermute | solution.py:557
  329.1 7.1 %collective-permute-start.63 = (bf16[6,160,128]{2,1,0:T(8,128)(2,1)}, bf16[6,160,128]{2,1,0:T(8,128)(2,1)}, u32[]{:S(2)}, u32[]{:S(2)}) collective-permute-start(bf16[6,160,128]{2,1,0:T(8,128)(2,1)} %get-tuple-element.180), channel_id=1, source_target_pairs={{0,5},{1,4},{2,7},{3,6},{4,1},{5,0},{6,3},{7,2},{8,13},{9,12},{10,... | collective-permute-start | bytes 737288 | tf_op jit(solution)/shard_map/ppermute | solution.py:557
  336.2 25.1 %collective-permute-done.62.refs_3_ = bf16[6,160,128]{2,1,0:T(8,128)(2,1)} collective-permute-done((bf16[6,160,128]{2,1,0:T(8,128)(2,1)}, bf16[6,160,128]{2,1,0:T(8,128)(2,1)}, u32[]{:S(2)}, u32[]{:S(2)}) %collective-permute-start.62) | collective-permute-done | bytes 245792 | tf_op jit(solution)/shard_map/ppermute | solution.py:557
  365.0 8.3 %collective-permute-start.27 = (bf16[6,160,128]{2,1,0:T(8,128)(2,1)}, bf16[6,160,128]{2,1,0:T(8,128)(2,1)S(1)}, u32[]{:S(2)}, u32[]{:S(2)}) collective-permute-start(bf16[6,160,128]{2,1,0:T(8,128)(2,1)} %get-tuple-element.139), channel_id=1, source_target_pairs={{0,1},{1,0},{2,3},{3,2},{4,5},{5,4},{6,7},{7,6},{8,9},{9,8},{10,11... | collective-permute-start | bytes 737288 | tf_op jit(solution)/shard_map/ppermute | solution.py:557
  374.8 13.4 %inverse.2.refs_9_ = f32[4,12,40,641]{3,2,1,0:T(8,128)} custom-call(s32[4]{0:T(128)} %get-tuple-element.127.refs_0_.slot_ref, f32[2,2]{1,0:T(2,128)} %refs_1_.7, f32[2,2]{1,0:T(2,128)} %refs_2_.3, bf16[6,160,128]{2,1,0:T(8,128)(2,1)} %get-tuple-element.168.refs_0_, bf16[6,160,128]{2,1,0:T(8,128)(2,1)} %copy-done.6, bf16[6,160,128]{2,1,0:T(8,128)(2,1)} %copy-done.7, ...), custom_call_target="tpu_custom_call" | custom-call | flops 1260257280 | bytes 20971520 | tf_op jit(solution)/shard_map/inverse/pallas_call | solution.py:658
  388.2 14.3 %inverse.3.refs_8_ = f32[4,12,40,641]{3,2,1,0:T(8,128)} custom-call(s32[4]{0:T(128)} %get-tuple-element.127.refs_0_.slot_ref, f32[2,2]{1,0:T(2,128)} %refs_1_.7, f32[2,2]{1,0:T(2,128)} %refs_2_.3, bf16[6,160,128]{2,1,0:T(8,128)(2,1)} %get-tuple-element.151.refs_0_, bf16[6,160,128]{2,1,0:T(8,128)(2,1)} %collective-permute-done.37.refs_1_, ...), custom_call_target="tpu_custom_call" | custom-call | flops 1260257280 | bytes 20971520 | tf_op jit(solution)/shard_map/inverse/pallas_call | solution.py:658
  402.5 9.3 %finish.2.refs_9_ = f32[4,12,40,641]{3,2,1,0:T(8,128)} custom-call(s32[1]{0:T(128)S(6)} %sub.66.group_ref, s32[4]{0:T(128)} %get-tuple-element.127.refs_0_.slot_ref, f32[2,2]{1,0:T(2,128)} %refs_1_.7, f32[2,2]{1,0:T(2,128)} %refs_2_.3, bf16[6,160,128]{2,1,0:T(8,128)(2,1)} %collective-permute-done.62.refs_3_, ...), custom_call_target="tpu_custom_call" | custom-call | flops 630128640 | bytes 16777216 | tf_op jit(solution)/shard_map/finish/pallas_call | solution.py:628
  412.7 9.3 %finish.3 = f32[4,12,40,641]{3,2,1,0:T(8,128)} custom-call(s32[1]{0:T(128)} %bitcast.group_ref, s32[4]{0:T(128)} %get-tuple-element.127.refs_0_.slot_ref, f32[2,2]{1,0:T(2,128)} %refs_1_.7, f32[2,2]{1,0:T(2,128)} %refs_2_.3, bf16[6,160,128]{2,1,0:T(8,128)(2,1)} %get-tuple-element.138.refs_3_, ...), custom_call_target="tpu_custom_call", output_to_operand_aliasing={{}: (10, {})} | custom-call | flops 630128640 | bytes 16777216 | tf_op jit(solution)/shard_map/finish/pallas_call | solution.py:628
  (185 shorter events, 100.7 us)
Async XLA Ops:
  9.9 80.1 %collective-permute-start.44 = (bf16[6,160,128]{2,1,0:T(8,128)(2,1)}, bf16[6,160,128]{2,1,0:T(8,128)(2,1)S(1)}, u32[]{:S(2)}, u32[]{:S(2)}) collective-permute-start(bf16[6,160,128]{2,1,0:T(8,128)(2,1)} %get-tuple-element.161), channel_id=1, source_target_pairs={{0,1},{1,0},{2,3},{3,2},{4,5},{5,4},{6,7},{7,6},{8,9},{9,8},{10,11... | collective-permute-start | bytes 737288 | tf_op jit(solution)/shard_map/ppermute | solution.py:557
  12.9 80.8 %collective-permute-start.45 = (bf16[6,160,128]{2,1,0:T(8,128)(2,1)}, bf16[6,160,128]{2,1,0:T(8,128)(2,1)}, u32[]{:S(2)}, u32[]{:S(2)}) collective-permute-start(bf16[6,160,128]{2,1,0:T(8,128)(2,1)} %get-tuple-element.162), channel_id=1, source_target_pairs={{0,2},{1,3},{2,0},{3,1},{4,6},{5,7},{6,4},{7,5},{8,10},{9,11},{10,... | collective-permute-start | bytes 737288 | tf_op jit(solution)/shard_map/ppermute | solution.py:557
  14.5 83.0 %collective-permute-start.46 = (bf16[6,160,128]{2,1,0:T(8,128)(2,1)}, bf16[6,160,128]{2,1,0:T(8,128)(2,1)}, u32[]{:S(2)}, u32[]{:S(2)}) collective-permute-start(bf16[6,160,128]{2,1,0:T(8,128)(2,1)} %get-tuple-element.163), channel_id=1, source_target_pairs={{0,3},{1,2},{2,1},{3,0},{4,7},{5,6},{6,5},{7,4},{8,11},{9,10},{10,... | collective-permute-start | bytes 737288 | tf_op jit(solution)/shard_map/ppermute | solution.py:557
  24.4 88.1 %collective-permute-start.47 = (bf16[6,160,128]{2,1,0:T(8,128)(2,1)}, bf16[6,160,128]{2,1,0:T(8,128)(2,1)}, u32[]{:S(2)}, u32[]{:S(2)}) collective-permute-start(bf16[6,160,128]{2,1,0:T(8,128)(2,1)} %get-tuple-element.164), channel_id=1, source_target_pairs={{0,4},{1,5},{2,6},{3,7},{4,0},{5,1},{6,2},{7,3},{8,12},{9,13},{10,... | collective-permute-start | bytes 737288 | tf_op jit(solution)/shard_map/ppermute | solution.py:557
  47.4 65.2 %collective-permute-start.48 = (bf16[6,160,128]{2,1,0:T(8,128)(2,1)}, bf16[6,160,128]{2,1,0:T(8,128)(2,1)}, u32[]{:S(2)}, u32[]{:S(2)}) collective-permute-start(bf16[6,160,128]{2,1,0:T(8,128)(2,1)} %get-tuple-element.165), channel_id=1, source_target_pairs={{0,5},{1,4},{2,7},{3,6},{4,1},{5,0},{6,3},{7,2},{8,13},{9,12},{10,... | collective-permute-start | bytes 737288 | tf_op jit(solution)/shard_map/ppermute | solution.py:557
  90.0 22.5 %collective-permute-start.49 = (bf16[6,160,128]{2,1,0:T(8,128)(2,1)}, bf16[6,160,128]{2,1,0:T(8,128)(2,1)}, u32[]{:S(2)}, u32[]{:S(2)}) collective-permute-start(bf16[6,160,128]{2,1,0:T(8,128)(2,1)} %get-tuple-element.166), channel_id=1, source_target_pairs={{0,6},{1,7},{2,4},{3,5},{4,2},{5,3},{6,0},{7,1},{8,14},{9,15},{10,... | collective-permute-start | bytes 737288 | tf_op jit(solution)/shard_map/ppermute | solution.py:557
  97.5 102.4 %collective-permute-start.58 = (f32[12,40,641]{2,1,0:T(8,128)}, f32[12,40,641]{2,1,0:T(8,128)}, u32[]{:S(2)}, u32[]{:S(2)}) collective-permute-start(f32[12,40,641]{2,1,0:T(8,128)} %get-tuple-element.188), channel_id=1, source_target_pairs={{0,8},{8,0},{16,24},{24,16},{1,9},{9,1},{17,25},{25,17},{2,10},{10... | collective-permute-start | bytes 3692168 | tf_op jit(solution)/shard_map/ppermute | solution.py:459
  112.5 102.5 %collective-permute-start.60 = (f32[12,40,641]{2,1,0:T(8,128)}, f32[12,40,641]{2,1,0:T(8,128)S(1)}, u32[]{:S(2)}, u32[]{:S(2)}) collective-permute-start(f32[12,40,641]{2,1,0:T(8,128)} %get-tuple-element.187), channel_id=1, source_target_pairs={{0,8},{8,0},{16,24},{24,16},{1,9},{9,1},{17,25},{25,17},{2,10},{10... | collective-permute-start | bytes 3692168 | tf_op jit(solution)/shard_map/ppermute | solution.py:459
  135.5 25.8 %collective-permute-start.54 = (bf16[6,160,128]{2,1,0:T(8,128)(2,1)}, bf16[6,160,128]{2,1,0:T(8,128)(2,1)S(1)}, u32[]{:S(2)}, u32[]{:S(2)}) collective-permute-start(bf16[6,160,128]{2,1,0:T(8,128)(2,1)} %get-tuple-element.172), channel_id=1, source_target_pairs={{0,4},{1,5},{2,6},{3,7},{4,0},{5,1},{6,2},{7,3},{8,12},{9,13},{10,... | collective-permute-start | bytes 737288 | tf_op jit(solution)/shard_map/ppermute | solution.py:557
  135.5 35.9 %collective-permute-start.55 = (bf16[6,160,128]{2,1,0:T(8,128)(2,1)}, bf16[6,160,128]{2,1,0:T(8,128)(2,1)S(1)}, u32[]{:S(2)}, u32[]{:S(2)}) collective-permute-start(bf16[6,160,128]{2,1,0:T(8,128)(2,1)} %get-tuple-element.173), channel_id=1, source_target_pairs={{0,5},{1,4},{2,7},{3,6},{4,1},{5,0},{6,3},{7,2},{8,13},{9,12},{10,... | collective-permute-start | bytes 737288 | tf_op jit(solution)/shard_map/ppermute | solution.py:557
  144.3 28.9 %collective-permute-start.56 = (bf16[6,160,128]{2,1,0:T(8,128)(2,1)}, bf16[6,160,128]{2,1,0:T(8,128)(2,1)S(1)}, u32[]{:S(2)}, u32[]{:S(2)}) collective-permute-start(bf16[6,160,128]{2,1,0:T(8,128)(2,1)} %get-tuple-element.174), channel_id=1, source_target_pairs={{0,6},{1,7},{2,4},{3,5},{4,2},{5,3},{6,0},{7,1},{8,14},{9,15},{10,... | collective-permute-start | bytes 737288 | tf_op jit(solution)/shard_map/ppermute | solution.py:557
  171.4 27.4 %collective-permute-start.20 = (bf16[6,160,128]{2,1,0:T(8,128)(2,1)}, bf16[6,160,128]{2,1,0:T(8,128)(2,1)}, u32[]{:S(2)}, u32[]{:S(2)}) collective-permute-start(bf16[6,160,128]{2,1,0:T(8,128)(2,1)} %get-tuple-element.131), channel_id=1, source_target_pairs={{0,1},{1,0},{2,3},{3,2},{4,5},{5,4},{6,7},{7,6},{8,9},{9,8},{10,11... | collective-permute-start | bytes 737288 | tf_op jit(solution)/shard_map/ppermute | solution.py:557
  173.3 26.4 %collective-permute-start.21 = (bf16[6,160,128]{2,1,0:T(8,128)(2,1)S(1)}, bf16[6,160,128]{2,1,0:T(8,128)(2,1)}, u32[]{:S(2)}, u32[]{:S(2)}) collective-permute-start(bf16[6,160,128]{2,1,0:T(8,128)(2,1)S(1)} %copy-done.26), channel_id=1, source_target_pairs={{0,2},{1,3},{2,0},{3,1},{4,6},{5,7},{6,4},{7,5},{8,10},{9,11},{10,... | collective-permute-start | bytes 737288 | tf_op jit(solution)/shard_map/ppermute | solution.py:557
  208.9 19.7 %collective-permute-start.34 = (bf16[6,160,128]{2,1,0:T(8,128)(2,1)S(1)}, bf16[6,160,128]{2,1,0:T(8,128)(2,1)S(1)}, u32[]{:S(2)}, u32[]{:S(2)}) collective-permute-start(bf16[6,160,128]{2,1,0:T(8,128)(2,1)S(1)} %copy-done.23), channel_id=1, source_target_pairs={{0,5},{1,4},{2,7},{3,6},{4,1},{5,0},{6,3},{7,2},{8,13},{9,12},{10,... | collective-permute-start | bytes 737288 | tf_op jit(solution)/shard_map/ppermute | solution.py:557
  212.4 19.8 %collective-permute-start.35 = (bf16[6,160,128]{2,1,0:T(8,128)(2,1)S(1)}, bf16[6,160,128]{2,1,0:T(8,128)(2,1)S(1)}, u32[]{:S(2)}, u32[]{:S(2)}) collective-permute-start(bf16[6,160,128]{2,1,0:T(8,128)(2,1)S(1)} %copy-done.22), channel_id=1, source_target_pairs={{0,6},{1,7},{2,4},{3,5},{4,2},{5,3},{6,0},{7,1},{8,14},{9,15},{10,... | collective-permute-start | bytes 737288 | tf_op jit(solution)/shard_map/ppermute | solution.py:557
  216.2 22.2 %collective-permute-start.36 = (bf16[6,160,128]{2,1,0:T(8,128)(2,1)S(1)}, bf16[6,160,128]{2,1,0:T(8,128)(2,1)S(1)}, u32[]{:S(2)}, u32[]{:S(2)}) collective-permute-start(bf16[6,160,128]{2,1,0:T(8,128)(2,1)S(1)} %copy-done.21), channel_id=1, source_target_pairs={{0,7},{1,6},{2,5},{3,4},{4,3},{5,2},{6,1},{7,0},{8,15},{9,14},{10,... | collective-permute-start | bytes 737288 | tf_op jit(solution)/shard_map/ppermute | solution.py:557
  221.6 54.1 %collective-permute-start.24 = (bf16[6,160,128]{2,1,0:T(8,128)(2,1)}, bf16[6,160,128]{2,1,0:T(8,128)(2,1)}, u32[]{:S(2)}, u32[]{:S(2)}) collective-permute-start(bf16[6,160,128]{2,1,0:T(8,128)(2,1)} %get-tuple-element.135), channel_id=1, source_target_pairs={{0,5},{1,4},{2,7},{3,6},{4,1},{5,0},{6,3},{7,2},{8,13},{9,12},{10,... | collective-permute-start | bytes 737288 | tf_op jit(solution)/shard_map/ppermute | solution.py:557
  221.6 55.9 %collective-permute-start.25 = (bf16[6,160,128]{2,1,0:T(8,128)(2,1)S(1)}, bf16[6,160,128]{2,1,0:T(8,128)(2,1)}, u32[]{:S(2)}, u32[]{:S(2)}) collective-permute-start(bf16[6,160,128]{2,1,0:T(8,128)(2,1)S(1)} %copy-done.20), channel_id=1, source_target_pairs={{0,6},{1,7},{2,4},{3,5},{4,2},{5,3},{6,0},{7,1},{8,14},{9,15},{10,... | collective-permute-start | bytes 737288 | tf_op jit(solution)/shard_map/ppermute | solution.py:557
  228.7 56.5 %collective-permute-start.26 = (bf16[6,160,128]{2,1,0:T(8,128)(2,1)S(1)}, bf16[6,160,128]{2,1,0:T(8,128)(2,1)}, u32[]{:S(2)}, u32[]{:S(2)}) collective-permute-start(bf16[6,160,128]{2,1,0:T(8,128)(2,1)S(1)} %copy-done.19), channel_id=1, source_target_pairs={{0,7},{1,6},{2,5},{3,4},{4,3},{5,2},{6,1},{7,0},{8,15},{9,14},{10,... | collective-permute-start | bytes 737288 | tf_op jit(solution)/shard_map/ppermute | solution.py:557
  232.1 141.2 %collective-permute-start.59 = (f32[12,40,641]{2,1,0:T(8,128)S(1)}, f32[12,40,641]{2,1,0:T(8,128)}, u32[]{:S(2)}, u32[]{:S(2)}) collective-permute-start(f32[12,40,641]{2,1,0:T(8,128)S(1)} %broadcast_select_fusion.1.refs_10_), channel_id=1, source_target_pairs={{0,16},{8,24},{16,0},{24,8},{1,17},{9,25},{17,1},{25,9},{2,18},{10... | collective-permute-start | bytes 3692168 | tf_op jit(solution)/shard_map/ppermute | solution.py:459
  238.4 134.9 %collective-permute-start.61 = (f32[12,40,641]{2,1,0:T(8,128)S(1)}, f32[12,40,641]{2,1,0:T(8,128)}, u32[]{:S(2)}, u32[]{:S(2)}) collective-permute-start(f32[12,40,641]{2,1,0:T(8,128)S(1)} %broadcast_select_fusion.refs_12_), channel_id=1, source_target_pairs={{0,16},{8,24},{16,0},{24,8},{1,17},{9,25},{17,1},{25,9},{2,18},{10... | collective-permute-start | bytes 3692168 | tf_op jit(solution)/shard_map/ppermute | solution.py:459
  277.5 19.9 %collective-permute-start.38 = (bf16[6,160,128]{2,1,0:T(8,128)(2,1)}, bf16[6,160,128]{2,1,0:T(8,128)(2,1)}, u32[]{:S(2)}, u32[]{:S(2)}) collective-permute-start(bf16[6,160,128]{2,1,0:T(8,128)(2,1)} %get-tuple-element.153), channel_id=1, source_target_pairs={{0,2},{1,3},{2,0},{3,1},{4,6},{5,7},{6,4},{7,5},{8,10},{9,11},{10,... | collective-permute-start | bytes 737288 | tf_op jit(solution)/shard_map/ppermute | solution.py:557
  288.0 33.8 %collective-permute-start.40 = (bf16[6,160,128]{2,1,0:T(8,128)(2,1)}, bf16[6,160,128]{2,1,0:T(8,128)(2,1)}, u32[]{:S(2)}, u32[]{:S(2)}) collective-permute-start(bf16[6,160,128]{2,1,0:T(8,128)(2,1)} %get-tuple-element.155), channel_id=1, source_target_pairs={{0,4},{1,5},{2,6},{3,7},{4,0},{5,1},{6,2},{7,3},{8,12},{9,13},{10,... | collective-permute-start | bytes 737288 | tf_op jit(solution)/shard_map/ppermute | solution.py:557
  297.4 25.5 %collective-permute-start.41 = (bf16[6,160,128]{2,1,0:T(8,128)(2,1)}, bf16[6,160,128]{2,1,0:T(8,128)(2,1)}, u32[]{:S(2)}, u32[]{:S(2)}) collective-permute-start(bf16[6,160,128]{2,1,0:T(8,128)(2,1)} %get-tuple-element.156), channel_id=1, source_target_pairs={{0,5},{1,4},{2,7},{3,6},{4,1},{5,0},{6,3},{7,2},{8,13},{9,12},{10,... | collective-permute-start | bytes 737288 | tf_op jit(solution)/shard_map/ppermute | solution.py:557
  297.4 31.7 %collective-permute-start.42 = (bf16[6,160,128]{2,1,0:T(8,128)(2,1)}, bf16[6,160,128]{2,1,0:T(8,128)(2,1)}, u32[]{:S(2)}, u32[]{:S(2)}) collective-permute-start(bf16[6,160,128]{2,1,0:T(8,128)(2,1)} %get-tuple-element.157), channel_id=1, source_target_pairs={{0,6},{1,7},{2,4},{3,5},{4,2},{5,3},{6,0},{7,1},{8,14},{9,15},{10,... | collective-permute-start | bytes 737288 | tf_op jit(solution)/shard_map/ppermute | solution.py:557
  322.9 38.4 %collective-permute-start.62 = (bf16[6,160,128]{2,1,0:T(8,128)(2,1)}, bf16[6,160,128]{2,1,0:T(8,128)(2,1)}, u32[]{:S(2)}, u32[]{:S(2)}) collective-permute-start(bf16[6,160,128]{2,1,0:T(8,128)(2,1)} %get-tuple-element.179), channel_id=1, source_target_pairs={{0,4},{1,5},{2,6},{3,7},{4,0},{5,1},{6,2},{7,3},{8,12},{9,13},{10,... | collective-permute-start | bytes 737288 | tf_op jit(solution)/shard_map/ppermute | solution.py:557
  329.1 35.9 %collective-permute-start.63 = (bf16[6,160,128]{2,1,0:T(8,128)(2,1)}, bf16[6,160,128]{2,1,0:T(8,128)(2,1)}, u32[]{:S(2)}, u32[]{:S(2)}) collective-permute-start(bf16[6,160,128]{2,1,0:T(8,128)(2,1)} %get-tuple-element.180), channel_id=1, source_target_pairs={{0,5},{1,4},{2,7},{3,6},{4,1},{5,0},{6,3},{7,2},{8,13},{9,12},{10,... | collective-permute-start | bytes 737288 | tf_op jit(solution)/shard_map/ppermute | solution.py:557
  336.2 66.3 %collective-permute-start.64 = (bf16[6,160,128]{2,1,0:T(8,128)(2,1)}, bf16[6,160,128]{2,1,0:T(8,128)(2,1)}, u32[]{:S(2)}, u32[]{:S(2)}) collective-permute-start(bf16[6,160,128]{2,1,0:T(8,128)(2,1)} %get-tuple-element.181), channel_id=1, source_target_pairs={{0,6},{1,7},{2,4},{3,5},{4,2},{5,3},{6,0},{7,1},{8,14},{9,15},{10,... | collective-permute-start | bytes 737288 | tf_op jit(solution)/shard_map/ppermute | solution.py:557
  361.3 41.2 %collective-permute-start.65 = (bf16[6,160,128]{2,1,0:T(8,128)(2,1)}, bf16[6,160,128]{2,1,0:T(8,128)(2,1)}, u32[]{:S(2)}, u32[]{:S(2)}) collective-permute-start(bf16[6,160,128]{2,1,0:T(8,128)(2,1)} %get-tuple-element.182), channel_id=1, source_target_pairs={{0,7},{1,6},{2,5},{3,4},{4,3},{5,2},{6,1},{7,0},{8,15},{9,14},{10,... | collective-permute-start | bytes 737288 | tf_op jit(solution)/shard_map/ppermute | solution.py:557
  365.0 46.8 %collective-permute-start.27 = (bf16[6,160,128]{2,1,0:T(8,128)(2,1)}, bf16[6,160,128]{2,1,0:T(8,128)(2,1)S(1)}, u32[]{:S(2)}, u32[]{:S(2)}) collective-permute-start(bf16[6,160,128]{2,1,0:T(8,128)(2,1)} %get-tuple-element.139), channel_id=1, source_target_pairs={{0,1},{1,0},{2,3},{3,2},{4,5},{5,4},{6,7},{7,6},{8,9},{9,8},{10,11... | collective-permute-start | bytes 737288 | tf_op jit(solution)/shard_map/ppermute | solution.py:557
  373.3 38.6 %collective-permute-start.28 = (bf16[6,160,128]{2,1,0:T(8,128)(2,1)}, bf16[6,160,128]{2,1,0:T(8,128)(2,1)S(1)}, u32[]{:S(2)}, u32[]{:S(2)}) collective-permute-start(bf16[6,160,128]{2,1,0:T(8,128)(2,1)} %get-tuple-element.140), channel_id=1, source_target_pairs={{0,2},{1,3},{2,0},{3,1},{4,6},{5,7},{6,4},{7,5},{8,10},{9,11},{10,... | collective-permute-start | bytes 737288 | tf_op jit(solution)/shard_map/ppermute | solution.py:557
  373.3 38.6 %collective-permute-start.29 = (bf16[6,160,128]{2,1,0:T(8,128)(2,1)}, bf16[6,160,128]{2,1,0:T(8,128)(2,1)S(1)}, u32[]{:S(2)}, u32[]{:S(2)}) collective-permute-start(bf16[6,160,128]{2,1,0:T(8,128)(2,1)} %get-tuple-element.141), channel_id=1, source_target_pairs={{0,3},{1,2},{2,1},{3,0},{4,7},{5,6},{6,5},{7,4},{8,11},{9,10},{10,... | collective-permute-start | bytes 737288 | tf_op jit(solution)/shard_map/ppermute | solution.py:557
  (55 other events, 773.7 us)

commit v4 on v2

--- a/solution.py
+++ b/solution.py
@@ -322,12 +322,6 @@
             for i in range(mended):
                 mine = slot_ref[i] == t
                 old = [jnp.where(mine, 0.0, old[c]) for c in range(comps)]
-            for i in range(patches):
-                here = jnp.logical_and(slot_ref[i] == t, slot_ref[count + i] == 0)
-                there = jnp.logical_and(slot_ref[i] == t, slot_ref[count + i] != 0)
-                for c in range(comps):
-                    old[c] = old[c] + jnp.where(here, fresh_refs[2 * i][c, :, lanes], 0.0)
-                    old[c] = old[c] + jnp.where(there, fresh_refs[2 * i + 1][c, :, lanes], 0.0)
             if last:
                 tend = semi_implicit_slabs(old, tend, terms, hm)
             else:
@@ -336,7 +330,16 @@
                 out_ref[t, c, :, lanes] = tend[c]
             return carry
 
-        lax.fori_loop(0, trajectories, body, 0)
+        lax.fori_loop(0, trajectories, body, 0, unroll=True)
+
+    for i in range(patches):
+        for there in range(2):
+            mine = jnp.logical_and(slot_ref[i] >= 0, (slot_ref[count + i] != 0) == bool(there))
+
+            @pl.when(mine)
+            def _():
+                for c in range(comps):
+                    out_ref[slot_ref[i], c] += fresh_refs[2 * i + there][c]
 
 
 def fourier_tables(pair_count, groups, truncation, longitudes):
@@ -468,6 +471,7 @@
     split = space // (2 * trajectories)
     lane_count = LANES // split
     chunk_count = half_lat // LANES
+    assert chunk_count > 2
     padded_pairs = -(-pairs // SUB) * SUB
     steps = padded_pairs // SUB
     tiles = -(-row_length // LANES)

time: 397 us -> 397 us (level)
  no operation moved by 1% of the time
where the time goes in v4:
time: 397 us; the launch traced here: 396 us
  Pallas kernels  133 us (34%)
  starting transfers between devices  118 us (30%)
  waiting for transfers between devices  109 us (27%)
  local copies, waits for them, and re-layouts  16.5 us (4%)
  other arithmetic  14.1 us (4%)
  between operations  5.35 us (1%)
    ppermute x42, waiting for transfers between devices, swap(): got[n] = lax.ppermute(parts[n], 'space', [(d, d ^ n) for d in range(space)])  109 us
    ppermute x42, starting transfers between devices, swap(): got[n] = lax.ppermute(parts[n], 'space', [(d, d ^ n) for d in range(space)])  73.6 us
    pallas_call x4, Pallas kernels, forward(): pl.pallas_call(functools.partial(forward_kernel, truncation=truncation, p...  45.7 us
    pallas_call x3, Pallas kernels, grid(): pl.pallas_call(functools.partial(grid_kernel, scale=1.0 / truncation), ou...  43.1 us
    ppermute x4, starting transfers between devices, share_row(): other = lax.ppermute(row, 'member', [(m, m ^ bit) for m in range(members)])  41.1 us
    pallas_call x3, Pallas kernels, inverse(): pl.pallas_call(functools.partial(inverse_kernel, truncation=truncation, p...  37.8 us
  transfers between devices with their start and end apart: 50, of which 18 were waited for; matrix products, arithmetic and copies ran while one was open for 6% of the time, Pallas kernels for 28%

profile of v4, /device:TPU:10, one launch (start us, length us, event | category | flops | bytes accessed | tf_op | source)
XLA Modules:
  0.0 395.6 jit_solution(228181770624417770)
XLA Ops:
  0.0 9.9 %forward.7 = (bf16[6,160,128]{2,1,0:T(8,128)(2,1)}, bf16[6,160,128]{2,1,0:T(8,128)(2,1)}, bf16[6,160,128]{2,1,0:T(8,128)(2,1)}, bf16[6,160,128]{2,1,0:T(8,128)(2,1)}) custom-call(f32[4,12,40,641]{3,2,1,0:T(8,128)} %refs_9_.1, bf16[641,40,384]{2,1,0:T(8,128)(2,1)} %bitcast.31), custom_call_target="tpu_custom_call" | custom-call | flops 630128640 | bytes 16777216 | tf_op jit(solution)/shard_map/forward/pallas_call | solution.py:510
  13.4 9.9 %forward.4 = (bf16[6,160,128]{2,1,0:T(8,128)(2,1)}, bf16[6,160,128]{2,1,0:T(8,128)(2,1)}, bf16[6,160,128]{2,1,0:T(8,128)(2,1)}, bf16[6,160,128]{2,1,0:T(8,128)(2,1)}) custom-call(f32[4,12,40,641]{3,2,1,0:T(8,128)} %refs_9_.1, bf16[641,40,384]{2,1,0:T(8,128)(2,1)} %bitcast.32), custom_call_target="tpu_custom_call" | custom-call | flops 630128640 | bytes 16777216 | tf_op jit(solution)/shard_map/forward/pallas_call | solution.py:510
  35.6 6.8 %fusion.3 = bf16[2,321,640]{2,1,0:T(8,128)(2,1)S(1)} fusion(s32[2]{0:T(128)S(1)} %iota_multiply_fusion.1, s32[321,640]{1,0:T(8,128)S(1)} %iota_multiply_fusion), kind=kLoop, calls=%fused_computation.5 | loop fusion | flops 4108800 | bytes 1643528 | tf_op jit(solution)/shard_map/convert_element_type | solution.py:352
  42.4 13.0 %forward.5 = (bf16[6,160,128]{2,1,0:T(8,128)(2,1)}, bf16[6,160,128]{2,1,0:T(8,128)(2,1)}, bf16[6,160,128]{2,1,0:T(8,128)(2,1)}, bf16[6,160,128]{2,1,0:T(8,128)(2...) custom-call(s32[4]{0:T(128)} %get-tuple-element.127.refs_0_.slot_ref, ...), custom_call_target="tpu_custom_call" | custom-call | flops 1260257280 | bytes 16777216 | tf_op jit(solution)/shard_map/forward/pallas_call | solution.py:510
  55.3 13.0 %forward.6 = (bf16[6,160,128]{2,1,0:T(8,128)(2,1)}, bf16[6,160,128]{2,1,0:T(8,128)(2,1)}, bf16[6,160,128]{2,1,0:T(8,128)(2,1)}, bf16[6,160,128]{2,1,0:T(8,128)(2...) custom-call(s32[4]{0:T(128)} %get-tuple-element.127.refs_0_.slot_ref, ...), custom_call_target="tpu_custom_call" | custom-call | flops 1260257280 | bytes 16777216 | tf_op jit(solution)/shard_map/forward/pallas_call | solution.py:510
  78.0 3.8 dynamic-slice_bitcast_fusion
  81.8 21.8 %collective-permute-start.64 = (f32[12,40,641]{2,1,0:T(8,128)}, f32[12,40,641]{2,1,0:T(8,128)}, u32[]{:S(2)}, u32[]{:S(2)}) collective-permute-start(f32[12,40,641]{2,1,0:T(8,128)} %get-tuple-element.187), channel_id=1, source_target_pairs={{0,8},{8,0},{16,24},{24,16},{1,9},{9,1},{17,25},{25,17},{2,10},{10... | collective-permute-start | bytes 3692168 | tf_op jit(solution)/shard_map/ppermute | solution.py:456
  108.1 14.4 %grid.5 = (bf16[6,160,128]{2,1,0:T(8,128)(2,1)}, bf16[6,160,128]{2,1,0:T(8,128)(2,1)}, bf16[6,160,128]{2,1,0:T(8,128)(2,1)}, bf16[6,160,128]{2,1,0:T(8,128)(2,1)...) custom-call(s32[8]{0:T(128)} %iota_xor_fusion.order_ref, ...), custom_call_target="tpu_custom_call" | custom-call | flops 5033164800 | bytes 12582912 | tf_op jit(solution)/shard_map/grid/pallas_call | solution.py:589
  129.1 5.8 %collective-permute-start.58 = (bf16[6,160,128]{2,1,0:T(8,128)(2,1)}, bf16[6,160,128]{2,1,0:T(8,128)(2,1)S(1)}, u32[]{:S(2)}, u32[]{:S(2)}) collective-permute-start(bf16[6,160,128]{2,1,0:T(8,128)(2,1)} %get-tuple-element.176), channel_id=1, source_target_pairs={{0,4},{1,5},{2,6},{3,7},{4,0},{5,1},{6,2},{7,3},{8,12},{9,13},{10,... | collective-permute-start | bytes 737288 | tf_op jit(solution)/shard_map/ppermute | solution.py:555
  136.9 5.4 %collective-permute-done.57.refs_3_ = bf16[6,160,128]{2,1,0:T(8,128)(2,1)S(1)} collective-permute-done((bf16[6,160,128]{2,1,0:T(8,128)(2,1)}, bf16[6,160,128]{2,1,0:T(8,128)(2,1)S(1)}, u32[]{:S(2)}, u32[]{:S(2)}) %collective-permute-start.57) | collective-permute-done | bytes 245792 | tf_op jit(solution)/shard_map/ppermute | solution.py:555
  142.4 14.3 %collective-permute-done.58.refs_4_ = bf16[6,160,128]{2,1,0:T(8,128)(2,1)S(1)} collective-permute-done((bf16[6,160,128]{2,1,0:T(8,128)(2,1)}, bf16[6,160,128]{2,1,0:T(8,128)(2,1)S(1)}, u32[]{:S(2)}, u32[]{:S(2)}) %collective-permute-start.58) | collective-permute-done | bytes 245792 | tf_op jit(solution)/shard_map/ppermute | solution.py:555
  157.8 9.4 %collective-permute-done.59.refs_5_ = bf16[6,160,128]{2,1,0:T(8,128)(2,1)S(1)} collective-permute-done((bf16[6,160,128]{2,1,0:T(8,128)(2,1)}, bf16[6,160,128]{2,1,0:T(8,128)(2,1)S(1)}, u32[]{:S(2)}, u32[]{:S(2)}) %collective-permute-start.59) | collective-permute-done | bytes 245792 | tf_op jit(solution)/shard_map/ppermute | solution.py:555
  168.7 4.8 %collective-permute-done.60.refs_6_ = bf16[6,160,128]{2,1,0:T(8,128)(2,1)S(1)} collective-permute-done((bf16[6,160,128]{2,1,0:T(8,128)(2,1)}, bf16[6,160,128]{2,1,0:T(8,128)(2,1)S(1)}, u32[]{:S(2)}, u32[]{:S(2)}) %collective-permute-start.60) | collective-permute-done | bytes 245792 | tf_op jit(solution)/shard_map/ppermute | solution.py:555
  173.5 4.6 %collective-permute-done.61.refs_7_ = bf16[6,160,128]{2,1,0:T(8,128)(2,1)S(1)} collective-permute-done((bf16[6,160,128]{2,1,0:T(8,128)(2,1)}, bf16[6,160,128]{2,1,0:T(8,128)(2,1)S(1)}, u32[]{:S(2)}, u32[]{:S(2)}) %collective-permute-start.61) | collective-permute-done | bytes 245792 | tf_op jit(solution)/shard_map/ppermute | solution.py:555
  194.0 8.6 %collective-permute-done.37.refs_4_ = bf16[6,160,128]{2,1,0:T(8,128)(2,1)S(1)} collective-permute-done((bf16[6,160,128]{2,1,0:T(8,128)(2,1)}, bf16[6,160,128]{2,1,0:T(8,128)(2,1)S(1)}, u32[]{:S(2)}, u32[]{:S(2)}) %collective-permute-start.37) | collective-permute-done | bytes 245792 | tf_op jit(solution)/shard_map/ppermute | solution.py:555
  208.5 4.6 %collective-permute-done.39.refs_6_ = bf16[6,160,128]{2,1,0:T(8,128)(2,1)S(1)} collective-permute-done((bf16[6,160,128]{2,1,0:T(8,128)(2,1)}, bf16[6,160,128]{2,1,0:T(8,128)(2,1)S(1)}, u32[]{:S(2)}, u32[]{:S(2)}) %collective-permute-start.39) | collective-permute-done | bytes 245792 | tf_op jit(solution)/shard_map/ppermute | solution.py:555
  215.0 4.9 %collective-permute-start.23 = (bf16[6,160,128]{2,1,0:T(8,128)(2,1)S(1)}, bf16[6,160,128]{2,1,0:T(8,128)(2,1)S(1)}, u32[]{:S(2)}, u32[]{:S(2)}) collective-permute-start(bf16[6,160,128]{2,1,0:T(8,128)(2,1)S(1)} %copy-done.27), channel_id=1, source_target_pairs={{0,4},{1,5},{2,6},{3,7},{4,0},{5,1},{6,2},{7,3},{8,12},{9,13},{10,... | collective-permute-start | bytes 737288 | tf_op jit(solution)/shard_map/ppermute | solution.py:555
  221.5 6.1 %collective-permute-done.40.refs_7_ = bf16[6,160,128]{2,1,0:T(8,128)(2,1)S(1)} collective-permute-done((bf16[6,160,128]{2,1,0:T(8,128)(2,1)S(1)}, bf16[6,160,128]{2,1,0:T(8,128)(2,1)S(1)}, u32[]{:S(2)}, u32[]{:S(2)}) %collective-permute-start.40) | collective-permute-done | bytes 245792 | tf_op jit(solution)/shard_map/ppermute | solution.py:555
  231.7 14.7 %collective-permute-start.65 = (f32[12,40,641]{2,1,0:T(8,128)S(1)}, f32[12,40,641]{2,1,0:T(8,128)}, u32[]{:S(2)}, u32[]{:S(2)}) collective-permute-start(f32[12,40,641]{2,1,0:T(8,128)S(1)} %broadcast_select_fusion.refs_12_), channel_id=1, source_target_pairs={{0,16},{8,24},{16,0},{24,8},{1,17},{9,25},{17,1},{25,9},{2,18},{10... | collective-permute-start | bytes 3692168 | tf_op jit(solution)/shard_map/ppermute | solution.py:456
  246.5 4.6 %collective-permute-start.63 = (f32[12,40,641]{2,1,0:T(8,128)S(1)}, f32[12,40,641]{2,1,0:T(8,128)}, u32[]{:S(2)}, u32[]{:S(2)}) collective-permute-start(f32[12,40,641]{2,1,0:T(8,128)S(1)} %broadcast_select_fusion.1.refs_10_), channel_id=1, source_target_pairs={{0,16},{8,24},{16,0},{24,8},{1,17},{9,25},{17,1},{25,9},{2,18},{10... | collective-permute-start | bytes 3692168 | tf_op jit(solution)/shard_map/ppermute | solution.py:456
  251.1 14.4 %grid.4 = (bf16[6,160,128]{2,1,0:T(8,128)(2,1)}, bf16[6,160,128]{2,1,0:T(8,128)(2,1)}, bf16[6,160,128]{2,1,0:T(8,128)(2,1)}, bf16[6,160,128]{2,1,0:T(8,128)(2,1)...) custom-call(s32[8]{0:T(128)} %iota_xor_fusion.order_ref, ...), custom_call_target="tpu_custom_call" | custom-call | flops 5033164800 | bytes 12582912 | tf_op jit(solution)/shard_map/grid/pallas_call | solution.py:589
  265.6 20.1 %collective-permute-start.42 = (bf16[6,160,128]{2,1,0:T(8,128)(2,1)}, bf16[6,160,128]{2,1,0:T(8,128)(2,1)S(1)}, u32[]{:S(2)}, u32[]{:S(2)}) collective-permute-start(bf16[6,160,128]{2,1,0:T(8,128)(2,1)} %get-tuple-element.157), channel_id=1, source_target_pairs={{0,2},{1,3},{2,0},{3,1},{4,6},{5,7},{6,4},{7,5},{8,10},{9,11},{10,... | collective-permute-start | bytes 737288 | tf_op jit(solution)/shard_map/ppermute | solution.py:555
  285.8 5.4 %collective-permute-done.42.refs_2_ = bf16[6,160,128]{2,1,0:T(8,128)(2,1)S(1)} collective-permute-done((bf16[6,160,128]{2,1,0:T(8,128)(2,1)}, bf16[6,160,128]{2,1,0:T(8,128)(2,1)S(1)}, u32[]{:S(2)}, u32[]{:S(2)}) %collective-permute-start.42) | collective-permute-done | bytes 245792 | tf_op jit(solution)/shard_map/ppermute | solution.py:555
  291.2 8.0 %collective-permute-done.43.refs_3_ = bf16[6,160,128]{2,1,0:T(8,128)(2,1)S(1)} collective-permute-done((bf16[6,160,128]{2,1,0:T(8,128)(2,1)}, bf16[6,160,128]{2,1,0:T(8,128)(2,1)S(1)}, u32[]{:S(2)}, u32[]{:S(2)}) %collective-permute-start.43) | collective-permute-done | bytes 245792 | tf_op jit(solution)/shard_map/ppermute | solution.py:555
  300.0 14.3 %grid.3 = (bf16[6,160,128]{2,1,0:T(8,128)(2,1)}, bf16[6,160,128]{2,1,0:T(8,128)(2,1)}, bf16[6,160,128]{2,1,0:T(8,128)(2,1)}, bf16[6,160,128]{2,1,0:T(8,128)(2,1)...) custom-call(s32[8]{0:T(128)} %iota_xor_fusion.order_ref, ...), custom_call_target="tpu_custom_call" | custom-call | flops 5033164800 | bytes 12582912 | tf_op jit(solution)/shard_map/grid/pallas_call | solution.py:589
  317.2 12.1 %collective-permute-done.46.refs_6_ = bf16[6,160,128]{2,1,0:T(8,128)(2,1)} collective-permute-done((bf16[6,160,128]{2,1,0:T(8,128)(2,1)}, bf16[6,160,128]{2,1,0:T(8,128)(2,1)}, u32[]{:S(2)}, u32[]{:S(2)}) %collective-permute-start.46) | collective-permute-done | bytes 245792 | tf_op jit(solution)/shard_map/ppermute | solution.py:555
  329.3 6.7 %collective-permute-done.47.refs_7_ = bf16[6,160,128]{2,1,0:T(8,128)(2,1)S(1)} collective-permute-done((bf16[6,160,128]{2,1,0:T(8,128)(2,1)}, bf16[6,160,128]{2,1,0:T(8,128)(2,1)S(1)}, u32[]{:S(2)}, u32[]{:S(2)}) %collective-permute-start.47) | collective-permute-done | bytes 245792 | tf_op jit(solution)/shard_map/ppermute | solution.py:555
  342.0 12.7 %inverse.3.refs_9_ = f32[4,12,40,641]{3,2,1,0:T(8,128)} custom-call(s32[4]{0:T(128)} %get-tuple-element.127.refs_0_.slot_ref, f32[2,2]{1,0:T(2,128)} %gravity_ref.5, f32[2,2]{1,0:T(2,128)} %stability_ref.5, bf16[6,160,128]{2,1,0:T(8,128)(2,1)} %get-tuple-element.172.refs_0_, bf16[6,160,128]{2,1,0:T(8,128)(2,1)} %copy-done.6, bf16[6,160,128]{2,1,0:T(8,128)(2,1)} %copy-done.7, ...), custom_call_target="tpu_custom_call" | custom-call | flops 1260257280 | bytes 20971520 | tf_op jit(solution)/shard_map/inverse/pallas_call | solution.py:611
  354.7 13.5 %inverse.4.refs_9_ = f32[4,12,40,641]{3,2,1,0:T(8,128)} custom-call(s32[4]{0:T(128)} %get-tuple-element.127.refs_0_.slot_ref, f32[2,2]{1,0:T(2,128)} %gravity_ref.5, f32[2,2]{1,0:T(2,128)} %stability_ref.5, bf16[6,160,128]{2,1,0:T(8,128)(2,1)} %get-tuple-element.155.refs_0_, bf16[6,160,128]{2,1,0:T(8,128)(2,1)} %copy-done.15, ...), custom_call_target="tpu_custom_call" | custom-call | flops 1260257280 | bytes 20971520 | tf_op jit(solution)/shard_map/inverse/pallas_call | solution.py:611
  370.2 7.1 %collective-permute-done.32.refs_6_ = bf16[6,160,128]{2,1,0:T(8,128)(2,1)S(1)} collective-permute-done((bf16[6,160,128]{2,1,0:T(8,128)(2,1)}, bf16[6,160,128]{2,1,0:T(8,128)(2,1)S(1)}, u32[]{:S(2)}, u32[]{:S(2)}) %collective-permute-start.32) | collective-permute-done | bytes 245792 | tf_op jit(solution)/shard_map/ppermute | solution.py:555
  377.2 6.0 %collective-permute-done.33.refs_7_ = bf16[6,160,128]{2,1,0:T(8,128)(2,1)S(1)} collective-permute-done((bf16[6,160,128]{2,1,0:T(8,128)(2,1)}, bf16[6,160,128]{2,1,0:T(8,128)(2,1)S(1)}, u32[]{:S(2)}, u32[]{:S(2)}) %collective-permute-start.33) | collective-permute-done | bytes 245792 | tf_op jit(solution)/shard_map/ppermute | solution.py:555
  383.9 11.6 %inverse.5 = f32[4,12,40,641]{3,2,1,0:T(8,128)} custom-call(s32[4]{0:T(128)} %get-tuple-element.127.refs_0_.slot_ref, f32[2,2]{1,0:T(2,128)} %gravity_ref.5, f32[2,2]{1,0:T(2,128)} %stability_ref.5, bf16[6,160,128]{2,1,0:T(8,128)(2,1)} %get-tuple-element.138.refs_0_, bf16[6,160,128]{2,1,0:T(8,128)(2,1)} %copy-done.18, bf16[6,160,128]{2,1,0:T(8,128)(2,1)} %copy-done.19, ...), custom_call_target="tpu_custom_call" | custom-call | flops 1260257280 | bytes 20971520 | tf_op jit(solution)/shard_map/inverse/pallas_call | solution.py:611
  (194 shorter events, 81.9 us)
Async XLA Ops:
  9.9 66.0 %collective-permute-start.48 = (bf16[6,160,128]{2,1,0:T(8,128)(2,1)}, bf16[6,160,128]{2,1,0:T(8,128)(2,1)S(1)}, u32[]{:S(2)}, u32[]{:S(2)}) collective-permute-start(bf16[6,160,128]{2,1,0:T(8,128)(2,1)} %get-tuple-element.165), channel_id=1, source_target_pairs={{0,1},{1,0},{2,3},{3,2},{4,5},{5,4},{6,7},{7,6},{8,9},{9,8},{10,11... | collective-permute-start | bytes 737288 | tf_op jit(solution)/shard_map/ppermute | solution.py:555
  11.4 66.1 %collective-permute-start.49 = (bf16[6,160,128]{2,1,0:T(8,128)(2,1)}, bf16[6,160,128]{2,1,0:T(8,128)(2,1)}, u32[]{:S(2)}, u32[]{:S(2)}) collective-permute-start(bf16[6,160,128]{2,1,0:T(8,128)(2,1)} %get-tuple-element.166), channel_id=1, source_target_pairs={{0,2},{1,3},{2,0},{3,1},{4,6},{5,7},{6,4},{7,5},{8,10},{9,11},{10,... | collective-permute-start | bytes 737288 | tf_op jit(solution)/shard_map/ppermute | solution.py:555
  11.9 69.9 %collective-permute-start.50 = (bf16[6,160,128]{2,1,0:T(8,128)(2,1)}, bf16[6,160,128]{2,1,0:T(8,128)(2,1)}, u32[]{:S(2)}, u32[]{:S(2)}) collective-permute-start(bf16[6,160,128]{2,1,0:T(8,128)(2,1)} %get-tuple-element.167), channel_id=1, source_target_pairs={{0,3},{1,2},{2,1},{3,0},{4,7},{5,6},{6,5},{7,4},{8,11},{9,10},{10,... | collective-permute-start | bytes 737288 | tf_op jit(solution)/shard_map/ppermute | solution.py:555
  23.3 84.8 %collective-permute-start.51 = (bf16[6,160,128]{2,1,0:T(8,128)(2,1)}, bf16[6,160,128]{2,1,0:T(8,128)(2,1)}, u32[]{:S(2)}, u32[]{:S(2)}) collective-permute-start(bf16[6,160,128]{2,1,0:T(8,128)(2,1)} %get-tuple-element.168), channel_id=1, source_target_pairs={{0,4},{1,5},{2,6},{3,7},{4,0},{5,1},{6,2},{7,3},{8,12},{9,13},{10,... | collective-permute-start | bytes 737288 | tf_op jit(solution)/shard_map/ppermute | solution.py:555
  33.9 74.2 %collective-permute-start.52 = (bf16[6,160,128]{2,1,0:T(8,128)(2,1)}, bf16[6,160,128]{2,1,0:T(8,128)(2,1)}, u32[]{:S(2)}, u32[]{:S(2)}) collective-permute-start(bf16[6,160,128]{2,1,0:T(8,128)(2,1)} %get-tuple-element.169), channel_id=1, source_target_pairs={{0,5},{1,4},{2,7},{3,6},{4,1},{5,0},{6,3},{7,2},{8,13},{9,12},{10,... | collective-permute-start | bytes 737288 | tf_op jit(solution)/shard_map/ppermute | solution.py:555
  75.9 32.2 %collective-permute-start.53 = (bf16[6,160,128]{2,1,0:T(8,128)(2,1)}, bf16[6,160,128]{2,1,0:T(8,128)(2,1)}, u32[]{:S(2)}, u32[]{:S(2)}) collective-permute-start(bf16[6,160,128]{2,1,0:T(8,128)(2,1)} %get-tuple-element.170), channel_id=1, source_target_pairs={{0,6},{1,7},{2,4},{3,5},{4,2},{5,3},{6,0},{7,1},{8,14},{9,15},{10,... | collective-permute-start | bytes 737288 | tf_op jit(solution)/shard_map/ppermute | solution.py:555
  77.6 30.5 %collective-permute-start.54 = (bf16[6,160,128]{2,1,0:T(8,128)(2,1)}, bf16[6,160,128]{2,1,0:T(8,128)(2,1)}, u32[]{:S(2)}, u32[]{:S(2)}) collective-permute-start(bf16[6,160,128]{2,1,0:T(8,128)(2,1)} %get-tuple-element.171), channel_id=1, source_target_pairs={{0,7},{1,6},{2,5},{3,4},{4,3},{5,2},{6,1},{7,0},{8,15},{9,14},{10,... | collective-permute-start | bytes 737288 | tf_op jit(solution)/shard_map/ppermute | solution.py:555
  81.8 107.1 %collective-permute-start.64 = (f32[12,40,641]{2,1,0:T(8,128)}, f32[12,40,641]{2,1,0:T(8,128)}, u32[]{:S(2)}, u32[]{:S(2)}) collective-permute-start(f32[12,40,641]{2,1,0:T(8,128)} %get-tuple-element.187), channel_id=1, source_target_pairs={{0,8},{8,0},{16,24},{24,16},{1,9},{9,1},{17,25},{25,17},{2,10},{10... | collective-permute-start | bytes 3692168 | tf_op jit(solution)/shard_map/ppermute | solution.py:456
  108.1 105.7 %collective-permute-start.62 = (f32[12,40,641]{2,1,0:T(8,128)}, f32[12,40,641]{2,1,0:T(8,128)S(1)}, u32[]{:S(2)}, u32[]{:S(2)}) collective-permute-start(f32[12,40,641]{2,1,0:T(8,128)} %get-tuple-element.188), channel_id=1, source_target_pairs={{0,8},{8,0},{16,24},{24,16},{1,9},{9,1},{17,25},{25,17},{2,10},{10... | collective-permute-start | bytes 3692168 | tf_op jit(solution)/shard_map/ppermute | solution.py:456
  129.1 27.6 %collective-permute-start.58 = (bf16[6,160,128]{2,1,0:T(8,128)(2,1)}, bf16[6,160,128]{2,1,0:T(8,128)(2,1)S(1)}, u32[]{:S(2)}, u32[]{:S(2)}) collective-permute-start(bf16[6,160,128]{2,1,0:T(8,128)(2,1)} %get-tuple-element.176), channel_id=1, source_target_pairs={{0,4},{1,5},{2,6},{3,7},{4,0},{5,1},{6,2},{7,3},{8,12},{9,13},{10,... | collective-permute-start | bytes 737288 | tf_op jit(solution)/shard_map/ppermute | solution.py:555
  134.9 32.3 %collective-permute-start.59 = (bf16[6,160,128]{2,1,0:T(8,128)(2,1)}, bf16[6,160,128]{2,1,0:T(8,128)(2,1)S(1)}, u32[]{:S(2)}, u32[]{:S(2)}) collective-permute-start(bf16[6,160,128]{2,1,0:T(8,128)(2,1)} %get-tuple-element.177), channel_id=1, source_target_pairs={{0,5},{1,4},{2,7},{3,6},{4,1},{5,0},{6,3},{7,2},{8,13},{9,12},{10,... | collective-permute-start | bytes 737288 | tf_op jit(solution)/shard_map/ppermute | solution.py:555
  142.2 31.2 %collective-permute-start.60 = (bf16[6,160,128]{2,1,0:T(8,128)(2,1)}, bf16[6,160,128]{2,1,0:T(8,128)(2,1)S(1)}, u32[]{:S(2)}, u32[]{:S(2)}) collective-permute-start(bf16[6,160,128]{2,1,0:T(8,128)(2,1)} %get-tuple-element.178), channel_id=1, source_target_pairs={{0,6},{1,7},{2,4},{3,5},{4,2},{5,3},{6,0},{7,1},{8,14},{9,15},{10,... | collective-permute-start | bytes 737288 | tf_op jit(solution)/shard_map/ppermute | solution.py:555
  189.0 24.1 %collective-permute-start.39 = (bf16[6,160,128]{2,1,0:T(8,128)(2,1)}, bf16[6,160,128]{2,1,0:T(8,128)(2,1)S(1)}, u32[]{:S(2)}, u32[]{:S(2)}) collective-permute-start(bf16[6,160,128]{2,1,0:T(8,128)(2,1)} %get-tuple-element.153), channel_id=1, source_target_pairs={{0,6},{1,7},{2,4},{3,5},{4,2},{5,3},{6,0},{7,1},{8,14},{9,15},{10,... | collective-permute-start | bytes 737288 | tf_op jit(solution)/shard_map/ppermute | solution.py:555
  191.6 36.0 %collective-permute-start.40 = (bf16[6,160,128]{2,1,0:T(8,128)(2,1)S(1)}, bf16[6,160,128]{2,1,0:T(8,128)(2,1)S(1)}, u32[]{:S(2)}, u32[]{:S(2)}) collective-permute-start(bf16[6,160,128]{2,1,0:T(8,128)(2,1)S(1)} %copy-done.31), channel_id=1, source_target_pairs={{0,7},{1,6},{2,5},{3,4},{4,3},{5,2},{6,1},{7,0},{8,15},{9,14},{10,... | collective-permute-start | bytes 737288 | tf_op jit(solution)/shard_map/ppermute | solution.py:555
  203.3 24.4 %collective-permute-start.20 = (bf16[6,160,128]{2,1,0:T(8,128)(2,1)S(1)}, bf16[6,160,128]{2,1,0:T(8,128)(2,1)S(1)}, u32[]{:S(2)}, u32[]{:S(2)}) collective-permute-start(bf16[6,160,128]{2,1,0:T(8,128)(2,1)S(1)} %copy-done.30), channel_id=1, source_target_pairs={{0,1},{1,0},{2,3},{3,2},{4,5},{5,4},{6,7},{7,6},{8,9},{9,8},{10,11... | collective-permute-start | bytes 737288 | tf_op jit(solution)/shard_map/ppermute | solution.py:555
  205.9 25.2 %collective-permute-start.21 = (bf16[6,160,128]{2,1,0:T(8,128)(2,1)S(1)}, bf16[6,160,128]{2,1,0:T(8,128)(2,1)S(1)}, u32[]{:S(2)}, u32[]{:S(2)}) collective-permute-start(bf16[6,160,128]{2,1,0:T(8,128)(2,1)S(1)} %copy-done.29), channel_id=1, source_target_pairs={{0,2},{1,3},{2,0},{3,1},{4,6},{5,7},{6,4},{7,5},{8,10},{9,11},{10,... | collective-permute-start | bytes 737288 | tf_op jit(solution)/shard_map/ppermute | solution.py:555
  215.0 31.4 %collective-permute-start.23 = (bf16[6,160,128]{2,1,0:T(8,128)(2,1)S(1)}, bf16[6,160,128]{2,1,0:T(8,128)(2,1)S(1)}, u32[]{:S(2)}, u32[]{:S(2)}) collective-permute-start(bf16[6,160,128]{2,1,0:T(8,128)(2,1)S(1)} %copy-done.27), channel_id=1, source_target_pairs={{0,4},{1,5},{2,6},{3,7},{4,0},{5,1},{6,2},{7,3},{8,12},{9,13},{10,... | collective-permute-start | bytes 737288 | tf_op jit(solution)/shard_map/ppermute | solution.py:555
  227.6 37.9 %collective-permute-start.24 = (bf16[6,160,128]{2,1,0:T(8,128)(2,1)}, bf16[6,160,128]{2,1,0:T(8,128)(2,1)}, u32[]{:S(2)}, u32[]{:S(2)}) collective-permute-start(bf16[6,160,128]{2,1,0:T(8,128)(2,1)} %get-tuple-element.135), channel_id=1, source_target_pairs={{0,5},{1,4},{2,7},{3,6},{4,1},{5,0},{6,3},{7,2},{8,13},{9,12},{10,... | collective-permute-start | bytes 737288 | tf_op jit(solution)/shard_map/ppermute | solution.py:555
  227.6 37.9 %collective-permute-start.25 = (bf16[6,160,128]{2,1,0:T(8,128)(2,1)S(1)}, bf16[6,160,128]{2,1,0:T(8,128)(2,1)}, u32[]{:S(2)}, u32[]{:S(2)}) collective-permute-start(bf16[6,160,128]{2,1,0:T(8,128)(2,1)S(1)} %copy-done.26), channel_id=1, source_target_pairs={{0,6},{1,7},{2,4},{3,5},{4,2},{5,3},{6,0},{7,1},{8,14},{9,15},{10,... | collective-permute-start | bytes 737288 | tf_op jit(solution)/shard_map/ppermute | solution.py:555
  231.1 54.6 %collective-permute-start.26 = (bf16[6,160,128]{2,1,0:T(8,128)(2,1)S(1)}, bf16[6,160,128]{2,1,0:T(8,128)(2,1)}, u32[]{:S(2)}, u32[]{:S(2)}) collective-permute-start(bf16[6,160,128]{2,1,0:T(8,128)(2,1)S(1)} %copy-done.25), channel_id=1, source_target_pairs={{0,7},{1,6},{2,5},{3,4},{4,3},{5,2},{6,1},{7,0},{8,15},{9,14},{10,... | collective-permute-start | bytes 737288 | tf_op jit(solution)/shard_map/ppermute | solution.py:555
  231.7 106.7 %collective-permute-start.65 = (f32[12,40,641]{2,1,0:T(8,128)S(1)}, f32[12,40,641]{2,1,0:T(8,128)}, u32[]{:S(2)}, u32[]{:S(2)}) collective-permute-start(f32[12,40,641]{2,1,0:T(8,128)S(1)} %broadcast_select_fusion.refs_12_), channel_id=1, source_target_pairs={{0,16},{8,24},{16,0},{24,8},{1,17},{9,25},{17,1},{25,9},{2,18},{10... | collective-permute-start | bytes 3692168 | tf_op jit(solution)/shard_map/ppermute | solution.py:456
  246.5 94.9 %collective-permute-start.63 = (f32[12,40,641]{2,1,0:T(8,128)S(1)}, f32[12,40,641]{2,1,0:T(8,128)}, u32[]{:S(2)}, u32[]{:S(2)}) collective-permute-start(f32[12,40,641]{2,1,0:T(8,128)S(1)} %broadcast_select_fusion.1.refs_10_), channel_id=1, source_target_pairs={{0,16},{8,24},{16,0},{24,8},{1,17},{9,25},{17,1},{25,9},{2,18},{10... | collective-permute-start | bytes 3692168 | tf_op jit(solution)/shard_map/ppermute | solution.py:456
  265.6 25.6 %collective-permute-start.42 = (bf16[6,160,128]{2,1,0:T(8,128)(2,1)}, bf16[6,160,128]{2,1,0:T(8,128)(2,1)S(1)}, u32[]{:S(2)}, u32[]{:S(2)}) collective-permute-start(bf16[6,160,128]{2,1,0:T(8,128)(2,1)} %get-tuple-element.157), channel_id=1, source_target_pairs={{0,2},{1,3},{2,0},{3,1},{4,6},{5,7},{6,4},{7,5},{8,10},{9,11},{10,... | collective-permute-start | bytes 737288 | tf_op jit(solution)/shard_map/ppermute | solution.py:555
  285.7 28.6 %collective-permute-start.44 = (bf16[6,160,128]{2,1,0:T(8,128)(2,1)}, bf16[6,160,128]{2,1,0:T(8,128)(2,1)}, u32[]{:S(2)}, u32[]{:S(2)}) collective-permute-start(bf16[6,160,128]{2,1,0:T(8,128)(2,1)} %get-tuple-element.159), channel_id=1, source_target_pairs={{0,4},{1,5},{2,6},{3,7},{4,0},{5,1},{6,2},{7,3},{8,12},{9,13},{10,... | collective-permute-start | bytes 737288 | tf_op jit(solution)/shard_map/ppermute | solution.py:555
  291.2 23.4 %collective-permute-start.45 = (bf16[6,160,128]{2,1,0:T(8,128)(2,1)}, bf16[6,160,128]{2,1,0:T(8,128)(2,1)}, u32[]{:S(2)}, u32[]{:S(2)}) collective-permute-start(bf16[6,160,128]{2,1,0:T(8,128)(2,1)} %get-tuple-element.160), channel_id=1, source_target_pairs={{0,5},{1,4},{2,7},{3,6},{4,1},{5,0},{6,3},{7,2},{8,13},{9,12},{10,... | collective-permute-start | bytes 737288 | tf_op jit(solution)/shard_map/ppermute | solution.py:555
  299.2 30.1 %collective-permute-start.46 = (bf16[6,160,128]{2,1,0:T(8,128)(2,1)}, bf16[6,160,128]{2,1,0:T(8,128)(2,1)}, u32[]{:S(2)}, u32[]{:S(2)}) collective-permute-start(bf16[6,160,128]{2,1,0:T(8,128)(2,1)} %get-tuple-element.161), channel_id=1, source_target_pairs={{0,6},{1,7},{2,4},{3,5},{4,2},{5,3},{6,0},{7,1},{8,14},{9,15},{10,... | collective-permute-start | bytes 737288 | tf_op jit(solution)/shard_map/ppermute | solution.py:555
  314.3 21.7 %collective-permute-start.47 = (bf16[6,160,128]{2,1,0:T(8,128)(2,1)}, bf16[6,160,128]{2,1,0:T(8,128)(2,1)S(1)}, u32[]{:S(2)}, u32[]{:S(2)}) collective-permute-start(bf16[6,160,128]{2,1,0:T(8,128)(2,1)} %get-tuple-element.162), channel_id=1, source_target_pairs={{0,7},{1,6},{2,5},{3,4},{4,3},{5,2},{6,1},{7,0},{8,15},{9,14},{10,... | collective-permute-start | bytes 737288 | tf_op jit(solution)/shard_map/ppermute | solution.py:555
  336.0 32.2 %collective-permute-start.29 = (bf16[6,160,128]{2,1,0:T(8,128)(2,1)}, bf16[6,160,128]{2,1,0:T(8,128)(2,1)}, u32[]{:S(2)}, u32[]{:S(2)}) collective-permute-start(bf16[6,160,128]{2,1,0:T(8,128)(2,1)} %get-tuple-element.141), channel_id=1, source_target_pairs={{0,3},{1,2},{2,1},{3,0},{4,7},{5,6},{6,5},{7,4},{8,11},{9,10},{10,... | collective-permute-start | bytes 737288 | tf_op jit(solution)/shard_map/ppermute | solution.py:555
  336.0 32.2 %collective-permute-start.30 = (bf16[6,160,128]{2,1,0:T(8,128)(2,1)}, bf16[6,160,128]{2,1,0:T(8,128)(2,1)}, u32[]{:S(2)}, u32[]{:S(2)}) collective-permute-start(bf16[6,160,128]{2,1,0:T(8,128)(2,1)} %get-tuple-element.142), channel_id=1, source_target_pairs={{0,4},{1,5},{2,6},{3,7},{4,0},{5,1},{6,2},{7,3},{8,12},{9,13},{10,... | collective-permute-start | bytes 737288 | tf_op jit(solution)/shard_map/ppermute | solution.py:555
  337.1 33.0 %collective-permute-start.31 = (bf16[6,160,128]{2,1,0:T(8,128)(2,1)}, bf16[6,160,128]{2,1,0:T(8,128)(2,1)}, u32[]{:S(2)}, u32[]{:S(2)}) collective-permute-start(bf16[6,160,128]{2,1,0:T(8,128)(2,1)} %get-tuple-element.143), channel_id=1, source_target_pairs={{0,5},{1,4},{2,7},{3,6},{4,1},{5,0},{6,3},{7,2},{8,13},{9,12},{10,... | collective-permute-start | bytes 737288 | tf_op jit(solution)/shard_map/ppermute | solution.py:555
  338.5 38.8 %collective-permute-start.32 = (bf16[6,160,128]{2,1,0:T(8,128)(2,1)}, bf16[6,160,128]{2,1,0:T(8,128)(2,1)S(1)}, u32[]{:S(2)}, u32[]{:S(2)}) collective-permute-start(bf16[6,160,128]{2,1,0:T(8,128)(2,1)} %get-tuple-element.144), channel_id=1, source_target_pairs={{0,6},{1,7},{2,4},{3,5},{4,2},{5,3},{6,0},{7,1},{8,14},{9,15},{10,... | collective-permute-start | bytes 737288 | tf_op jit(solution)/shard_map/ppermute | solution.py:555
  341.4 41.9 %collective-permute-start.33 = (bf16[6,160,128]{2,1,0:T(8,128)(2,1)}, bf16[6,160,128]{2,1,0:T(8,128)(2,1)S(1)}, u32[]{:S(2)}, u32[]{:S(2)}) collective-permute-start(bf16[6,160,128]{2,1,0:T(8,128)(2,1)} %get-tuple-element.145), channel_id=1, source_target_pairs={{0,7},{1,6},{2,5},{3,4},{4,3},{5,2},{6,1},{7,0},{8,15},{9,14},{10,... | collective-permute-start | bytes 737288 | tf_op jit(solution)/shard_map/ppermute | solution.py:555
  (60 other events, 901.6 us)

commit v5 on v4

--- a/solution.py
+++ b/solution.py
@@ -12,6 +12,7 @@
 LANES = 128
 SUB = 8
 PACKED = 16
+DEEP = 256
 UNROLL_FORWARD = 8
 UNROLL_INVERSE = 8
 LONGITUDES_PER_WAVE = 2
@@ -279,23 +280,62 @@
             )
     first_pair = lax.axis_index("space") * real_pairs + step * block
 
+    def split_product(q):
+        edge = truncation - first_pair - q
+        late = edge > 2 * DEEP
+        border = jnp.where(late, 2, 1)
+
+        def half(h):
+            got = []
+            for s in range(2):
+                start = (2 * s + h) * (rows * pairs) + step * block + q
+                got.append(ws[0, pl.ds(start, rows, stride=pairs), :].astype(jnp.bfloat16))
+            return jnp.concatenate(got, axis=0)
+
+        def product(rows_of, first, width, shift):
+            got = lax.dot_general(
+                rows_of,
+                leg_refs[0][q, pl.ds(first, width), :],
+                (((1,), (1,)), ((), ())),
+                preferred_element_type=jnp.float32,
+            )
+            column = first + lax.broadcasted_iota(jnp.int32, (1, width), 1) - shift
+            south = got[rows:]
+            return got[:rows] + jnp.where((column & 1) == 1, -south, south)
+
+        lead = product(half(0), 0, 2 * DEEP, 0)
+        trail = product(half(1), 2 * DEEP, DEEP, edge)
+        other = product(
+            half(jnp.where(late, 0, 1)),
+            pl.multiple_of(border * DEEP, DEEP),
+            DEEP,
+            jnp.where(late, 0, edge),
+        )
+        column = lax.broadcasted_iota(jnp.int32, (1, DEEP), 1)
+        middle = jnp.where(column < edge - DEEP, lead[:, DEEP:], other)
+        tail = jnp.where(column < edge - 2 * DEEP, other, trail)
+        return jnp.concatenate([lead[:, :DEEP], middle, tail], axis=1)
+
     def one(q, carry):
-        at = pl.ds(step * block + q, 4 * rows, stride=pairs)
-        lhs = jnp.concatenate([ws[k, at, :].astype(jnp.bfloat16) for k in range(chunks)], axis=1)
-        if not stored:
-            rhs = jnp.concatenate([leg_refs[k][q] for k in range(chunks)], axis=1)
+        if last and tiles * LANES == 3 * DEEP:
+            total = split_product(q)
         else:
-            at = pl.ds(q, padded, stride=block)
-            rhs = jnp.concatenate(
-                [wide[k, at, :].astype(jnp.bfloat16) for k in range(chunks)], axis=1
+            at = pl.ds(step * block + q, 4 * rows, stride=pairs)
+            lhs = jnp.concatenate([ws[k, at, :].astype(jnp.bfloat16) for k in range(chunks)], axis=1)
+            if not stored:
+                rhs = jnp.concatenate([leg_refs[k][q] for k in range(chunks)], axis=1)
+            else:
+                at = pl.ds(q, padded, stride=block)
+                rhs = jnp.concatenate(
+                    [wide[k, at, :].astype(jnp.bfloat16) for k in range(chunks)], axis=1
+                )
+            got = lax.dot_general(
+                lhs, rhs, (((1,), (1,)), ((), ())), preferred_element_type=jnp.float32
             )
-        got = lax.dot_general(
-            lhs, rhs, (((1,), (1,)), ((), ())), preferred_element_type=jnp.float32
-        )
-        leading, odd, _ = layout_terms(first_pair + q, 1, 0, padded, truncation)
-        north = jnp.where(leading, got[:rows], got[rows : 2 * rows])
-        south = jnp.where(leading, got[2 * rows : 3 * rows], got[3 * rows :])
-        total = north + jnp.where(odd, -south, south)
+            leading, odd, _ = layout_terms(first_pair + q, 1, 0, padded, truncation)
+            north = jnp.where(leading, got[:rows], got[rows : 2 * rows])
+            south = jnp.where(leading, got[2 * rows : 3 * rows], got[3 * rows :])
+            total = north + jnp.where(odd, -south, south)
         for k in range(tiles):
             ten[k, pl.ds(q, rows, stride=block), :] = total[:, k * LANES : (k + 1) * LANES]
         return carry
@@ -319,9 +359,11 @@
                 value = ten[k, pl.ds(at, block), :][:, :width]
                 tend.append(value)
             old = [spec_ref[t, c, :, lanes] for c in range(comps)]
-            for i in range(mended):
-                mine = slot_ref[i] == t
-                old = [jnp.where(mine, 0.0, old[c]) for c in range(comps)]
+            if mended:
+                killed = slot_ref[0] == t
+                for i in range(1, mended):
+                    killed = jnp.logical_or(killed, slot_ref[i] == t)
+                old = [jnp.where(killed, 0.0, old[c]) for c in range(comps)]
             if last:
                 tend = semi_implicit_slabs(old, tend, terms, hm)
             else:

time: 397 us -> 397 us (level)
  no operation moved by 1% of the time
where the time goes in v5:
time: 397 us; the launch traced here: 396 us
  Pallas kernels  133 us (34%)
  starting transfers between devices  118 us (30%)
  waiting for transfers between devices  109 us (27%)
  local copies, waits for them, and re-layouts  16.5 us (4%)
  other arithmetic  14.1 us (4%)
  between operations  5.35 us (1%)
    ppermute x42, waiting for transfers between devices, swap(): got[n] = lax.ppermute(parts[n], 'space', [(d, d ^ n) for d in range(space)])  109 us
    ppermute x42, starting transfers between devices, swap(): got[n] = lax.ppermute(parts[n], 'space', [(d, d ^ n) for d in range(space)])  73.6 us
    pallas_call x4, Pallas kernels, forward(): pl.pallas_call(functools.partial(forward_kernel, truncation=truncation, p...  45.7 us
    pallas_call x3, Pallas kernels, grid(): pl.pallas_call(functools.partial(grid_kernel, scale=1.0 / truncation), ou...  43.1 us
    ppermute x4, starting transfers between devices, share_row(): other = lax.ppermute(row, 'member', [(m, m ^ bit) for m in range(members)])  41.1 us
    pallas_call x3, Pallas kernels, inverse(): pl.pallas_call(functools.partial(inverse_kernel, truncation=truncation, p...  37.8 us
  transfers between devices with their start and end apart: 50, of which 18 were waited for; matrix products, arithmetic and copies ran while one was open for 6% of the time, Pallas kernels for 28%

profile of v5, /device:TPU:10, one launch (start us, length us, event | category | flops | bytes accessed | tf_op | source)
XLA Modules:
  0.0 395.6 jit_solution(5199219996781584470)
XLA Ops:
  0.0 9.9 %forward.7 = (bf16[6,160,128]{2,1,0:T(8,128)(2,1)}, bf16[6,160,128]{2,1,0:T(8,128)(2,1)}, bf16[6,160,128]{2,1,0:T(8,128)(2,1)}, bf16[6,160,128]{2,1,0:T(8,128)(2,1)}) custom-call(f32[4,12,40,641]{3,2,1,0:T(8,128)} %refs_9_.1, bf16[641,40,384]{2,1,0:T(8,128)(2,1)} %bitcast.31), custom_call_target="tpu_custom_call" | custom-call | flops 630128640 | bytes 16777216 | tf_op jit(solution)/shard_map/forward/pallas_call | solution.py:552
  13.4 9.9 %forward.4 = (bf16[6,160,128]{2,1,0:T(8,128)(2,1)}, bf16[6,160,128]{2,1,0:T(8,128)(2,1)}, bf16[6,160,128]{2,1,0:T(8,128)(2,1)}, bf16[6,160,128]{2,1,0:T(8,128)(2,1)}) custom-call(f32[4,12,40,641]{3,2,1,0:T(8,128)} %refs_9_.1, bf16[641,40,384]{2,1,0:T(8,128)(2,1)} %bitcast.32), custom_call_target="tpu_custom_call" | custom-call | flops 630128640 | bytes 16777216 | tf_op jit(solution)/shard_map/forward/pallas_call | solution.py:552
  35.6 6.8 %fusion.3 = bf16[2,321,640]{2,1,0:T(8,128)(2,1)S(1)} fusion(s32[2]{0:T(128)S(1)} %iota_multiply_fusion.1, s32[321,640]{1,0:T(8,128)S(1)} %iota_multiply_fusion), kind=kLoop, calls=%fused_computation.5 | loop fusion | flops 4108800 | bytes 1643528 | tf_op jit(solution)/shard_map/convert_element_type | solution.py:394
  42.4 13.0 %forward.5 = (bf16[6,160,128]{2,1,0:T(8,128)(2,1)}, bf16[6,160,128]{2,1,0:T(8,128)(2,1)}, bf16[6,160,128]{2,1,0:T(8,128)(2,1)}, bf16[6,160,128]{2,1,0:T(8,128)(2...) custom-call(s32[4]{0:T(128)} %get-tuple-element.127.refs_0_.slot_ref, ...), custom_call_target="tpu_custom_call" | custom-call | flops 1260257280 | bytes 16777216 | tf_op jit(solution)/shard_map/forward/pallas_call | solution.py:552
  55.3 13.0 %forward.6 = (bf16[6,160,128]{2,1,0:T(8,128)(2,1)}, bf16[6,160,128]{2,1,0:T(8,128)(2,1)}, bf16[6,160,128]{2,1,0:T(8,128)(2,1)}, bf16[6,160,128]{2,1,0:T(8,128)(2...) custom-call(s32[4]{0:T(128)} %get-tuple-element.127.refs_0_.slot_ref, ...), custom_call_target="tpu_custom_call" | custom-call | flops 1260257280 | bytes 16777216 | tf_op jit(solution)/shard_map/forward/pallas_call | solution.py:552
  78.0 3.8 dynamic-slice_bitcast_fusion
  81.8 21.8 %collective-permute-start.64 = (f32[12,40,641]{2,1,0:T(8,128)}, f32[12,40,641]{2,1,0:T(8,128)}, u32[]{:S(2)}, u32[]{:S(2)}) collective-permute-start(f32[12,40,641]{2,1,0:T(8,128)} %get-tuple-element.187), channel_id=1, source_target_pairs={{0,8},{8,0},{16,24},{24,16},{1,9},{9,1},{17,25},{25,17},{2,10},{10... | collective-permute-start | bytes 3692168 | tf_op jit(solution)/shard_map/ppermute | solution.py:498
  108.1 14.4 %grid.5 = (bf16[6,160,128]{2,1,0:T(8,128)(2,1)}, bf16[6,160,128]{2,1,0:T(8,128)(2,1)}, bf16[6,160,128]{2,1,0:T(8,128)(2,1)}, bf16[6,160,128]{2,1,0:T(8,128)(2,1)...) custom-call(s32[8]{0:T(128)} %iota_xor_fusion.order_ref, ...), custom_call_target="tpu_custom_call" | custom-call | flops 5033164800 | bytes 12582912 | tf_op jit(solution)/shard_map/grid/pallas_call | solution.py:631
  129.1 5.8 %collective-permute-start.58 = (bf16[6,160,128]{2,1,0:T(8,128)(2,1)}, bf16[6,160,128]{2,1,0:T(8,128)(2,1)S(1)}, u32[]{:S(2)}, u32[]{:S(2)}) collective-permute-start(bf16[6,160,128]{2,1,0:T(8,128)(2,1)} %get-tuple-element.176), channel_id=1, source_target_pairs={{0,4},{1,5},{2,6},{3,7},{4,0},{5,1},{6,2},{7,3},{8,12},{9,13},{10,... | collective-permute-start | bytes 737288 | tf_op jit(solution)/shard_map/ppermute | solution.py:597
  136.9 5.4 %collective-permute-done.57.refs_3_ = bf16[6,160,128]{2,1,0:T(8,128)(2,1)S(1)} collective-permute-done((bf16[6,160,128]{2,1,0:T(8,128)(2,1)}, bf16[6,160,128]{2,1,0:T(8,128)(2,1)S(1)}, u32[]{:S(2)}, u32[]{:S(2)}) %collective-permute-start.57) | collective-permute-done | bytes 245792 | tf_op jit(solution)/shard_map/ppermute | solution.py:597
  142.4 14.3 %collective-permute-done.58.refs_4_ = bf16[6,160,128]{2,1,0:T(8,128)(2,1)S(1)} collective-permute-done((bf16[6,160,128]{2,1,0:T(8,128)(2,1)}, bf16[6,160,128]{2,1,0:T(8,128)(2,1)S(1)}, u32[]{:S(2)}, u32[]{:S(2)}) %collective-permute-start.58) | collective-permute-done | bytes 245792 | tf_op jit(solution)/shard_map/ppermute | solution.py:597
  157.8 9.4 %collective-permute-done.59.refs_5_ = bf16[6,160,128]{2,1,0:T(8,128)(2,1)S(1)} collective-permute-done((bf16[6,160,128]{2,1,0:T(8,128)(2,1)}, bf16[6,160,128]{2,1,0:T(8,128)(2,1)S(1)}, u32[]{:S(2)}, u32[]{:S(2)}) %collective-permute-start.59) | collective-permute-done | bytes 245792 | tf_op jit(solution)/shard_map/ppermute | solution.py:597
  168.7 4.8 %collective-permute-done.60.refs_6_ = bf16[6,160,128]{2,1,0:T(8,128)(2,1)S(1)} collective-permute-done((bf16[6,160,128]{2,1,0:T(8,128)(2,1)}, bf16[6,160,128]{2,1,0:T(8,128)(2,1)S(1)}, u32[]{:S(2)}, u32[]{:S(2)}) %collective-permute-start.60) | collective-permute-done | bytes 245792 | tf_op jit(solution)/shard_map/ppermute | solution.py:597
  173.5 4.6 %collective-permute-done.61.refs_7_ = bf16[6,160,128]{2,1,0:T(8,128)(2,1)S(1)} collective-permute-done((bf16[6,160,128]{2,1,0:T(8,128)(2,1)}, bf16[6,160,128]{2,1,0:T(8,128)(2,1)S(1)}, u32[]{:S(2)}, u32[]{:S(2)}) %collective-permute-start.61) | collective-permute-done | bytes 245792 | tf_op jit(solution)/shard_map/ppermute | solution.py:597
  194.0 8.6 %collective-permute-done.37.refs_4_ = bf16[6,160,128]{2,1,0:T(8,128)(2,1)S(1)} collective-permute-done((bf16[6,160,128]{2,1,0:T(8,128)(2,1)}, bf16[6,160,128]{2,1,0:T(8,128)(2,1)S(1)}, u32[]{:S(2)}, u32[]{:S(2)}) %collective-permute-start.37) | collective-permute-done | bytes 245792 | tf_op jit(solution)/shard_map/ppermute | solution.py:597
  208.5 4.6 %collective-permute-done.39.refs_6_ = bf16[6,160,128]{2,1,0:T(8,128)(2,1)S(1)} collective-permute-done((bf16[6,160,128]{2,1,0:T(8,128)(2,1)}, bf16[6,160,128]{2,1,0:T(8,128)(2,1)S(1)}, u32[]{:S(2)}, u32[]{:S(2)}) %collective-permute-start.39) | collective-permute-done | bytes 245792 | tf_op jit(solution)/shard_map/ppermute | solution.py:597
  215.0 4.9 %collective-permute-start.23 = (bf16[6,160,128]{2,1,0:T(8,128)(2,1)S(1)}, bf16[6,160,128]{2,1,0:T(8,128)(2,1)S(1)}, u32[]{:S(2)}, u32[]{:S(2)}) collective-permute-start(bf16[6,160,128]{2,1,0:T(8,128)(2,1)S(1)} %copy-done.27), channel_id=1, source_target_pairs={{0,4},{1,5},{2,6},{3,7},{4,0},{5,1},{6,2},{7,3},{8,12},{9,13},{10,... | collective-permute-start | bytes 737288 | tf_op jit(solution)/shard_map/ppermute | solution.py:597
  221.5 6.1 %collective-permute-done.40.refs_7_ = bf16[6,160,128]{2,1,0:T(8,128)(2,1)S(1)} collective-permute-done((bf16[6,160,128]{2,1,0:T(8,128)(2,1)S(1)}, bf16[6,160,128]{2,1,0:T(8,128)(2,1)S(1)}, u32[]{:S(2)}, u32[]{:S(2)}) %collective-permute-start.40) | collective-permute-done | bytes 245792 | tf_op jit(solution)/shard_map/ppermute | solution.py:597
  231.7 14.7 %collective-permute-start.65 = (f32[12,40,641]{2,1,0:T(8,128)S(1)}, f32[12,40,641]{2,1,0:T(8,128)}, u32[]{:S(2)}, u32[]{:S(2)}) collective-permute-start(f32[12,40,641]{2,1,0:T(8,128)S(1)} %broadcast_select_fusion.refs_12_), channel_id=1, source_target_pairs={{0,16},{8,24},{16,0},{24,8},{1,17},{9,25},{17,1},{25,9},{2,18},{10... | collective-permute-start | bytes 3692168 | tf_op jit(solution)/shard_map/ppermute | solution.py:498
  246.5 4.6 %collective-permute-start.63 = (f32[12,40,641]{2,1,0:T(8,128)S(1)}, f32[12,40,641]{2,1,0:T(8,128)}, u32[]{:S(2)}, u32[]{:S(2)}) collective-permute-start(f32[12,40,641]{2,1,0:T(8,128)S(1)} %broadcast_select_fusion.1.refs_10_), channel_id=1, source_target_pairs={{0,16},{8,24},{16,0},{24,8},{1,17},{9,25},{17,1},{25,9},{2,18},{10... | collective-permute-start | bytes 3692168 | tf_op jit(solution)/shard_map/ppermute | solution.py:498
  251.1 14.4 %grid.4 = (bf16[6,160,128]{2,1,0:T(8,128)(2,1)}, bf16[6,160,128]{2,1,0:T(8,128)(2,1)}, bf16[6,160,128]{2,1,0:T(8,128)(2,1)}, bf16[6,160,128]{2,1,0:T(8,128)(2,1)...) custom-call(s32[8]{0:T(128)} %iota_xor_fusion.order_ref, ...), custom_call_target="tpu_custom_call" | custom-call | flops 5033164800 | bytes 12582912 | tf_op jit(solution)/shard_map/grid/pallas_call | solution.py:631
  265.6 20.1 %collective-permute-start.42 = (bf16[6,160,128]{2,1,0:T(8,128)(2,1)}, bf16[6,160,128]{2,1,0:T(8,128)(2,1)S(1)}, u32[]{:S(2)}, u32[]{:S(2)}) collective-permute-start(bf16[6,160,128]{2,1,0:T(8,128)(2,1)} %get-tuple-element.157), channel_id=1, source_target_pairs={{0,2},{1,3},{2,0},{3,1},{4,6},{5,7},{6,4},{7,5},{8,10},{9,11},{10,... | collective-permute-start | bytes 737288 | tf_op jit(solution)/shard_map/ppermute | solution.py:597
  285.8 5.4 %collective-permute-done.42.refs_2_ = bf16[6,160,128]{2,1,0:T(8,128)(2,1)S(1)} collective-permute-done((bf16[6,160,128]{2,1,0:T(8,128)(2,1)}, bf16[6,160,128]{2,1,0:T(8,128)(2,1)S(1)}, u32[]{:S(2)}, u32[]{:S(2)}) %collective-permute-start.42) | collective-permute-done | bytes 245792 | tf_op jit(solution)/shard_map/ppermute | solution.py:597
  291.2 8.0 %collective-permute-done.43.refs_3_ = bf16[6,160,128]{2,1,0:T(8,128)(2,1)S(1)} collective-permute-done((bf16[6,160,128]{2,1,0:T(8,128)(2,1)}, bf16[6,160,128]{2,1,0:T(8,128)(2,1)S(1)}, u32[]{:S(2)}, u32[]{:S(2)}) %collective-permute-start.43) | collective-permute-done | bytes 245792 | tf_op jit(solution)/shard_map/ppermute | solution.py:597
  300.0 14.3 %grid.3 = (bf16[6,160,128]{2,1,0:T(8,128)(2,1)}, bf16[6,160,128]{2,1,0:T(8,128)(2,1)}, bf16[6,160,128]{2,1,0:T(8,128)(2,1)}, bf16[6,160,128]{2,1,0:T(8,128)(2,1)...) custom-call(s32[8]{0:T(128)} %iota_xor_fusion.order_ref, ...), custom_call_target="tpu_custom_call" | custom-call | flops 5033164800 | bytes 12582912 | tf_op jit(solution)/shard_map/grid/pallas_call | solution.py:631
  317.2 12.1 %collective-permute-done.46.refs_6_ = bf16[6,160,128]{2,1,0:T(8,128)(2,1)} collective-permute-done((bf16[6,160,128]{2,1,0:T(8,128)(2,1)}, bf16[6,160,128]{2,1,0:T(8,128)(2,1)}, u32[]{:S(2)}, u32[]{:S(2)}) %collective-permute-start.46) | collective-permute-done | bytes 245792 | tf_op jit(solution)/shard_map/ppermute | solution.py:597
  329.3 6.7 %collective-permute-done.47.refs_7_ = bf16[6,160,128]{2,1,0:T(8,128)(2,1)S(1)} collective-permute-done((bf16[6,160,128]{2,1,0:T(8,128)(2,1)}, bf16[6,160,128]{2,1,0:T(8,128)(2,1)S(1)}, u32[]{:S(2)}, u32[]{:S(2)}) %collective-permute-start.47) | collective-permute-done | bytes 245792 | tf_op jit(solution)/shard_map/ppermute | solution.py:597
  342.0 12.6 %inverse.3.refs_9_ = f32[4,12,40,641]{3,2,1,0:T(8,128)} custom-call(s32[4]{0:T(128)} %get-tuple-element.127.refs_0_.slot_ref, f32[2,2]{1,0:T(2,128)} %gravity_ref.5, f32[2,2]{1,0:T(2,128)} %stability_ref.5, bf16[6,160,128]{2,1,0:T(8,128)(2,1)} %get-tuple-element.172.refs_0_, bf16[6,160,128]{2,1,0:T(8,128)(2,1)} %copy-done.6, bf16[6,160,128]{2,1,0:T(8,128)(2,1)} %copy-done.7, ...), custom_call_target="tpu_custom_call" | custom-call | flops 1260257280 | bytes 20971520 | tf_op jit(solution)/shard_map/inverse/pallas_call | solution.py:653
  354.7 13.5 %inverse.4.refs_9_ = f32[4,12,40,641]{3,2,1,0:T(8,128)} custom-call(s32[4]{0:T(128)} %get-tuple-element.127.refs_0_.slot_ref, f32[2,2]{1,0:T(2,128)} %gravity_ref.5, f32[2,2]{1,0:T(2,128)} %stability_ref.5, bf16[6,160,128]{2,1,0:T(8,128)(2,1)} %get-tuple-element.155.refs_0_, bf16[6,160,128]{2,1,0:T(8,128)(2,1)} %copy-done.15, ...), custom_call_target="tpu_custom_call" | custom-call | flops 1260257280 | bytes 20971520 | tf_op jit(solution)/shard_map/inverse/pallas_call | solution.py:653
  370.2 7.1 %collective-permute-done.32.refs_6_ = bf16[6,160,128]{2,1,0:T(8,128)(2,1)S(1)} collective-permute-done((bf16[6,160,128]{2,1,0:T(8,128)(2,1)}, bf16[6,160,128]{2,1,0:T(8,128)(2,1)S(1)}, u32[]{:S(2)}, u32[]{:S(2)}) %collective-permute-start.32) | collective-permute-done | bytes 245792 | tf_op jit(solution)/shard_map/ppermute | solution.py:597
  377.2 6.0 %collective-permute-done.33.refs_7_ = bf16[6,160,128]{2,1,0:T(8,128)(2,1)S(1)} collective-permute-done((bf16[6,160,128]{2,1,0:T(8,128)(2,1)}, bf16[6,160,128]{2,1,0:T(8,128)(2,1)S(1)}, u32[]{:S(2)}, u32[]{:S(2)}) %collective-permute-start.33) | collective-permute-done | bytes 245792 | tf_op jit(solution)/shard_map/ppermute | solution.py:597
  383.9 11.6 %inverse.5 = f32[4,12,40,641]{3,2,1,0:T(8,128)} custom-call(s32[4]{0:T(128)} %get-tuple-element.127.refs_0_.slot_ref, f32[2,2]{1,0:T(2,128)} %gravity_ref.5, f32[2,2]{1,0:T(2,128)} %stability_ref.5, bf16[6,160,128]{2,1,0:T(8,128)(2,1)} %get-tuple-element.138.refs_0_, bf16[6,160,128]{2,1,0:T(8,128)(2,1)} %copy-done.18, bf16[6,160,128]{2,1,0:T(8,128)(2,1)} %copy-done.19, ...), custom_call_target="tpu_custom_call" | custom-call | flops 1260257280 | bytes 20971520 | tf_op jit(solution)/shard_map/inverse/pallas_call | solution.py:653
  (194 shorter events, 81.9 us)
Async XLA Ops:
  9.9 66.0 %collective-permute-start.48 = (bf16[6,160,128]{2,1,0:T(8,128)(2,1)}, bf16[6,160,128]{2,1,0:T(8,128)(2,1)S(1)}, u32[]{:S(2)}, u32[]{:S(2)}) collective-permute-start(bf16[6,160,128]{2,1,0:T(8,128)(2,1)} %get-tuple-element.165), channel_id=1, source_target_pairs={{0,1},{1,0},{2,3},{3,2},{4,5},{5,4},{6,7},{7,6},{8,9},{9,8},{10,11... | collective-permute-start | bytes 737288 | tf_op jit(solution)/shard_map/ppermute | solution.py:597
  11.4 66.1 %collective-permute-start.49 = (bf16[6,160,128]{2,1,0:T(8,128)(2,1)}, bf16[6,160,128]{2,1,0:T(8,128)(2,1)}, u32[]{:S(2)}, u32[]{:S(2)}) collective-permute-start(bf16[6,160,128]{2,1,0:T(8,128)(2,1)} %get-tuple-element.166), channel_id=1, source_target_pairs={{0,2},{1,3},{2,0},{3,1},{4,6},{5,7},{6,4},{7,5},{8,10},{9,11},{10,... | collective-permute-start | bytes 737288 | tf_op jit(solution)/shard_map/ppermute | solution.py:597
  11.9 69.9 %collective-permute-start.50 = (bf16[6,160,128]{2,1,0:T(8,128)(2,1)}, bf16[6,160,128]{2,1,0:T(8,128)(2,1)}, u32[]{:S(2)}, u32[]{:S(2)}) collective-permute-start(bf16[6,160,128]{2,1,0:T(8,128)(2,1)} %get-tuple-element.167), channel_id=1, source_target_pairs={{0,3},{1,2},{2,1},{3,0},{4,7},{5,6},{6,5},{7,4},{8,11},{9,10},{10,... | collective-permute-start | bytes 737288 | tf_op jit(solution)/shard_map/ppermute | solution.py:597
  23.3 84.8 %collective-permute-start.51 = (bf16[6,160,128]{2,1,0:T(8,128)(2,1)}, bf16[6,160,128]{2,1,0:T(8,128)(2,1)}, u32[]{:S(2)}, u32[]{:S(2)}) collective-permute-start(bf16[6,160,128]{2,1,0:T(8,128)(2,1)} %get-tuple-element.168), channel_id=1, source_target_pairs={{0,4},{1,5},{2,6},{3,7},{4,0},{5,1},{6,2},{7,3},{8,12},{9,13},{10,... | collective-permute-start | bytes 737288 | tf_op jit(solution)/shard_map/ppermute | solution.py:597
  33.9 74.2 %collective-permute-start.52 = (bf16[6,160,128]{2,1,0:T(8,128)(2,1)}, bf16[6,160,128]{2,1,0:T(8,128)(2,1)}, u32[]{:S(2)}, u32[]{:S(2)}) collective-permute-start(bf16[6,160,128]{2,1,0:T(8,128)(2,1)} %get-tuple-element.169), channel_id=1, source_target_pairs={{0,5},{1,4},{2,7},{3,6},{4,1},{5,0},{6,3},{7,2},{8,13},{9,12},{10,... | collective-permute-start | bytes 737288 | tf_op jit(solution)/shard_map/ppermute | solution.py:597
  75.9 32.2 %collective-permute-start.53 = (bf16[6,160,128]{2,1,0:T(8,128)(2,1)}, bf16[6,160,128]{2,1,0:T(8,128)(2,1)}, u32[]{:S(2)}, u32[]{:S(2)}) collective-permute-start(bf16[6,160,128]{2,1,0:T(8,128)(2,1)} %get-tuple-element.170), channel_id=1, source_target_pairs={{0,6},{1,7},{2,4},{3,5},{4,2},{5,3},{6,0},{7,1},{8,14},{9,15},{10,... | collective-permute-start | bytes 737288 | tf_op jit(solution)/shard_map/ppermute | solution.py:597
  77.6 30.5 %collective-permute-start.54 = (bf16[6,160,128]{2,1,0:T(8,128)(2,1)}, bf16[6,160,128]{2,1,0:T(8,128)(2,1)}, u32[]{:S(2)}, u32[]{:S(2)}) collective-permute-start(bf16[6,160,128]{2,1,0:T(8,128)(2,1)} %get-tuple-element.171), channel_id=1, source_target_pairs={{0,7},{1,6},{2,5},{3,4},{4,3},{5,2},{6,1},{7,0},{8,15},{9,14},{10,... | collective-permute-start | bytes 737288 | tf_op jit(solution)/shard_map/ppermute | solution.py:597
  81.8 107.1 %collective-permute-start.64 = (f32[12,40,641]{2,1,0:T(8,128)}, f32[12,40,641]{2,1,0:T(8,128)}, u32[]{:S(2)}, u32[]{:S(2)}) collective-permute-start(f32[12,40,641]{2,1,0:T(8,128)} %get-tuple-element.187), channel_id=1, source_target_pairs={{0,8},{8,0},{16,24},{24,16},{1,9},{9,1},{17,25},{25,17},{2,10},{10... | collective-permute-start | bytes 3692168 | tf_op jit(solution)/shard_map/ppermute | solution.py:498
  108.1 105.7 %collective-permute-start.62 = (f32[12,40,641]{2,1,0:T(8,128)}, f32[12,40,641]{2,1,0:T(8,128)S(1)}, u32[]{:S(2)}, u32[]{:S(2)}) collective-permute-start(f32[12,40,641]{2,1,0:T(8,128)} %get-tuple-element.188), channel_id=1, source_target_pairs={{0,8},{8,0},{16,24},{24,16},{1,9},{9,1},{17,25},{25,17},{2,10},{10... | collective-permute-start | bytes 3692168 | tf_op jit(solution)/shard_map/ppermute | solution.py:498
  129.1 27.6 %collective-permute-start.58 = (bf16[6,160,128]{2,1,0:T(8,128)(2,1)}, bf16[6,160,128]{2,1,0:T(8,128)(2,1)S(1)}, u32[]{:S(2)}, u32[]{:S(2)}) collective-permute-start(bf16[6,160,128]{2,1,0:T(8,128)(2,1)} %get-tuple-element.176), channel_id=1, source_target_pairs={{0,4},{1,5},{2,6},{3,7},{4,0},{5,1},{6,2},{7,3},{8,12},{9,13},{10,... | collective-permute-start | bytes 737288 | tf_op jit(solution)/shard_map/ppermute | solution.py:597
  134.9 32.3 %collective-permute-start.59 = (bf16[6,160,128]{2,1,0:T(8,128)(2,1)}, bf16[6,160,128]{2,1,0:T(8,128)(2,1)S(1)}, u32[]{:S(2)}, u32[]{:S(2)}) collective-permute-start(bf16[6,160,128]{2,1,0:T(8,128)(2,1)} %get-tuple-element.177), channel_id=1, source_target_pairs={{0,5},{1,4},{2,7},{3,6},{4,1},{5,0},{6,3},{7,2},{8,13},{9,12},{10,... | collective-permute-start | bytes 737288 | tf_op jit(solution)/shard_map/ppermute | solution.py:597
  142.2 31.2 %collective-permute-start.60 = (bf16[6,160,128]{2,1,0:T(8,128)(2,1)}, bf16[6,160,128]{2,1,0:T(8,128)(2,1)S(1)}, u32[]{:S(2)}, u32[]{:S(2)}) collective-permute-start(bf16[6,160,128]{2,1,0:T(8,128)(2,1)} %get-tuple-element.178), channel_id=1, source_target_pairs={{0,6},{1,7},{2,4},{3,5},{4,2},{5,3},{6,0},{7,1},{8,14},{9,15},{10,... | collective-permute-start | bytes 737288 | tf_op jit(solution)/shard_map/ppermute | solution.py:597
  189.0 24.1 %collective-permute-start.39 = (bf16[6,160,128]{2,1,0:T(8,128)(2,1)}, bf16[6,160,128]{2,1,0:T(8,128)(2,1)S(1)}, u32[]{:S(2)}, u32[]{:S(2)}) collective-permute-start(bf16[6,160,128]{2,1,0:T(8,128)(2,1)} %get-tuple-element.153), channel_id=1, source_target_pairs={{0,6},{1,7},{2,4},{3,5},{4,2},{5,3},{6,0},{7,1},{8,14},{9,15},{10,... | collective-permute-start | bytes 737288 | tf_op jit(solution)/shard_map/ppermute | solution.py:597
  191.6 36.0 %collective-permute-start.40 = (bf16[6,160,128]{2,1,0:T(8,128)(2,1)S(1)}, bf16[6,160,128]{2,1,0:T(8,128)(2,1)S(1)}, u32[]{:S(2)}, u32[]{:S(2)}) collective-permute-start(bf16[6,160,128]{2,1,0:T(8,128)(2,1)S(1)} %copy-done.31), channel_id=1, source_target_pairs={{0,7},{1,6},{2,5},{3,4},{4,3},{5,2},{6,1},{7,0},{8,15},{9,14},{10,... | collective-permute-start | bytes 737288 | tf_op jit(solution)/shard_map/ppermute | solution.py:597
  203.3 24.4 %collective-permute-start.20 = (bf16[6,160,128]{2,1,0:T(8,128)(2,1)S(1)}, bf16[6,160,128]{2,1,0:T(8,128)(2,1)S(1)}, u32[]{:S(2)}, u32[]{:S(2)}) collective-permute-start(bf16[6,160,128]{2,1,0:T(8,128)(2,1)S(1)} %copy-done.30), channel_id=1, source_target_pairs={{0,1},{1,0},{2,3},{3,2},{4,5},{5,4},{6,7},{7,6},{8,9},{9,8},{10,11... | collective-permute-start | bytes 737288 | tf_op jit(solution)/shard_map/ppermute | solution.py:597
  205.9 25.2 %collective-permute-start.21 = (bf16[6,160,128]{2,1,0:T(8,128)(2,1)S(1)}, bf16[6,160,128]{2,1,0:T(8,128)(2,1)S(1)}, u32[]{:S(2)}, u32[]{:S(2)}) collective-permute-start(bf16[6,160,128]{2,1,0:T(8,128)(2,1)S(1)} %copy-done.29), channel_id=1, source_target_pairs={{0,2},{1,3},{2,0},{3,1},{4,6},{5,7},{6,4},{7,5},{8,10},{9,11},{10,... | collective-permute-start | bytes 737288 | tf_op jit(solution)/shard_map/ppermute | solution.py:597
  215.0 31.4 %collective-permute-start.23 = (bf16[6,160,128]{2,1,0:T(8,128)(2,1)S(1)}, bf16[6,160,128]{2,1,0:T(8,128)(2,1)S(1)}, u32[]{:S(2)}, u32[]{:S(2)}) collective-permute-start(bf16[6,160,128]{2,1,0:T(8,128)(2,1)S(1)} %copy-done.27), channel_id=1, source_target_pairs={{0,4},{1,5},{2,6},{3,7},{4,0},{5,1},{6,2},{7,3},{8,12},{9,13},{10,... | collective-permute-start | bytes 737288 | tf_op jit(solution)/shard_map/ppermute | solution.py:597
  227.6 37.9 %collective-permute-start.24 = (bf16[6,160,128]{2,1,0:T(8,128)(2,1)}, bf16[6,160,128]{2,1,0:T(8,128)(2,1)}, u32[]{:S(2)}, u32[]{:S(2)}) collective-permute-start(bf16[6,160,128]{2,1,0:T(8,128)(2,1)} %get-tuple-element.135), channel_id=1, source_target_pairs={{0,5},{1,4},{2,7},{3,6},{4,1},{5,0},{6,3},{7,2},{8,13},{9,12},{10,... | collective-permute-start | bytes 737288 | tf_op jit(solution)/shard_map/ppermute | solution.py:597
  227.6 37.9 %collective-permute-start.25 = (bf16[6,160,128]{2,1,0:T(8,128)(2,1)S(1)}, bf16[6,160,128]{2,1,0:T(8,128)(2,1)}, u32[]{:S(2)}, u32[]{:S(2)}) collective-permute-start(bf16[6,160,128]{2,1,0:T(8,128)(2,1)S(1)} %copy-done.26), channel_id=1, source_target_pairs={{0,6},{1,7},{2,4},{3,5},{4,2},{5,3},{6,0},{7,1},{8,14},{9,15},{10,... | collective-permute-start | bytes 737288 | tf_op jit(solution)/shard_map/ppermute | solution.py:597
  231.1 54.6 %collective-permute-start.26 = (bf16[6,160,128]{2,1,0:T(8,128)(2,1)S(1)}, bf16[6,160,128]{2,1,0:T(8,128)(2,1)}, u32[]{:S(2)}, u32[]{:S(2)}) collective-permute-start(bf16[6,160,128]{2,1,0:T(8,128)(2,1)S(1)} %copy-done.25), channel_id=1, source_target_pairs={{0,7},{1,6},{2,5},{3,4},{4,3},{5,2},{6,1},{7,0},{8,15},{9,14},{10,... | collective-permute-start | bytes 737288 | tf_op jit(solution)/shard_map/ppermute | solution.py:597
  231.7 106.7 %collective-permute-start.65 = (f32[12,40,641]{2,1,0:T(8,128)S(1)}, f32[12,40,641]{2,1,0:T(8,128)}, u32[]{:S(2)}, u32[]{:S(2)}) collective-permute-start(f32[12,40,641]{2,1,0:T(8,128)S(1)} %broadcast_select_fusion.refs_12_), channel_id=1, source_target_pairs={{0,16},{8,24},{16,0},{24,8},{1,17},{9,25},{17,1},{25,9},{2,18},{10... | collective-permute-start | bytes 3692168 | tf_op jit(solution)/shard_map/ppermute | solution.py:498
  246.5 94.9 %collective-permute-start.63 = (f32[12,40,641]{2,1,0:T(8,128)S(1)}, f32[12,40,641]{2,1,0:T(8,128)}, u32[]{:S(2)}, u32[]{:S(2)}) collective-permute-start(f32[12,40,641]{2,1,0:T(8,128)S(1)} %broadcast_select_fusion.1.refs_10_), channel_id=1, source_target_pairs={{0,16},{8,24},{16,0},{24,8},{1,17},{9,25},{17,1},{25,9},{2,18},{10... | collective-permute-start | bytes 3692168 | tf_op jit(solution)/shard_map/ppermute | solution.py:498
  265.6 25.6 %collective-permute-start.42 = (bf16[6,160,128]{2,1,0:T(8,128)(2,1)}, bf16[6,160,128]{2,1,0:T(8,128)(2,1)S(1)}, u32[]{:S(2)}, u32[]{:S(2)}) collective-permute-start(bf16[6,160,128]{2,1,0:T(8,128)(2,1)} %get-tuple-element.157), channel_id=1, source_target_pairs={{0,2},{1,3},{2,0},{3,1},{4,6},{5,7},{6,4},{7,5},{8,10},{9,11},{10,... | collective-permute-start | bytes 737288 | tf_op jit(solution)/shard_map/ppermute | solution.py:597
  285.7 28.6 %collective-permute-start.44 = (bf16[6,160,128]{2,1,0:T(8,128)(2,1)}, bf16[6,160,128]{2,1,0:T(8,128)(2,1)}, u32[]{:S(2)}, u32[]{:S(2)}) collective-permute-start(bf16[6,160,128]{2,1,0:T(8,128)(2,1)} %get-tuple-element.159), channel_id=1, source_target_pairs={{0,4},{1,5},{2,6},{3,7},{4,0},{5,1},{6,2},{7,3},{8,12},{9,13},{10,... | collective-permute-start | bytes 737288 | tf_op jit(solution)/shard_map/ppermute | solution.py:597
  291.2 23.4 %collective-permute-start.45 = (bf16[6,160,128]{2,1,0:T(8,128)(2,1)}, bf16[6,160,128]{2,1,0:T(8,128)(2,1)}, u32[]{:S(2)}, u32[]{:S(2)}) collective-permute-start(bf16[6,160,128]{2,1,0:T(8,128)(2,1)} %get-tuple-element.160), channel_id=1, source_target_pairs={{0,5},{1,4},{2,7},{3,6},{4,1},{5,0},{6,3},{7,2},{8,13},{9,12},{10,... | collective-permute-start | bytes 737288 | tf_op jit(solution)/shard_map/ppermute | solution.py:597
  299.2 30.1 %collective-permute-start.46 = (bf16[6,160,128]{2,1,0:T(8,128)(2,1)}, bf16[6,160,128]{2,1,0:T(8,128)(2,1)}, u32[]{:S(2)}, u32[]{:S(2)}) collective-permute-start(bf16[6,160,128]{2,1,0:T(8,128)(2,1)} %get-tuple-element.161), channel_id=1, source_target_pairs={{0,6},{1,7},{2,4},{3,5},{4,2},{5,3},{6,0},{7,1},{8,14},{9,15},{10,... | collective-permute-start | bytes 737288 | tf_op jit(solution)/shard_map/ppermute | solution.py:597
  314.3 21.7 %collective-permute-start.47 = (bf16[6,160,128]{2,1,0:T(8,128)(2,1)}, bf16[6,160,128]{2,1,0:T(8,128)(2,1)S(1)}, u32[]{:S(2)}, u32[]{:S(2)}) collective-permute-start(bf16[6,160,128]{2,1,0:T(8,128)(2,1)} %get-tuple-element.162), channel_id=1, source_target_pairs={{0,7},{1,6},{2,5},{3,4},{4,3},{5,2},{6,1},{7,0},{8,15},{9,14},{10,... | collective-permute-start | bytes 737288 | tf_op jit(solution)/shard_map/ppermute | solution.py:597
  336.0 32.2 %collective-permute-start.29 = (bf16[6,160,128]{2,1,0:T(8,128)(2,1)}, bf16[6,160,128]{2,1,0:T(8,128)(2,1)}, u32[]{:S(2)}, u32[]{:S(2)}) collective-permute-start(bf16[6,160,128]{2,1,0:T(8,128)(2,1)} %get-tuple-element.141), channel_id=1, source_target_pairs={{0,3},{1,2},{2,1},{3,0},{4,7},{5,6},{6,5},{7,4},{8,11},{9,10},{10,... | collective-permute-start | bytes 737288 | tf_op jit(solution)/shard_map/ppermute | solution.py:597
  336.0 32.2 %collective-permute-start.30 = (bf16[6,160,128]{2,1,0:T(8,128)(2,1)}, bf16[6,160,128]{2,1,0:T(8,128)(2,1)}, u32[]{:S(2)}, u32[]{:S(2)}) collective-permute-start(bf16[6,160,128]{2,1,0:T(8,128)(2,1)} %get-tuple-element.142), channel_id=1, source_target_pairs={{0,4},{1,5},{2,6},{3,7},{4,0},{5,1},{6,2},{7,3},{8,12},{9,13},{10,... | collective-permute-start | bytes 737288 | tf_op jit(solution)/shard_map/ppermute | solution.py:597
  337.1 33.0 %collective-permute-start.31 = (bf16[6,160,128]{2,1,0:T(8,128)(2,1)}, bf16[6,160,128]{2,1,0:T(8,128)(2,1)}, u32[]{:S(2)}, u32[]{:S(2)}) collective-permute-start(bf16[6,160,128]{2,1,0:T(8,128)(2,1)} %get-tuple-element.143), channel_id=1, source_target_pairs={{0,5},{1,4},{2,7},{3,6},{4,1},{5,0},{6,3},{7,2},{8,13},{9,12},{10,... | collective-permute-start | bytes 737288 | tf_op jit(solution)/shard_map/ppermute | solution.py:597
  338.5 38.8 %collective-permute-start.32 = (bf16[6,160,128]{2,1,0:T(8,128)(2,1)}, bf16[6,160,128]{2,1,0:T(8,128)(2,1)S(1)}, u32[]{:S(2)}, u32[]{:S(2)}) collective-permute-start(bf16[6,160,128]{2,1,0:T(8,128)(2,1)} %get-tuple-element.144), channel_id=1, source_target_pairs={{0,6},{1,7},{2,4},{3,5},{4,2},{5,3},{6,0},{7,1},{8,14},{9,15},{10,... | collective-permute-start | bytes 737288 | tf_op jit(solution)/shard_map/ppermute | solution.py:597
  341.4 41.9 %collective-permute-start.33 = (bf16[6,160,128]{2,1,0:T(8,128)(2,1)}, bf16[6,160,128]{2,1,0:T(8,128)(2,1)S(1)}, u32[]{:S(2)}, u32[]{:S(2)}) collective-permute-start(bf16[6,160,128]{2,1,0:T(8,128)(2,1)} %get-tuple-element.145), channel_id=1, source_target_pairs={{0,7},{1,6},{2,5},{3,4},{4,3},{5,2},{6,1},{7,0},{8,15},{9,14},{10,... | collective-permute-start | bytes 737288 | tf_op jit(solution)/shard_map/ppermute | solution.py:597
  (60 other events, 901.6 us)
